TPU v7x, 128 devices: a whole 4x4x4 slice. The times are simulated.
128 devices in a mesh: seq: 16 (over y, x), hg: 8 (over z, core).
Axes of the slice: x: 4, y: 4, z: 4, core: 2. Of those that a mesh axis runs over, the one named last changes fastest.
Arguments:
- hidden_in: bfloat16 [6144, 2048], P('seq'), may hold values from -6 to 6
- w_query: bfloat16 [2048, 2048], P(None, 'hg'), may hold values from -0.125 to 0.125
- w_key: bfloat16 [2048, 2048], P(None, 'hg'), may hold values from -0.125 to 0.125
- w_value: bfloat16 [2048, 4096], P(None, 'hg'), may hold values from -0.125 to 0.125
- w_zgate: bfloat16 [2048, 4096], P(None, 'hg'), may hold values from -0.125 to 0.125
- w_decay: bfloat16 [2048, 32], P(None, 'hg'), may hold values from -0.125 to 0.125
- w_beta: bfloat16 [2048, 32], P(None, 'hg'), may hold values from -0.125 to 0.125
- conv_query: bfloat16 [4, 2048], P(None, 'hg'), may hold values from -3 to 3
- conv_key: bfloat16 [4, 2048], P(None, 'hg'), may hold values from -3 to 3
- conv_value: bfloat16 [4, 4096], P(None, 'hg'), may hold values from -3 to 3
- a_log: float32 [32], P('hg'), may hold values from -2 to 1
- dt_bias: float32 [32], P('hg'), may hold values from -9 to -3
- norm_gain: float32 [128], replicated, may hold values from 0.5 to 1.5
- w_out: bfloat16 [4096, 2048], P('hg'), may hold values from -0.09375 to 0.09375
Outputs:
- mixer_out: bfloat16 [6144, 2048], P(('seq', 'hg'))
All inputs are finite; a program needn't handle non-finite values.
Results may differ from a plain program's by a relative error of at most 0.02.
Values may be sent and summed in bfloat16 or wider, within the bound.
A program may use at most 128 MiB of HBM per device.

v0:
```python
import jax
import jax.numpy as jnp
from jax import lax
from jax.sharding import PartitionSpec as P

VH = 32
KH = 16
DK = 128
DV = 128
SPAN = 64


highest = lax.Precision.HIGHEST
norm_eps = 1e-06


def passed_along(block, axis, distance):
    devices = range(lax.axis_size(axis))
    route = [(i - distance, i) for i in devices if i - distance in devices]
    return lax.ppermute(block, axis, route)


def project_inputs(hidden_in, w_query, w_key, w_value):
    pre_query = jnp.dot(hidden_in, w_query, preferred_element_type=jnp.float32).astype(jnp.bfloat16)
    pre_key = jnp.dot(hidden_in, w_key, preferred_element_type=jnp.float32).astype(jnp.bfloat16)
    pre_value = jnp.dot(hidden_in, w_value, preferred_element_type=jnp.float32).astype(jnp.bfloat16)
    return (pre_query, pre_key, pre_value)


def conv_silu(projected, kernel, prior):
    kernel_len = kernel.shape[0]
    tok_rows = projected.shape[0]
    padded = jnp.concatenate([prior.astype(jnp.float32), projected.astype(jnp.float32)], axis=0)
    summed = jnp.zeros((tok_rows, projected.shape[1]), jnp.float32)
    for offset in range(kernel_len):
        summed = summed + kernel[offset].astype(jnp.float32) * padded[offset : offset + tok_rows]
    return jax.nn.silu(summed)


def unit_length(vectors):
    return vectors * lax.rsqrt(jnp.sum(vectors * vectors, axis=-1, keepdims=True) + norm_eps)


def mixer_inputs(
    hidden_in,
    pre_query,
    pre_key,
    pre_value,
    prior,
    conv_query,
    conv_key,
    conv_value,
    w_zgate,
    w_decay,
    w_beta,
    a_log,
    dt_bias,
):
    tok_rows = hidden_in.shape[0]
    query_cols = pre_query.shape[1]
    key_cols = pre_key.shape[1]
    ratio = VH // KH
    queries = unit_length(
        conv_silu(pre_query, conv_query, prior[:, :query_cols]).reshape(tok_rows, -1, DK)
    ) * DK ** (-0.5)
    key_vecs = unit_length(
        conv_silu(pre_key, conv_key, prior[:, query_cols : query_cols + key_cols]).reshape(
            tok_rows, -1, DK
        )
    )
    values = conv_silu(pre_value, conv_value, prior[:, query_cols + key_cols :]).reshape(
        tok_rows, -1, DV
    )
    queries = jnp.repeat(queries, ratio, axis=1)
    key_vecs = jnp.repeat(key_vecs, ratio, axis=1)
    zgate = jnp.dot(hidden_in, w_zgate, preferred_element_type=jnp.float32).astype(jnp.bfloat16)
    rate_logits = jnp.dot(hidden_in, w_decay, preferred_element_type=jnp.float32)
    log_decay = -jnp.exp(a_log) * jax.nn.softplus(rate_logits + dt_bias)
    write_rate = jax.nn.sigmoid(jnp.dot(hidden_in, w_beta, preferred_element_type=jnp.float32))
    return (queries, key_vecs, values, log_decay, write_rate, zgate)


def to_blocks(array_3d):
    tok_rows, head_count = (array_3d.shape[0], array_3d.shape[1])
    return array_3d.reshape(tok_rows // SPAN, SPAN, head_count, -1).transpose(0, 2, 1, 3)


def span_terms(queries, key_vecs, values, log_decay, write_rate):
    block_len = log_decay.shape[-1]
    cum_decay = jnp.cumsum(log_decay, axis=-1)
    row_ids = lax.broadcasted_iota(jnp.int32, (block_len, block_len), 0)
    col_ids = lax.broadcasted_iota(jnp.int32, (block_len, block_len), 1)
    inclusive = row_ids >= col_ids
    strict = row_ids > col_ids
    gap_mat = cum_decay[..., :, None] - cum_decay[..., None, :]
    falloff = jnp.where(inclusive, jnp.exp(jnp.where(inclusive, gap_mat, 0.0)), 0.0)
    key_dots = jnp.einsum("...sd,...td->...st", key_vecs, key_vecs, precision=highest)
    lower_part = jnp.where(strict, write_rate[..., :, None] * falloff * key_dots, 0.0)
    unit_lower = lower_part + jnp.eye(block_len, dtype=jnp.float32)
    wy_keys = lax.linalg.triangular_solve(
        unit_lower,
        (write_rate * jnp.exp(cum_decay))[..., None] * key_vecs,
        left_side=True,
        lower=True,
        unit_diagonal=True,
    )
    wy_values = lax.linalg.triangular_solve(
        unit_lower, write_rate[..., None] * values, left_side=True, lower=True, unit_diagonal=True
    )
    scores = falloff * jnp.einsum("...sd,...td->...st", queries, key_vecs, precision=highest)
    tail_keys = jnp.exp(cum_decay[..., -1:] - cum_decay)[..., None] * key_vecs
    whole_decay = jnp.exp(cum_decay[..., -1])[..., None, None]
    transition = whole_decay * jnp.eye(key_vecs.shape[-1], dtype=jnp.float32) - jnp.einsum(
        "...sd,...se->...de", tail_keys, wy_keys, precision=highest
    )
    written = jnp.einsum("...sd,...se->...de", tail_keys, wy_values, precision=highest)
    carry_map = jnp.exp(cum_decay)[..., None] * queries - jnp.einsum(
        "...st,...td->...sd", scores, wy_keys, precision=highest
    )
    local_out = jnp.einsum("...st,...te->...se", scores, wy_values, precision=highest)
    return (transition, written, carry_map, local_out)


def gated_output(produced, zgate, norm_gain):
    tok_rows = produced.shape[0]
    mean_sq = jnp.mean(produced * produced, axis=-1, keepdims=True)
    gate_vals = jax.nn.silu(zgate.astype(jnp.float32).reshape(produced.shape))
    normed = produced * lax.rsqrt(mean_sq + norm_eps) * norm_gain * gate_vals
    return normed.reshape(tok_rows, -1).astype(jnp.bfloat16)


def advance(state_now, per_span):
    transition, written, carry_map, local_out = per_span
    produced = jnp.einsum("hsd,hde->hse", carry_map, state_now, precision=highest) + local_out
    state_next = jnp.einsum("hde,hef->hdf", transition, state_now, precision=highest) + written
    return (state_next, produced)


def apply_shard(trans_mat, state_now, written):
    return jnp.einsum("hde,hef->hdf", trans_mat, state_now, precision=highest) + written


def on_device(
    hidden_in,
    w_query,
    w_key,
    w_value,
    w_zgate,
    w_decay,
    w_beta,
    conv_query,
    conv_key,
    conv_value,
    a_log,
    dt_bias,
    norm_gain,
    w_out,
):
    tok_rows = hidden_in.shape[0]
    pre_query, pre_key, pre_value = project_inputs(hidden_in, w_query, w_key, w_value)
    kernel_len = conv_query.shape[0]
    rim_rows = tok_rows - kernel_len + 1
    rim_block = jnp.concatenate(
        [pre_query[rim_rows:], pre_key[rim_rows:], pre_value[rim_rows:]], axis=1
    )
    prior = passed_along(rim_block, "seq", 1)
    queries, key_vecs, values, log_decay, write_rate, zgate = mixer_inputs(
        hidden_in,
        pre_query,
        pre_key,
        pre_value,
        prior,
        conv_query,
        conv_key,
        conv_value,
        w_zgate,
        w_decay,
        w_beta,
        a_log,
        dt_bias,
    )
    terms = span_terms(
        to_blocks(queries),
        to_blocks(key_vecs),
        to_blocks(values),
        to_blocks(log_decay[..., None])[..., 0],
        to_blocks(write_rate[..., None])[..., 0],
    )
    transition, written, carry_map, local_out = terms
    head_count = values.shape[1]
    identity = jnp.broadcast_to(jnp.eye(DK, dtype=jnp.float32), (head_count, DK, DK))
    empty_state = jnp.zeros((head_count, DK, DV), jnp.float32)

    def compose(carried, per_span):
        prefix_a, prefix_b = carried
        step_trans, step_written = per_span
        new_a = jnp.einsum("hde,hef->hdf", step_trans, prefix_a, precision=highest)
        return ((new_a, apply_shard(step_trans, prefix_b, step_written)), None)

    (shard_a, shard_b), unused = lax.scan(compose, (identity, empty_state), (transition, written))

    def relay(turn_index, state_now):
        return passed_along(
            apply_shard(shard_a, state_now, shard_b).astype(jnp.bfloat16), "seq", 1
        ).astype(jnp.float32)

    state_in = lax.fori_loop(0, lax.axis_size("seq") - 1, relay, empty_state)
    final_state, produced = lax.scan(advance, state_in, terms)
    produced = produced.transpose(0, 2, 1, 3).reshape(tok_rows, head_count, DV)
    gated = gated_output(produced, zgate, norm_gain)
    return lax.psum_scatter(
        jnp.dot(gated, w_out, preferred_element_type=jnp.float32).astype(jnp.bfloat16),
        "hg",
        scatter_dimension=0,
        tiled=True,
    )


def solution(mesh):
    return jax.shard_map(
        on_device,
        mesh=mesh,
        in_specs=(
            P("seq", None),
            P(None, "hg"),
            P(None, "hg"),
            P(None, "hg"),
            P(None, "hg"),
            P(None, "hg"),
            P(None, "hg"),
            P(None, "hg"),
            P(None, "hg"),
            P(None, "hg"),
            P("hg"),
            P("hg"),
            P(),
            P("hg", None),
        ),
        out_specs=P(("seq", "hg"), None),
        check_vma=False,
    )
```

profile of v0, /device:TPU:1, one launch (start us, length us, event | category | flops | bytes accessed | tf_op | source)
XLA Modules:
  0.0 410.7 jit_solution(7166664444184242953)
XLA Ops:
  6.5 4.1 fusion.84
  13.1 4.5 %collective-permute-start.1 = (bf16[3,1024]{1,0:T(4,128)(2,1)}, bf16[3,1024]{1,0:T(4,128)(2,1)}, u32[]{:S(2)}, u32[]{:S(2)}) collective-permute-start(bf16[3,1024]{1,0:T(4,128)(2,1)} %pad_maximum_fusion.3), channel_id=1, source_target_pairs={{0,8},{8,16},{16,24},{24,32},{32,40},{40,48},{48,56},{56,64},{64,7... | collective-permute-start | bytes 18440 | tf_op jit(solution)/shard_map/ppermute | solution.py:20
  20.9 1.9 fusion.32
  28.6 2.1 divide_multiply_fusion.1
  35.6 2.3 convolution_multiply_fusion
  38.0 2.4 fusion.28
  40.3 119.3 %custom-call.6 = f32[6,4,1,64,64]{3,4,2,1,0:T(8,128)} custom-call(f32[6,4,1,64,64]{4,3,2,1,0:T(8,128)} %fusion.28), custom_call_target="InvertDiagBlocksLowerTriangular" | custom-call | tf_op jit(solution)/shard_map/triangular_solve/custom-call.1 | solution.py:100
  160.4 3.8 divide_multiply_fusion
  164.1 2.3 reshape_reshape.10
  166.4 3.1 fusion.45
  174.0 3.8 fusion.52
  179.6 4.0 multiply_subtract_fusion
  183.6 17.4 %while.37 = (s32[]{:T(128)}, f32[4,128,128]{2,1,0:T(8,128)S(1)}, f32[4,128,128]{2,1,0:T(8,128)S(1)}, f32[6,4,128,128]{3,2,1,0:T(8,128)}, f32[6,4,128,128]{3,2,1,0:T(8,128)}, /*index=5*/s32[]{:T(128)}, s32[]{:T(128)}) while((s32[]{:T(128)}, f32[4,128,128]{2,1,0:T(8,128)S(1)}, f32[4,128,128]{2,1,0:T(8,128)S(1)}, ...), condition=%wide.region_3.5_spmd.clone, body=%wide.region_2.4_spmd.clone.sunk | while | flops 201457664 | bytes 2885207 | solution.py:200
  201.0 114.8 %while.38 = (s32[]{:T(128)}, f32[4,128,128]{2,1,0:T(8,128)S(1)}, f32[4,128,128]{2,1,0:T(8,128)S(1)}, f32[4,128,128]{2,1,0:T(8,128)S(1)}, s32[]{:T(128)}, /*index=5*/s32[]{:T(128)}) while((s32[]{:T(128)}, f32[4,128,128]{2,1,0:T(8,128)S(1)}, f32[4,128,128]{2,1,0:T(8,128)S(1)}, f32[4,128,128]{2,1,0:T(8,128)S(1)}, s32[]{:T(128)}, ...), condition=%wide.region_5.7_spmd.clone, body=%wide.region_4.6_spmd.clone.sunk | while | flops 100925440 | bytes 1835127 | solution.py:207
  201.4 2.5 collective-permute-start
  204.0 1.9 collective-permute-done
  206.4 3.8 collective-permute-start
  210.1 1.9 collective-permute-done
  212.5 3.8 collective-permute-start
  216.3 1.9 collective-permute-done
  218.7 3.8 collective-permute-start
  224.8 3.8 collective-permute-start
  228.6 2.0 collective-permute-done
  231.0 5.7 %collective-permute-start = (bf16[4,128,128]{2,1,0:T(8,128)(2,1)S(1)}, bf16[4,128,128]{2,1,0:T(8,128)(2,1)S(1)}, u32[]{:S(2)}, u32[]{:S(2)}) collective-permute-start(bf16[4,128,128]{2,1,0:T(8,128)(2,1)S(1)} %fusion.135), channel_id=1, source_target_pairs={{0,8},{8,16},{16,24},{24,32},{32,40},{40,48},{48,56},{56,64},{64,7... | collective-permute-start | bytes 393224 | tf_op jit(solution)/shard_map/while/body/eval_jaxpr/ppermute | solution.py:20
  239.1 5.9 %collective-permute-start = (bf16[4,128,128]{2,1,0:T(8,128)(2,1)S(1)}, bf16[4,128,128]{2,1,0:T(8,128)(2,1)S(1)}, u32[]{:S(2)}, u32[]{:S(2)}) collective-permute-start(bf16[4,128,128]{2,1,0:T(8,128)(2,1)S(1)} %fusion.135), channel_id=1, source_target_pairs={{0,8},{8,16},{16,24},{24,32},{32,40},{40,48},{48,56},{56,64},{64,7... | collective-permute-start | bytes 393224 | tf_op jit(solution)/shard_map/while/body/eval_jaxpr/ppermute | solution.py:20
  245.0 1.9 collective-permute-done
  247.3 5.9 %collective-permute-start = (bf16[4,128,128]{2,1,0:T(8,128)(2,1)S(1)}, bf16[4,128,128]{2,1,0:T(8,128)(2,1)S(1)}, u32[]{:S(2)}, u32[]{:S(2)}) collective-permute-start(bf16[4,128,128]{2,1,0:T(8,128)(2,1)S(1)} %fusion.135), channel_id=1, source_target_pairs={{0,8},{8,16},{16,24},{24,32},{32,40},{40,48},{48,56},{56,64},{64,7... | collective-permute-start | bytes 393224 | tf_op jit(solution)/shard_map/while/body/eval_jaxpr/ppermute | solution.py:20
  253.2 2.5 collective-permute-done
  256.1 6.2 %collective-permute-start = (bf16[4,128,128]{2,1,0:T(8,128)(2,1)S(1)}, bf16[4,128,128]{2,1,0:T(8,128)(2,1)S(1)}, u32[]{:S(2)}, u32[]{:S(2)}) collective-permute-start(bf16[4,128,128]{2,1,0:T(8,128)(2,1)S(1)} %fusion.135), channel_id=1, source_target_pairs={{0,8},{8,16},{16,24},{24,32},{32,40},{40,48},{48,56},{56,64},{64,7... | collective-permute-start | bytes 393224 | tf_op jit(solution)/shard_map/while/body/eval_jaxpr/ppermute | solution.py:20
  262.3 3.0 collective-permute-done
  265.8 6.2 %collective-permute-start = (bf16[4,128,128]{2,1,0:T(8,128)(2,1)S(1)}, bf16[4,128,128]{2,1,0:T(8,128)(2,1)S(1)}, u32[]{:S(2)}, u32[]{:S(2)}) collective-permute-start(bf16[4,128,128]{2,1,0:T(8,128)(2,1)S(1)} %fusion.135), channel_id=1, source_target_pairs={{0,8},{8,16},{16,24},{24,32},{32,40},{40,48},{48,56},{56,64},{64,7... | collective-permute-start | bytes 393224 | tf_op jit(solution)/shard_map/while/body/eval_jaxpr/ppermute | solution.py:20
  274.3 5.8 %collective-permute-start = (bf16[4,128,128]{2,1,0:T(8,128)(2,1)S(1)}, bf16[4,128,128]{2,1,0:T(8,128)(2,1)S(1)}, u32[]{:S(2)}, u32[]{:S(2)}) collective-permute-start(bf16[4,128,128]{2,1,0:T(8,128)(2,1)S(1)} %fusion.135), channel_id=1, source_target_pairs={{0,8},{8,16},{16,24},{24,32},{32,40},{40,48},{48,56},{56,64},{64,7... | collective-permute-start | bytes 393224 | tf_op jit(solution)/shard_map/while/body/eval_jaxpr/ppermute | solution.py:20
  282.5 6.3 %collective-permute-start = (bf16[4,128,128]{2,1,0:T(8,128)(2,1)S(1)}, bf16[4,128,128]{2,1,0:T(8,128)(2,1)S(1)}, u32[]{:S(2)}, u32[]{:S(2)}) collective-permute-start(bf16[4,128,128]{2,1,0:T(8,128)(2,1)S(1)} %fusion.135), channel_id=1, source_target_pairs={{0,8},{8,16},{16,24},{24,32},{32,40},{40,48},{48,56},{56,64},{64,7... | collective-permute-start | bytes 393224 | tf_op jit(solution)/shard_map/while/body/eval_jaxpr/ppermute | solution.py:20
  291.1 6.2 %collective-permute-start = (bf16[4,128,128]{2,1,0:T(8,128)(2,1)S(1)}, bf16[4,128,128]{2,1,0:T(8,128)(2,1)S(1)}, u32[]{:S(2)}, u32[]{:S(2)}) collective-permute-start(bf16[4,128,128]{2,1,0:T(8,128)(2,1)S(1)} %fusion.135), channel_id=1, source_target_pairs={{0,8},{8,16},{16,24},{24,32},{32,40},{40,48},{48,56},{56,64},{64,7... | collective-permute-start | bytes 393224 | tf_op jit(solution)/shard_map/while/body/eval_jaxpr/ppermute | solution.py:20
  297.3 1.9 collective-permute-done
  299.7 5.9 %collective-permute-start = (bf16[4,128,128]{2,1,0:T(8,128)(2,1)S(1)}, bf16[4,128,128]{2,1,0:T(8,128)(2,1)S(1)}, u32[]{:S(2)}, u32[]{:S(2)}) collective-permute-start(bf16[4,128,128]{2,1,0:T(8,128)(2,1)S(1)} %fusion.135), channel_id=1, source_target_pairs={{0,8},{8,16},{16,24},{24,32},{32,40},{40,48},{48,56},{56,64},{64,7... | collective-permute-start | bytes 393224 | tf_op jit(solution)/shard_map/while/body/eval_jaxpr/ppermute | solution.py:20
  305.6 1.9 collective-permute-done
  307.9 5.9 %collective-permute-start = (bf16[4,128,128]{2,1,0:T(8,128)(2,1)S(1)}, bf16[4,128,128]{2,1,0:T(8,128)(2,1)S(1)}, u32[]{:S(2)}, u32[]{:S(2)}) collective-permute-start(bf16[4,128,128]{2,1,0:T(8,128)(2,1)S(1)} %fusion.135), channel_id=1, source_target_pairs={{0,8},{8,16},{16,24},{24,32},{32,40},{40,48},{48,56},{56,64},{64,7... | collective-permute-start | bytes 393224 | tf_op jit(solution)/shard_map/while/body/eval_jaxpr/ppermute | solution.py:20
  313.8 1.9 collective-permute-done
  315.8 20.7 %while.36 = (s32[]{:T(128)}, f32[4,128,128]{2,1,0:T(8,128)S(1)}, f32[6,4,64,128]{3,2,1,0:T(8,128)}, f32[6,4,128,128]{3,2,1,0:T(8,128)}, f32[6,4,128,128]{3,2,1,0...) while((s32[]{:T(128)}, f32[4,128,128]{2,1,0:T(8,128)S(1)}, ...), condition=%wide.region_8.10_spmd, body=%wide.region_7.9_spmd.sunk | while | flops 151093248 | bytes 2230357 | solution.py:208
  315.8 2.0 fusion.127
  319.3 2.0 fusion.127
  322.8 2.0 fusion.127
  326.2 2.0 fusion.127
  329.7 2.0 fusion.127
  333.1 2.0 fusion.127
  340.2 5.4 %convolution_convert_fusion = bf16[384,2048]{1,0:T(8,128)(2,1)} fusion(bf16[512,2048]{1,0:T(8,128)(2,1)S(1)} %copy-done, f32[48,8,4,128]{3,2,1,0:T(4,128)S(1)} %bitcast.154, f32[48,8,4,128]{3,2,1,0:T(4,128)} %bitcast.153, bf16[384,2048]{1,0:T(8,128)(2,1)} %param.22, bf16[2048,512]{1,0:T(8,128)(2,1)} %param.26, f32[512]{0:T(512)S(1)} %copy-done.23), kind=kOutput, calls=%fused_computation.28 | convolution fusion | flops 1613365248 | bytes 8914944 | tf_op jit(solution)/shard_map/dot_general | solution.py:212
  345.6 58.2 %reduce-scatter.2.cloned.1.call-done = bf16[48,2048]{1,0:T(8,128)(2,1)} async-done(((bf16[384,2048]{1,0:T(8,128)(2,1)}), bf16[48,2048]{1,0:T(8,128)(2,1)}) %reduce-scatter.2.cloned.1.call-update) | async-done | bytes 196624 | tf_op jit(solution)/shard_map/reduce_scatter | solution.py:211
  (186 shorter events, 67.9 us)
Async XLA Ops:
  6.5 333.6 %copy-start = (bf16[512,2048]{1,0:T(8,128)(2,1)S(1)}, bf16[512,2048]{1,0:T(8,128)(2,1)}, u32[]{:S(2)}) copy-start(bf16[512,2048]{1,0:T(8,128)(2,1)} %param.35) | copy-start | bytes 6291460
  6.5 397.3 %reduce-scatter.2.cloned.1.call-start = ((), (), s32[]{:S(2)}) async-start(), calls=%async_computation.1 | async-start | bytes 1769472 | tf_op jit(solution)/shard_map/reduce_scatter | solution.py:211
  6.5 4.1 copy-start.1
  6.5 4.1 %copy-start.9 = (bf16[2048,256]{1,0:T(8,128)(2,1)S(1)}, bf16[2048,256]{1,0:T(8,128)(2,1)}, u32[]{:S(2)}) copy-start(bf16[2048,256]{1,0:T(8,128)(2,1)} %param.23) | copy-start | bytes 3145732
  10.7 1.2 copy-start.10
  11.9 6.4 %copy-start.21 = (bf16[4,256]{1,0:T(4,128)(2,1)S(1)}, bf16[4,256]{1,0:T(4,128)(2,1)}, u32[]{:S(2)}) copy-start(bf16[4,256]{1,0:T(4,128)(2,1)} %param.30) | copy-start | bytes 6148
  11.9 7.0 %copy-start.22 = (bf16[4,256]{1,0:T(4,128)(2,1)S(1)}, bf16[4,256]{1,0:T(4,128)(2,1)}, u32[]{:S(2)}) copy-start(bf16[4,256]{1,0:T(4,128)(2,1)} %param.29) | copy-start | bytes 6148
  11.9 7.6 %copy-start.26 = (f32[4]{0:T(128)S(1)}, f32[4]{0:T(128)}, u32[]{:S(2)}) copy-start(f32[4]{0:T(128)} %param.32) | copy-start | bytes 52
  11.9 7.6 %copy-start.14 = (bf16[2048,4]{0,1:T(4,128)(2,1)S(1)}, bf16[2048,4]{0,1:T(4,128)(2,1)}, u32[]{:S(2)}) copy-start(bf16[2048,4]{0,1:T(4,128)(2,1)} %param.27) | copy-start | bytes 49156
  11.9 7.6 %copy-start.24 = (f32[4]{0:T(128)S(1)}, f32[4]{0:T(128)}, u32[]{:S(2)}) copy-start(f32[4]{0:T(128)} %param.33) | copy-start | bytes 52
  12.5 8.4 %copy-start.15 = (bf16[2048,4]{0,1:T(4,128)(2,1)S(1)}, bf16[2048,4]{0,1:T(4,128)(2,1)}, u32[]{:S(2)}) copy-start(bf16[2048,4]{0,1:T(4,128)(2,1)} %param.28) | copy-start | bytes 49156
  13.1 14.8 %collective-permute-start.1 = (bf16[3,1024]{1,0:T(4,128)(2,1)}, bf16[3,1024]{1,0:T(4,128)(2,1)}, u32[]{:S(2)}, u32[]{:S(2)}) collective-permute-start(bf16[3,1024]{1,0:T(4,128)(2,1)} %pad_maximum_fusion.3), channel_id=1, source_target_pairs={{0,8},{8,16},{16,24},{24,32},{32,40},{40,48},{48,56},{56,64},{64,7... | collective-permute-start | bytes 18440 | tf_op jit(solution)/shard_map/ppermute | solution.py:20
  19.5 3.4 copy-start.16
  19.5 6.4 %copy-start.25 = (f32[128]{0:T(128)S(1)}, f32[128]{0:T(128)}, u32[]{:S(2)}) copy-start(f32[128]{0:T(128)} %param.34) | copy-start | bytes 1540
  31.9 1.8 copy-start.7
  33.9 1.1 copy-start.8
  34.9 0.7 copy-start.11
  35.0 2.9 copy-start.3
  35.0 2.9 copy-start.12
  35.1 2.9 copy-start.13
  35.1 2.9 copy-start.19
  35.1 2.9 copy-start.20
  38.0 122.4 %copy-start.17 = (f32[1,512]{1,0:T(1,128)S(1)}, f32[1,512]{1,0:T(1,128)}, u32[]{:S(2)}) copy-start(f32[1,512]{1,0:T(1,128)} %get-tuple-element.168) | copy-start | bytes 6148
  38.0 122.4 %copy-start.18 = (f32[1,512]{1,0:T(1,128)S(1)}, f32[1,512]{1,0:T(1,128)}, u32[]{:S(2)}) copy-start(f32[1,512]{1,0:T(1,128)} %get-tuple-element.169) | copy-start | bytes 6148
  166.4 3.1 copy-start.4
  169.5 1.1 copy-start.6
  170.0 2.1 copy-start.2
  201.4 4.5 %collective-permute-start = (bf16[4,128,128]{2,1,0:T(8,128)(2,1)S(1)}, bf16[4,128,128]{2,1,0:T(8,128)(2,1)S(1)}, u32[]{:S(2)}, u32[]{:S(2)}) collective-permute-start(bf16[4,128,128]{2,1,0:T(8,128)(2,1)S(1)} %fusion.135), channel_id=1, source_target_pairs={{0,8},{8,16},{16,24},{24,32},{32,40},{40,48},{48,56},{56,64},{64,7... | collective-permute-start | bytes 393224 | tf_op jit(solution)/shard_map/while/body/eval_jaxpr/ppermute | solution.py:20
  206.4 5.7 %collective-permute-start = (bf16[4,128,128]{2,1,0:T(8,128)(2,1)S(1)}, bf16[4,128,128]{2,1,0:T(8,128)(2,1)S(1)}, u32[]{:S(2)}, u32[]{:S(2)}) collective-permute-start(bf16[4,128,128]{2,1,0:T(8,128)(2,1)S(1)} %fusion.135), channel_id=1, source_target_pairs={{0,8},{8,16},{16,24},{24,32},{32,40},{40,48},{48,56},{56,64},{64,7... | collective-permute-start | bytes 393224 | tf_op jit(solution)/shard_map/while/body/eval_jaxpr/ppermute | solution.py:20
  212.5 5.7 %collective-permute-start = (bf16[4,128,128]{2,1,0:T(8,128)(2,1)S(1)}, bf16[4,128,128]{2,1,0:T(8,128)(2,1)S(1)}, u32[]{:S(2)}, u32[]{:S(2)}) collective-permute-start(bf16[4,128,128]{2,1,0:T(8,128)(2,1)S(1)} %fusion.135), channel_id=1, source_target_pairs={{0,8},{8,16},{16,24},{24,32},{32,40},{40,48},{48,56},{56,64},{64,7... | collective-permute-start | bytes 393224 | tf_op jit(solution)/shard_map/while/body/eval_jaxpr/ppermute | solution.py:20
  218.7 5.7 %collective-permute-start = (bf16[4,128,128]{2,1,0:T(8,128)(2,1)S(1)}, bf16[4,128,128]{2,1,0:T(8,128)(2,1)S(1)}, u32[]{:S(2)}, u32[]{:S(2)}) collective-permute-start(bf16[4,128,128]{2,1,0:T(8,128)(2,1)S(1)} %fusion.135), channel_id=1, source_target_pairs={{0,8},{8,16},{16,24},{24,32},{32,40},{40,48},{48,56},{56,64},{64,7... | collective-permute-start | bytes 393224 | tf_op jit(solution)/shard_map/while/body/eval_jaxpr/ppermute | solution.py:20
  224.8 5.8 %collective-permute-start = (bf16[4,128,128]{2,1,0:T(8,128)(2,1)S(1)}, bf16[4,128,128]{2,1,0:T(8,128)(2,1)S(1)}, u32[]{:S(2)}, u32[]{:S(2)}) collective-permute-start(bf16[4,128,128]{2,1,0:T(8,128)(2,1)S(1)} %fusion.135), channel_id=1, source_target_pairs={{0,8},{8,16},{16,24},{24,32},{32,40},{40,48},{48,56},{56,64},{64,7... | collective-permute-start | bytes 393224 | tf_op jit(solution)/shard_map/while/body/eval_jaxpr/ppermute | solution.py:20
  231.0 7.6 %collective-permute-start = (bf16[4,128,128]{2,1,0:T(8,128)(2,1)S(1)}, bf16[4,128,128]{2,1,0:T(8,128)(2,1)S(1)}, u32[]{:S(2)}, u32[]{:S(2)}) collective-permute-start(bf16[4,128,128]{2,1,0:T(8,128)(2,1)S(1)} %fusion.135), channel_id=1, source_target_pairs={{0,8},{8,16},{16,24},{24,32},{32,40},{40,48},{48,56},{56,64},{64,7... | collective-permute-start | bytes 393224 | tf_op jit(solution)/shard_map/while/body/eval_jaxpr/ppermute | solution.py:20
  239.1 7.8 %collective-permute-start = (bf16[4,128,128]{2,1,0:T(8,128)(2,1)S(1)}, bf16[4,128,128]{2,1,0:T(8,128)(2,1)S(1)}, u32[]{:S(2)}, u32[]{:S(2)}) collective-permute-start(bf16[4,128,128]{2,1,0:T(8,128)(2,1)S(1)} %fusion.135), channel_id=1, source_target_pairs={{0,8},{8,16},{16,24},{24,32},{32,40},{40,48},{48,56},{56,64},{64,7... | collective-permute-start | bytes 393224 | tf_op jit(solution)/shard_map/while/body/eval_jaxpr/ppermute | solution.py:20
  247.3 8.3 %collective-permute-start = (bf16[4,128,128]{2,1,0:T(8,128)(2,1)S(1)}, bf16[4,128,128]{2,1,0:T(8,128)(2,1)S(1)}, u32[]{:S(2)}, u32[]{:S(2)}) collective-permute-start(bf16[4,128,128]{2,1,0:T(8,128)(2,1)S(1)} %fusion.135), channel_id=1, source_target_pairs={{0,8},{8,16},{16,24},{24,32},{32,40},{40,48},{48,56},{56,64},{64,7... | collective-permute-start | bytes 393224 | tf_op jit(solution)/shard_map/while/body/eval_jaxpr/ppermute | solution.py:20
  256.1 9.2 %collective-permute-start = (bf16[4,128,128]{2,1,0:T(8,128)(2,1)S(1)}, bf16[4,128,128]{2,1,0:T(8,128)(2,1)S(1)}, u32[]{:S(2)}, u32[]{:S(2)}) collective-permute-start(bf16[4,128,128]{2,1,0:T(8,128)(2,1)S(1)} %fusion.135), channel_id=1, source_target_pairs={{0,8},{8,16},{16,24},{24,32},{32,40},{40,48},{48,56},{56,64},{64,7... | collective-permute-start | bytes 393224 | tf_op jit(solution)/shard_map/while/body/eval_jaxpr/ppermute | solution.py:20
  265.8 8.1 %collective-permute-start = (bf16[4,128,128]{2,1,0:T(8,128)(2,1)S(1)}, bf16[4,128,128]{2,1,0:T(8,128)(2,1)S(1)}, u32[]{:S(2)}, u32[]{:S(2)}) collective-permute-start(bf16[4,128,128]{2,1,0:T(8,128)(2,1)S(1)} %fusion.135), channel_id=1, source_target_pairs={{0,8},{8,16},{16,24},{24,32},{32,40},{40,48},{48,56},{56,64},{64,7... | collective-permute-start | bytes 393224 | tf_op jit(solution)/shard_map/while/body/eval_jaxpr/ppermute | solution.py:20
  274.3 7.7 %collective-permute-start = (bf16[4,128,128]{2,1,0:T(8,128)(2,1)S(1)}, bf16[4,128,128]{2,1,0:T(8,128)(2,1)S(1)}, u32[]{:S(2)}, u32[]{:S(2)}) collective-permute-start(bf16[4,128,128]{2,1,0:T(8,128)(2,1)S(1)} %fusion.135), channel_id=1, source_target_pairs={{0,8},{8,16},{16,24},{24,32},{32,40},{40,48},{48,56},{56,64},{64,7... | collective-permute-start | bytes 393224 | tf_op jit(solution)/shard_map/while/body/eval_jaxpr/ppermute | solution.py:20
  282.5 8.2 %collective-permute-start = (bf16[4,128,128]{2,1,0:T(8,128)(2,1)S(1)}, bf16[4,128,128]{2,1,0:T(8,128)(2,1)S(1)}, u32[]{:S(2)}, u32[]{:S(2)}) collective-permute-start(bf16[4,128,128]{2,1,0:T(8,128)(2,1)S(1)} %fusion.135), channel_id=1, source_target_pairs={{0,8},{8,16},{16,24},{24,32},{32,40},{40,48},{48,56},{56,64},{64,7... | collective-permute-start | bytes 393224 | tf_op jit(solution)/shard_map/while/body/eval_jaxpr/ppermute | solution.py:20
  291.1 8.2 %collective-permute-start = (bf16[4,128,128]{2,1,0:T(8,128)(2,1)S(1)}, bf16[4,128,128]{2,1,0:T(8,128)(2,1)S(1)}, u32[]{:S(2)}, u32[]{:S(2)}) collective-permute-start(bf16[4,128,128]{2,1,0:T(8,128)(2,1)S(1)} %fusion.135), channel_id=1, source_target_pairs={{0,8},{8,16},{16,24},{24,32},{32,40},{40,48},{48,56},{56,64},{64,7... | collective-permute-start | bytes 393224 | tf_op jit(solution)/shard_map/while/body/eval_jaxpr/ppermute | solution.py:20
  299.7 7.8 %collective-permute-start = (bf16[4,128,128]{2,1,0:T(8,128)(2,1)S(1)}, bf16[4,128,128]{2,1,0:T(8,128)(2,1)S(1)}, u32[]{:S(2)}, u32[]{:S(2)}) collective-permute-start(bf16[4,128,128]{2,1,0:T(8,128)(2,1)S(1)} %fusion.135), channel_id=1, source_target_pairs={{0,8},{8,16},{16,24},{24,32},{32,40},{40,48},{48,56},{56,64},{64,7... | collective-permute-start | bytes 393224 | tf_op jit(solution)/shard_map/while/body/eval_jaxpr/ppermute | solution.py:20
  307.9 7.8 %collective-permute-start = (bf16[4,128,128]{2,1,0:T(8,128)(2,1)S(1)}, bf16[4,128,128]{2,1,0:T(8,128)(2,1)S(1)}, u32[]{:S(2)}, u32[]{:S(2)}) collective-permute-start(bf16[4,128,128]{2,1,0:T(8,128)(2,1)S(1)} %fusion.135), channel_id=1, source_target_pairs={{0,8},{8,16},{16,24},{24,32},{32,40},{40,48},{48,56},{56,64},{64,7... | collective-permute-start | bytes 393224 | tf_op jit(solution)/shard_map/while/body/eval_jaxpr/ppermute | solution.py:20
  336.6 1.7 copy-start.5
  338.1 2.1 copy-start.23
Sparse Core Ops, SparseCore 0:
  345.7 58.0 reduce-scatter.1
where the time goes:
time: 414 us; the launch traced here: 411 us
  other arithmetic  137 us (33%)
  waiting for transfers between devices  88.8 us (21%)
  starting transfers between devices  82.1 us (20%)
  matrix products  76.8 us (19%)
  between operations  13.9 us (3%)
  local copies, waits for them, and re-layouts  11.2 us (3%)
    another operation x4, other arithmetic, span_terms(): lax.linalg.triangular_solve(unit_lower, (write_rate * jnp.exp(cum_decay))...  121 us
    ppermute x16, starting transfers between devices, passed_along(): return lax.ppermute(block, axis, route)  82.1 us
    reduce_scatter x1, waiting for transfers between devices, on_device(): lax.psum_scatter(jnp.dot(gated, w_out, preferred_element_type=jnp.float32...  58.2 us
    ppermute x16, waiting for transfers between devices, passed_along(): return lax.ppermute(block, axis, route)  30.5 us
    dot_general x21, matrix products, apply_shard(): jnp.einsum('hde,hef->hdf', trans_mat, state_now, precision=highest)  14.4 us
    dot_general x6, matrix products, advance(): jnp.einsum('hsd,hde->hse', carry_map, state_now, precision=highest)  11.9 us
    dot_general x6, matrix products, advance(): jnp.einsum('hde,hef->hdf', transition, state_now, precision=highest)  8.52 us
  transfers between devices with their start and end apart: 17, of which 16 were waited for; matrix products, arithmetic and copies ran while one was open for 2% of the time, Pallas kernels for 0%

commit v1 on v0

--- a/solution.py
+++ b/solution.py
@@ -1,4 +1,5 @@
 import jax
+import numpy as np
 import jax.numpy as jnp
 from jax import lax
 from jax.sharding import PartitionSpec as P
@@ -85,6 +86,24 @@
     return array_3d.reshape(tok_rows // SPAN, SPAN, head_count, -1).transpose(0, 2, 1, 3)
 
 
+def unit_lower_inverse(lower_part):
+    block_len = lower_part.shape[-1]
+    row_ids = np.arange(block_len)[:, None]
+    col_ids = np.arange(block_len)[None, :]
+    first = jnp.asarray((row_ids // 2 == col_ids // 2) & (row_ids != col_ids), jnp.float32)
+    inverse = lax.optimization_barrier(
+        jnp.asarray(np.eye(block_len), jnp.float32) - lower_part * first
+    )
+    size = 2
+    while size < block_len:
+        band = (row_ids // (2 * size) == col_ids // (2 * size)) & (row_ids // size != col_ids // size)
+        off_blocks = lower_part * jnp.asarray(band, jnp.float32)
+        step = jnp.einsum("...st,...tu->...su", inverse, off_blocks, precision=highest)
+        inverse = inverse - jnp.einsum("...st,...tu->...su", step, inverse, precision=highest)
+        size *= 2
+    return inverse
+
+
 def span_terms(queries, key_vecs, values, log_decay, write_rate):
     block_len = log_decay.shape[-1]
     cum_decay = jnp.cumsum(log_decay, axis=-1)
@@ -96,16 +115,15 @@
     falloff = jnp.where(inclusive, jnp.exp(jnp.where(inclusive, gap_mat, 0.0)), 0.0)
     key_dots = jnp.einsum("...sd,...td->...st", key_vecs, key_vecs, precision=highest)
     lower_part = jnp.where(strict, write_rate[..., :, None] * falloff * key_dots, 0.0)
-    unit_lower = lower_part + jnp.eye(block_len, dtype=jnp.float32)
-    wy_keys = lax.linalg.triangular_solve(
-        unit_lower,
+    inverse = unit_lower_inverse(lower_part)
+    wy_keys = jnp.einsum(
+        "...st,...td->...sd",
+        inverse,
         (write_rate * jnp.exp(cum_decay))[..., None] * key_vecs,
-        left_side=True,
-        lower=True,
-        unit_diagonal=True,
-    )
-    wy_values = lax.linalg.triangular_solve(
-        unit_lower, write_rate[..., None] * values, left_side=True, lower=True, unit_diagonal=True
+        precision=highest,
+    )
+    wy_values = jnp.einsum(
+        "...st,...td->...sd", inverse, write_rate[..., None] * values, precision=highest
     )
     scores = falloff * jnp.einsum("...sd,...td->...st", queries, key_vecs, precision=highest)
     tail_keys = jnp.exp(cum_decay[..., -1:] - cum_decay)[..., None] * key_vecs
@@ -186,26 +204,44 @@
         to_blocks(log_decay[..., None])[..., 0],
         to_blocks(write_rate[..., None])[..., 0],
     )
-    transition, written, carry_map, local_out = terms
     head_count = values.shape[1]
     identity = jnp.broadcast_to(jnp.eye(DK, dtype=jnp.float32), (head_count, DK, DK))
     empty_state = jnp.zeros((head_count, DK, DV), jnp.float32)
 
     def compose(carried, per_span):
         prefix_a, prefix_b = carried
-        step_trans, step_written = per_span
+        step_trans, step_written, step_carry, step_local = per_span
+        local_mix = (
+            jnp.einsum("hsd,hde->hse", step_carry, prefix_b, precision=highest) + step_local
+        )
+        entry_map = jnp.einsum("hsd,hde->hse", step_carry, prefix_a, precision=highest)
         new_a = jnp.einsum("hde,hef->hdf", step_trans, prefix_a, precision=highest)
-        return ((new_a, apply_shard(step_trans, prefix_b, step_written)), None)
-
-    (shard_a, shard_b), unused = lax.scan(compose, (identity, empty_state), (transition, written))
-
-    def relay(turn_index, state_now):
-        return passed_along(
-            apply_shard(shard_a, state_now, shard_b).astype(jnp.bfloat16), "seq", 1
-        ).astype(jnp.float32)
-
-    state_in = lax.fori_loop(0, lax.axis_size("seq") - 1, relay, empty_state)
-    final_state, produced = lax.scan(advance, state_in, terms)
+        new_b = apply_shard(step_trans, prefix_b, step_written)
+        return ((new_a, new_b), (local_mix, entry_map))
+
+    (shard_a, shard_b), (local_mix, entry_map) = lax.scan(
+        compose, (identity, empty_state), terms
+    )
+
+    shard_count = lax.axis_size("seq")
+    shard_index = lax.axis_index("seq")
+    acc_a, acc_b = shard_a, shard_b
+    distance = 1
+    while distance < shard_count:
+        has_prev = shard_index >= distance
+        prev_b = passed_along(acc_b, "seq", distance)
+        new_b = jnp.where(has_prev, apply_shard(acc_a, prev_b, acc_b), acc_b)
+        if 2 * distance < shard_count:
+            prev_a = passed_along(acc_a, "seq", distance)
+            acc_a = jnp.where(
+                has_prev,
+                jnp.einsum("hde,hef->hdf", acc_a, prev_a, precision=highest),
+                acc_a,
+            )
+        acc_b = new_b
+        distance *= 2
+    state_in = passed_along(acc_b, "seq", 1)
+    produced = local_mix + jnp.einsum("jhsd,hde->jhse", entry_map, state_in, precision=highest)
     produced = produced.transpose(0, 2, 1, 3).reshape(tok_rows, head_count, DV)
     gated = gated_output(produced, zgate, norm_gain)
     return lax.psum_scatter(

time: 414 us -> 211 us (0.51)
  the two profiles are of different devices: /device:TPU:1 before, /device:TPU:0 now
where the time goes in v1:
time: 211 us; the launch traced here: 207 us
  matrix products  79.4 us (38%)
  waiting for transfers between devices  51.8 us (25%)
  starting transfers between devices  39.6 us (19%)
  between operations  14.5 us (7%)
  other arithmetic  11.3 us (5%)
  local copies, waits for them, and re-layouts  10.1 us (5%)
    ppermute x9, starting transfers between devices, passed_along(): return lax.ppermute(block, axis, route)  39.6 us
    reduce_scatter x1, waiting for transfers between devices, on_device(): lax.psum_scatter(jnp.dot(gated, w_out, preferred_element_type=jnp.float32...  38.9 us
    ppermute x9, waiting for transfers between devices, passed_along(): return lax.ppermute(block, axis, route)  12.8 us
    dot_general x6, matrix products, compose(): jnp.einsum('hsd,hde->hse', step_carry, prefix_b, precision=highest)  11.6 us
    dot_general x10, matrix products, apply_shard(): jnp.einsum('hde,hef->hdf', trans_mat, state_now, precision=highest)  11 us
    dot_general x6, matrix products, compose(): new_a = jnp.einsum('hde,hef->hdf', step_trans, prefix_a, precision=highest)  8.04 us
    dot_general x6, matrix products, compose(): jnp.einsum('hsd,hde->hse', step_carry, prefix_a, precision=highest)  6.15 us
    dot_general x5, matrix products, unit_lower_inverse(): jnp.einsum('...st,...tu->...su', step, inverse, precision=highest)  5.8 us
  transfers between devices with their start and end apart: 10, of which 5 were waited for; matrix products, arithmetic and copies ran while one was open for 7% of the time, Pallas kernels for 0%

profile of v1, /device:TPU:0, one launch (start us, length us, event | category | flops | bytes accessed | tf_op | source)
XLA Modules:
  0.0 206.9 jit_solution(7333602692625852869)
XLA Ops:
  6.5 4.1 %fusion.98 = (f32[384,512]{1,0:T(8,128)}, bf16[384,512]{1,0:T(8,128)(2,1)S(1)}) fusion(bf16[384,2048]{1,0:T(8,128)(2,1)} %param.23, bf16[2048,512]{1,0:T(8,128)(2,1)} %param.26), kind=kOutput, calls=%fused_computation.178 | convolution fusion | flops 805699584 | bytes 4849664 | tf_op jit(solution)/shard_map/dot_general | solution.py:27
  12.5 3.5 %collective-permute-start = (bf16[3,1024]{1,0:T(4,128)(2,1)S(1)}, bf16[3,1024]{1,0:T(4,128)(2,1)S(1)}, u32[]{:S(2)}, u32[]{:S(2)}) collective-permute-start(bf16[3,1024]{1,0:T(4,128)(2,1)S(1)} %pad_maximum_fusion.3), channel_id=1, source_target_pairs={{0,8},{8,16},{16,24},{24,32},{32,40},{40,48},{48,56},{56,64},{64,7... | collective-permute-start | bytes 18440 | tf_op jit(solution)/shard_map/ppermute | solution.py:21
  18.5 1.9 fusion.34
  21.2 1.9 reduce_window_sum.11
  27.1 1.9 divide_multiply_fusion.1
  30.6 1.4 multiply_subtract_fusion.1
  40.6 2.0 convolution_subtract_fusion
  42.7 1.4 divide_multiply_fusion
  44.0 2.3 %reshape_reshape.10 = f32[6,64,4,128]{3,2,1,0:T(4,128)} reshape(f32[384,512]{1,0:T(8,128)} %divide_multiply_fusion) | data formatting | bytes 1572864 | tf_op jit(solution)/shard_map/reshape;reshape | solution.py:86
  48.7 1.4 convolution_multiply_fusion
  52.6 1.9 fusion.100
  54.5 3.9 %fusion.62 = f32[6,4,128,128]{3,2,1,0:T(8,128)} fusion(f32[6,4,64,128]{3,2,1,0:T(8,128)S(1)} %fusion.47, f32[6,4,64,128]{3,2,0,1:T(8,128)S(1)} %get-tuple-element.107), kind=kOutput, calls=%fused_computation.99 | convolution fusion | flops 301989888 | bytes 3145728 | tf_op jit(solution)/shard_map/...sd,...se->...de/dot_general | solution.py:134
  59.3 4.2 %multiply_subtract_fusion = f32[6,4,128,128]{3,2,1,0:T(8,128)} fusion(f32[6,4,64,128]{3,2,1,0:T(8,128)S(1)} %fusion.49, f32[128,128]{1,0:T(8,128)S(1)} %copy-done.7, f32[6,4]{1,0:T(8,128)S(1)} %copy.74, f32[6,4,64,128]{3,2,0,1:T(8,128)S(1)} %get-tuple-element.107), kind=kOutput, calls=%fused_computation.28 | convolution fusion | flops 302776320 | bytes 3211360 | tf_op jit(solution)/shard_map/...sd,...se->...de/dot_general | solution.py:131
  63.5 34.8 %while.17 = (s32[]{:T(128)}, f32[4,128,128]{2,1,0:T(8,128)S(1)}, f32[4,128,128]{2,1,0:T(8,128)S(1)}, f32[6,4,64,128]{3,2,0,1:T(8,128)}, f32[6,4,64,128]{3,2,0,1:...) while((s32[]{:T(128)}, f32[4,128,128]{2,1,0:T(8,128)S(1)}, ...), condition=%wide.region_4.5_spmd.clone, body=%wide.region_3.4_spmd.clone.sunk | while | flops 302219264 | bytes 4066936 | solution.py:222
  63.6 1.9 fusion.174
  65.5 1.4 convolution_add_fusion.8
  68.0 1.3 fusion.173
  69.3 1.9 fusion.174
  71.3 1.4 convolution_add_fusion.8
  73.7 1.3 fusion.173
  75.1 1.9 fusion.174
  77.1 1.4 convolution_add_fusion.8
  79.6 1.3 fusion.173
  80.9 1.9 fusion.174
  82.9 1.4 convolution_add_fusion.8
  85.4 1.3 fusion.173
  86.7 1.9 fusion.174
  88.7 1.4 convolution_add_fusion.8
  91.2 1.3 fusion.173
  92.6 1.9 fusion.174
  94.5 1.4 convolution_add_fusion.8
  97.0 1.3 fusion.173
  98.3 3.4 %collective-permute-start.4 = (f32[4,128,128]{2,1,0:T(8,128)S(1)}, f32[4,128,128]{2,1,0:T(8,128)S(1)}, u32[]{:S(2)}, u32[]{:S(2)}) collective-permute-start(f32[4,128,128]{2,1,0:T(8,128)S(1)} %get-tuple-element.57), channel_id=1, source_target_pairs={{0,8},{8,16},{16,24},{24,32},{32,40},{40,48},{48,56},{56,64},{64,7... | collective-permute-start | bytes 786440 | tf_op jit(solution)/shard_map/ppermute | solution.py:21
  101.8 3.1 %collective-permute-start.1 = (f32[4,128,128]{2,1,0:T(8,128)S(1)}, f32[4,128,128]{2,1,0:T(8,128)S(1)}, u32[]{:S(2)}, u32[]{:S(2)}) collective-permute-start(f32[4,128,128]{2,1,0:T(8,128)S(1)} %get-tuple-element.56), channel_id=1, source_target_pairs={{0,8},{8,16},{16,24},{24,32},{32,40},{40,48},{48,56},{56,64},{64,7... | collective-permute-start | bytes 786440 | tf_op jit(solution)/shard_map/ppermute | solution.py:21
  104.9 3.6 %collective-permute-done.4 = f32[4,128,128]{2,1,0:T(8,128)S(1)} collective-permute-done((f32[4,128,128]{2,1,0:T(8,128)S(1)}, f32[4,128,128]{2,1,0:T(8,128)S(1)}, u32[]{:S(2)}, u32[]{:S(2)}) %collective-permute-start.4) | collective-permute-done | bytes 262176 | tf_op jit(solution)/shard_map/ppermute | solution.py:21
  108.9 5.6 %collective-permute-start.5 = (f32[4,128,128]{2,1,0:T(8,128)S(1)}, f32[4,128,128]{2,1,0:T(8,128)S(1)}, u32[]{:S(2)}, u32[]{:S(2)}) collective-permute-start(f32[4,128,128]{2,1,0:T(8,128)S(1)} %fusion.31), channel_id=1, source_target_pairs={{0,16},{8,24},{16,32},{24,40},{32,48},{40,56},{48,64},{56,72},{64,... | collective-permute-start | bytes 786440 | tf_op jit(solution)/shard_map/ppermute | solution.py:21
  115.0 5.8 %collective-permute-start.2 = (f32[4,128,128]{2,1,0:T(8,128)S(1)}, f32[4,128,128]{2,1,0:T(8,128)S(1)}, u32[]{:S(2)}, u32[]{:S(2)}) collective-permute-start(f32[4,128,128]{2,1,0:T(8,128)S(1)} %convolution_select_fusion.2), channel_id=1, source_target_pairs={{0,16},{8,24},{16,32},{24,40},{32,48},{40,56},{48,64},{56,72},{64,... | collective-permute-start | bytes 786440 | tf_op jit(solution)/shard_map/ppermute | solution.py:21
  121.2 7.0 %collective-permute-start.6 = (f32[4,128,128]{2,1,0:T(8,128)S(1)}, f32[4,128,128]{2,1,0:T(8,128)}, u32[]{:S(2)}, u32[]{:S(2)}) collective-permute-start(f32[4,128,128]{2,1,0:T(8,128)S(1)} %fusion.30), channel_id=1, source_target_pairs={{0,32},{8,40},{16,48},{24,56},{32,64},{40,72},{48,80},{56,88},{64,... | collective-permute-start | bytes 786440 | tf_op jit(solution)/shard_map/ppermute | solution.py:21
  128.6 3.7 %collective-permute-start.3 = (f32[4,128,128]{2,1,0:T(8,128)S(1)}, f32[4,128,128]{2,1,0:T(8,128)S(1)}, u32[]{:S(2)}, u32[]{:S(2)}) collective-permute-start(f32[4,128,128]{2,1,0:T(8,128)S(1)} %convolution_select_fusion.1), channel_id=1, source_target_pairs={{0,32},{8,40},{16,48},{24,56},{32,64},{40,72},{48,80},{56,88},{64,... | collective-permute-start | bytes 786440 | tf_op jit(solution)/shard_map/ppermute | solution.py:21
  132.3 1.9 collective-permute-done.6
  134.2 1.3 fusion.29
  135.6 6.1 %collective-permute-start.7 = (f32[4,128,128]{2,1,0:T(8,128)S(1)}, f32[4,128,128]{2,1,0:T(8,128)S(1)}, u32[]{:S(2)}, u32[]{:S(2)}) collective-permute-start(f32[4,128,128]{2,1,0:T(8,128)S(1)} %fusion.29), channel_id=1, source_target_pairs={{0,64},{8,72},{16,80},{24,88},{32,96},{40,104},{48,112},{56,120},{... | collective-permute-start | bytes 786440 | tf_op jit(solution)/shard_map/ppermute | solution.py:21
  142.1 3.4 %collective-permute-done.7 = f32[4,128,128]{2,1,0:T(8,128)S(1)} collective-permute-done((f32[4,128,128]{2,1,0:T(8,128)S(1)}, f32[4,128,128]{2,1,0:T(8,128)S(1)}, u32[]{:S(2)}, u32[]{:S(2)}) %collective-permute-start.7) | collective-permute-done | bytes 262176 | tf_op jit(solution)/shard_map/ppermute | solution.py:21
  147.3 3.8 %collective-permute-done.8 = f32[4,128,128]{2,1,0:T(8,128)S(1)} collective-permute-done((f32[4,128,128]{2,1,0:T(8,128)S(1)}, f32[4,128,128]{2,1,0:T(8,128)S(1)}, u32[]{:S(2)}, u32[]{:S(2)}) %collective-permute-start.8) | collective-permute-done | bytes 262176 | tf_op jit(solution)/shard_map/ppermute | solution.py:21
  151.1 2.3 %multiply_reduce_fusion = (f32[6,64,4]{1,0,2:T(8,128)S(1)}, f32[6,64,4,128]{3,1,0,2:T(8,128)S(1)}) fusion(f32[6,4,64,128]{3,2,0,1:T(8,128)} %get-tuple-element.55, f32[6,4,64,128]{3,2,0,1:T(8,128)} %get-tuple-element.58, f32[4,128,128]{2,1,0:T(8,128)S(1)} %collective-permute-done.8), kind=kOutput, calls=%fused_computation.84 | convolution fusion | flops 302578176 | bytes 2627584 | tf_op jit(solution)/shard_map/jhsd,hde->jhse/dot_general | solution.py:244
  153.6 1.4 copy.91
  155.5 5.4 %convolution_convert_fusion = bf16[384,2048]{1,0:T(8,128)(2,1)} fusion(bf16[512,2048]{1,0:T(8,128)(2,1)S(1)} %copy-done, f32[48,8,4,128]{3,2,1,0:T(4,128)S(1)} %bitcast.186, f32[48,8,4,128]{3,2,1,0:T(4,128)} %bitcast.185, bf16[384,2048]{1,0:T(8,128)(2,1)} %param.23, bf16[2048,512]{1,0:T(8,128)(2,1)} %param.27, f32[512]{0:T(512)S(1)} %broadcast_bitcast_fusion), kind=kOutput, calls=%fused_computation.27 | convolution fusion | flops 1613365248 | bytes 8914944 | tf_op jit(solution)/shard_map/dot_general | solution.py:248
  160.9 38.9 %reduce-scatter.2.cloned.1.call-done = bf16[48,2048]{1,0:T(8,128)(2,1)} async-done(((bf16[384,2048]{1,0:T(8,128)(2,1)}), bf16[48,2048]{1,0:T(8,128)(2,1)}) %reduce-scatter.2.cloned.1.call-update) | async-done | bytes 196624 | tf_op jit(solution)/shard_map/reduce_scatter | solution.py:247
  (167 shorter events, 35.4 us)
Async XLA Ops:
  6.5 149.0 %copy-start = (bf16[512,2048]{1,0:T(8,128)(2,1)S(1)}, bf16[512,2048]{1,0:T(8,128)(2,1)}, u32[]{:S(2)}) copy-start(bf16[512,2048]{1,0:T(8,128)(2,1)} %param.36) | copy-start | bytes 6291460
  6.5 193.3 %reduce-scatter.2.cloned.1.call-start = ((), (), s32[]{:S(2)}) async-start(), calls=%async_computation.1 | async-start | bytes 1769472 | tf_op jit(solution)/shard_map/reduce_scatter | solution.py:247
  6.5 4.1 %copy-start.1 = (bf16[384,2048]{1,0:T(8,128)(2,1)S(1)}, bf16[384,2048]{1,0:T(8,128)(2,1)}, u32[]{:S(2)}) copy-start(bf16[384,2048]{1,0:T(8,128)(2,1)} %param.23) | copy-start | bytes 4718596
  6.5 4.1 %copy-start.4 = (bf16[2048,256]{1,0:T(8,128)(2,1)S(1)}, bf16[2048,256]{1,0:T(8,128)(2,1)}, u32[]{:S(2)}) copy-start(bf16[2048,256]{1,0:T(8,128)(2,1)} %param.24) | copy-start | bytes 3145732
  10.7 1.2 copy-start.5
  11.9 4.8 %copy-start.30 = (bf16[4,256]{1,0:T(4,128)(2,1)S(1)}, bf16[4,256]{1,0:T(4,128)(2,1)}, u32[]{:S(2)}) copy-start(bf16[4,256]{1,0:T(4,128)(2,1)} %param.30) | copy-start | bytes 6148
  11.9 5.4 %copy-start.31 = (bf16[4,256]{1,0:T(4,128)(2,1)S(1)}, bf16[4,256]{1,0:T(4,128)(2,1)}, u32[]{:S(2)}) copy-start(bf16[4,256]{1,0:T(4,128)(2,1)} %param.31) | copy-start | bytes 6148
  11.9 6.0 %copy-start.34 = (f32[4]{0:T(128)S(1)}, f32[4]{0:T(128)}, u32[]{:S(2)}) copy-start(f32[4]{0:T(128)} %param.33) | copy-start | bytes 52
  11.9 6.0 %copy-start.20 = (bf16[2048,4]{0,1:T(4,128)(2,1)S(1)}, bf16[2048,4]{0,1:T(4,128)(2,1)}, u32[]{:S(2)}) copy-start(bf16[2048,4]{0,1:T(4,128)(2,1)} %param.28) | copy-start | bytes 49156
  11.9 6.0 %copy-start.32 = (f32[4]{0:T(128)S(1)}, f32[4]{0:T(128)}, u32[]{:S(2)}) copy-start(f32[4]{0:T(128)} %param.34) | copy-start | bytes 52
  12.5 6.1 %copy-start.21 = (bf16[2048,4]{0,1:T(4,128)(2,1)S(1)}, bf16[2048,4]{0,1:T(4,128)(2,1)}, u32[]{:S(2)}) copy-start(bf16[2048,4]{0,1:T(4,128)(2,1)} %param.29) | copy-start | bytes 49156
  12.5 13.9 %collective-permute-start = (bf16[3,1024]{1,0:T(4,128)(2,1)S(1)}, bf16[3,1024]{1,0:T(4,128)(2,1)S(1)}, u32[]{:S(2)}, u32[]{:S(2)}) collective-permute-start(bf16[3,1024]{1,0:T(4,128)(2,1)S(1)} %pad_maximum_fusion.3), channel_id=1, source_target_pairs={{0,8},{8,16},{16,24},{24,32},{32,40},{40,48},{48,56},{56,64},{64,7... | collective-permute-start | bytes 18440 | tf_op jit(solution)/shard_map/ppermute | solution.py:21
  17.9 2.7 %copy-start.22 = (bf16[4,512]{1,0:T(4,128)(2,1)S(1)}, bf16[4,512]{1,0:T(4,128)(2,1)}, u32[]{:S(2)}) copy-start(bf16[4,512]{1,0:T(4,128)(2,1)} %param.32) | copy-start | bytes 12292
  26.5 0.6 copy-start.27
  29.7 0.7 copy-start.10
  29.8 0.7 copy-start.18
  29.8 0.7 copy-start.29
  29.8 0.8 copy-start.35
  29.8 0.8 copy-start.36
  30.4 1.6 copy-start.17
  32.9 1.0 copy-start.16
  34.9 0.9 copy-start.15
  36.7 1.0 copy-start.14
  38.6 1.0 copy-start.13
  40.6 2.1 copy-start.28
  40.6 2.0 copy-start.6
  40.6 2.0 copy-start.23
  40.6 2.0 copy-start.24
  40.6 2.0 copy-start.25
  40.6 2.0 copy-start.26
  48.0 0.7 copy-start.19
  48.6 1.6 copy-start.2
  48.6 1.6 copy-start.3
  48.6 1.6 copy-start.11
  50.2 1.0 copy-start.8
  50.2 1.0 copy-start.9
  54.5 3.9 %copy-start.12 = (f32[6,4,64]{2,1,0:T(4,128)S(1)}, f32[6,4,64]{2,1,0:T(4,128)}, u32[]{:S(2)}) copy-start(f32[6,4,64]{2,1,0:T(4,128)} %get-tuple-element.109) | copy-start | bytes 18436
  58.3 1.0 copy-start.7
  98.3 10.1 %collective-permute-start.4 = (f32[4,128,128]{2,1,0:T(8,128)S(1)}, f32[4,128,128]{2,1,0:T(8,128)S(1)}, u32[]{:S(2)}, u32[]{:S(2)}) collective-permute-start(f32[4,128,128]{2,1,0:T(8,128)S(1)} %get-tuple-element.57), channel_id=1, source_target_pairs={{0,8},{8,16},{16,24},{24,32},{32,40},{40,48},{48,56},{56,64},{64,7... | collective-permute-start | bytes 786440 | tf_op jit(solution)/shard_map/ppermute | solution.py:21
  101.8 12.8 %collective-permute-start.1 = (f32[4,128,128]{2,1,0:T(8,128)S(1)}, f32[4,128,128]{2,1,0:T(8,128)S(1)}, u32[]{:S(2)}, u32[]{:S(2)}) collective-permute-start(f32[4,128,128]{2,1,0:T(8,128)S(1)} %get-tuple-element.56), channel_id=1, source_target_pairs={{0,8},{8,16},{16,24},{24,32},{32,40},{40,48},{48,56},{56,64},{64,7... | collective-permute-start | bytes 786440 | tf_op jit(solution)/shard_map/ppermute | solution.py:21
  108.9 11.9 %collective-permute-start.5 = (f32[4,128,128]{2,1,0:T(8,128)S(1)}, f32[4,128,128]{2,1,0:T(8,128)S(1)}, u32[]{:S(2)}, u32[]{:S(2)}) collective-permute-start(f32[4,128,128]{2,1,0:T(8,128)S(1)} %fusion.31), channel_id=1, source_target_pairs={{0,16},{8,24},{16,32},{24,40},{32,48},{40,56},{48,64},{56,72},{64,... | collective-permute-start | bytes 786440 | tf_op jit(solution)/shard_map/ppermute | solution.py:21
  115.0 13.2 %collective-permute-start.2 = (f32[4,128,128]{2,1,0:T(8,128)S(1)}, f32[4,128,128]{2,1,0:T(8,128)S(1)}, u32[]{:S(2)}, u32[]{:S(2)}) collective-permute-start(f32[4,128,128]{2,1,0:T(8,128)S(1)} %convolution_select_fusion.2), channel_id=1, source_target_pairs={{0,16},{8,24},{16,32},{24,40},{32,48},{40,56},{48,64},{56,72},{64,... | collective-permute-start | bytes 786440 | tf_op jit(solution)/shard_map/ppermute | solution.py:21
  121.2 13.0 %collective-permute-start.6 = (f32[4,128,128]{2,1,0:T(8,128)S(1)}, f32[4,128,128]{2,1,0:T(8,128)}, u32[]{:S(2)}, u32[]{:S(2)}) collective-permute-start(f32[4,128,128]{2,1,0:T(8,128)S(1)} %fusion.30), channel_id=1, source_target_pairs={{0,32},{8,40},{16,48},{24,56},{32,64},{40,72},{48,80},{56,88},{64,... | collective-permute-start | bytes 786440 | tf_op jit(solution)/shard_map/ppermute | solution.py:21
  128.6 18.7 %copy-start.33 = (f32[128]{0:T(128)S(1)}, f32[128]{0:T(128)}, u32[]{:S(2)}) copy-start(f32[128]{0:T(128)} %param.35) | copy-start | bytes 1540
  128.6 13.1 %collective-permute-start.3 = (f32[4,128,128]{2,1,0:T(8,128)S(1)}, f32[4,128,128]{2,1,0:T(8,128)S(1)}, u32[]{:S(2)}, u32[]{:S(2)}) collective-permute-start(f32[4,128,128]{2,1,0:T(8,128)S(1)} %convolution_select_fusion.1), channel_id=1, source_target_pairs={{0,32},{8,40},{16,48},{24,56},{32,64},{40,72},{48,80},{56,88},{64,... | collective-permute-start | bytes 786440 | tf_op jit(solution)/shard_map/ppermute | solution.py:21
  135.6 10.0 %collective-permute-start.7 = (f32[4,128,128]{2,1,0:T(8,128)S(1)}, f32[4,128,128]{2,1,0:T(8,128)S(1)}, u32[]{:S(2)}, u32[]{:S(2)}) collective-permute-start(f32[4,128,128]{2,1,0:T(8,128)S(1)} %fusion.29), channel_id=1, source_target_pairs={{0,64},{8,72},{16,80},{24,88},{32,96},{40,104},{48,112},{56,120},{... | collective-permute-start | bytes 786440 | tf_op jit(solution)/shard_map/ppermute | solution.py:21
  146.0 5.2 %collective-permute-start.8 = (f32[4,128,128]{2,1,0:T(8,128)S(1)}, f32[4,128,128]{2,1,0:T(8,128)S(1)}, u32[]{:S(2)}, u32[]{:S(2)}) collective-permute-start(f32[4,128,128]{2,1,0:T(8,128)S(1)} %fusion.28), channel_id=1, source_target_pairs={{0,8},{8,16},{16,24},{24,32},{32,40},{40,48},{48,56},{56,64},{64,7... | collective-permute-start | bytes 786440 | tf_op jit(solution)/shard_map/ppermute | solution.py:21
Sparse Core Ops, SparseCore 0:
  161.0 38.7 reduce-scatter.1

commit v2 on v1

--- a/solution.py
+++ b/solution.py
@@ -1,8 +1,14 @@
+import functools
+
 import jax
 import numpy as np
 import jax.numpy as jnp
 from jax import lax
+from jax.experimental import pallas as pl
+from jax.experimental.pallas import tpu as pltpu
 from jax.sharding import PartitionSpec as P
+
+MESH = pl.DeviceIdType.MESH
 
 VH = 32
 KH = 16
@@ -158,6 +164,69 @@
     return jnp.einsum("hde,hef->hdf", trans_mat, state_now, precision=highest) + written
 
 
+def group_sum_kernel(group_count, part_ref, out_ref, landed, send_sems, recv_sems, own_sem):
+    me = lax.axis_index("hg")
+    seq_me = lax.axis_index("seq")
+    rows = out_ref.shape[0]
+    barrier = pltpu.get_barrier_semaphore()
+    for step in range(1, group_count):
+        peer = lax.rem(me + step, group_count)
+        pl.semaphore_signal(barrier, inc=1, device_id=(seq_me, peer), device_id_type=MESH)
+    pl.semaphore_wait(barrier, group_count - 1)
+    sends = []
+    for step in range(1, group_count):
+        peer = lax.rem(me + step, group_count)
+        copy = pltpu.make_async_remote_copy(
+            src_ref=part_ref.at[pl.ds(pl.multiple_of(peer * rows, 8), rows)],
+            dst_ref=landed.at[me],
+            send_sem=send_sems.at[step],
+            recv_sem=recv_sems.at[me],
+            device_id=(seq_me, peer),
+            device_id_type=MESH,
+        )
+        copy.start()
+        sends.append(copy)
+    own = pltpu.make_async_copy(
+        part_ref.at[pl.ds(pl.multiple_of(me * rows, 8), rows)], landed.at[me], own_sem
+    )
+    own.start()
+    own.wait()
+    for step in range(1, group_count):
+        source = lax.rem(me + group_count - step, group_count)
+        pltpu.make_async_remote_copy(
+            src_ref=part_ref.at[pl.ds(0, rows)],
+            dst_ref=landed.at[source],
+            send_sem=send_sems.at[step],
+            recv_sem=recv_sems.at[source],
+            device_id=(seq_me, source),
+            device_id_type=MESH,
+        ).wait_recv()
+    for copy in sends:
+        copy.wait_send()
+    total = landed[0].astype(jnp.float32)
+    for slot in range(1, group_count):
+        total = total + landed[slot].astype(jnp.float32)
+    out_ref[...] = total.astype(out_ref.dtype)
+
+
+def group_sum(part, group_count):
+    rows = part.shape[0] // group_count
+    cols = part.shape[1]
+    return pl.pallas_call(
+        functools.partial(group_sum_kernel, group_count),
+        out_shape=jax.ShapeDtypeStruct((rows, cols), part.dtype),
+        in_specs=[pl.BlockSpec(memory_space=pltpu.VMEM)],
+        out_specs=pl.BlockSpec(memory_space=pltpu.VMEM),
+        scratch_shapes=[
+            pltpu.VMEM((group_count, rows, cols), part.dtype),
+            pltpu.SemaphoreType.DMA((group_count,)),
+            pltpu.SemaphoreType.DMA((group_count,)),
+            pltpu.SemaphoreType.DMA,
+        ],
+        compiler_params=pltpu.CompilerParams(collective_id=0, has_side_effects=True),
+    )(part)
+
+
 def on_device(
     hidden_in,
     w_query,
@@ -220,7 +289,7 @@
         return ((new_a, new_b), (local_mix, entry_map))
 
     (shard_a, shard_b), (local_mix, entry_map) = lax.scan(
-        compose, (identity, empty_state), terms
+        compose, (identity, empty_state), terms, unroll=True
     )
 
     shard_count = lax.axis_size("seq")
@@ -244,12 +313,8 @@
     produced = local_mix + jnp.einsum("jhsd,hde->jhse", entry_map, state_in, precision=highest)
     produced = produced.transpose(0, 2, 1, 3).reshape(tok_rows, head_count, DV)
     gated = gated_output(produced, zgate, norm_gain)
-    return lax.psum_scatter(
-        jnp.dot(gated, w_out, preferred_element_type=jnp.float32).astype(jnp.bfloat16),
-        "hg",
-        scatter_dimension=0,
-        tiled=True,
-    )
+    part = jnp.dot(gated, w_out, preferred_element_type=jnp.float32).astype(jnp.bfloat16)
+    return group_sum(part, lax.axis_size("hg"))
 
 
 def solution(mesh):

time: 211 us -> 152 us (0.72)
  the two profiles are of different devices: /device:TPU:0 before, /device:TPU:17 now
where the time goes in v2:
time: 152 us; the launch traced here: 149 us
  matrix products  50.3 us (33%)
  Pallas kernels  30 us (20%)
  waiting for transfers between devices  28.2 us (19%)
  starting transfers between devices  23.3 us (15%)
  local copies, waits for them, and re-layouts  9.35 us (6%)
  other arithmetic  7.12 us (5%)
    pallas_call x1, Pallas kernels, group_sum(): pl.pallas_call(functools.partial(group_sum_kernel, group_count), out_shap...  30 us
    ppermute x9, waiting for transfers between devices, passed_along(): return lax.ppermute(block, axis, route)  28.2 us
    ppermute x9, starting transfers between devices, passed_along(): return lax.ppermute(block, axis, route)  23.3 us
    dot_general x5, matrix products, unit_lower_inverse(): jnp.einsum('...st,...tu->...su', step, inverse, precision=highest)  5.63 us
    dot_general x1, matrix products, on_device(): jnp.dot(gated, w_out, preferred_element_type=jnp.float32)  5.38 us
    dot_general x5, matrix products, unit_lower_inverse(): jnp.einsum('...st,...tu->...su', inverse, off_blocks, precision=highest)  4.77 us
    dot_general x10, matrix products, apply_shard(): jnp.einsum('hde,hef->hdf', trans_mat, state_now, precision=highest)  3.95 us
  transfers between devices with their start and end apart: 9, of which 8 were waited for; matrix products, arithmetic and copies ran while one was open for 7% of the time, Pallas kernels for 0%

profile of v2, /device:TPU:17, one launch (start us, length us, event | category | flops | bytes accessed | tf_op | source)
XLA Modules:
  0.0 149.5 jit_solution(1475161866333156643)
XLA Ops:
  0.0 2.4 %fusion.102 = (f32[384,256]{1,0:T(8,128)S(1)}, bf16[384,256]{1,0:T(8,128)(2,1)S(1)}) fusion(bf16[384,2048]{1,0:T(8,128)(2,1)} %param.21, bf16[2048,256]{1,0:T(8,128)(2,1)} %param.23), kind=kOutput, calls=%fused_computation.221 | convolution fusion | flops 402849792 | bytes 3211264 | tf_op jit(solution)/shard_map/dot_general | solution.py:32
  3.0 1.9 %fusion.104 = (f32[384,512]{1,0:T(8,128)}, bf16[384,512]{1,0:T(8,128)(2,1)S(1)}) fusion(bf16[384,2048]{1,0:T(8,128)(2,1)S(1)} %copy-done.1, bf16[2048,512]{1,0:T(8,128)(2,1)S(1)} %copy-done.20), kind=kOutput, calls=%fused_computation.223 | convolution fusion | flops 805699584 | bytes 4849664 | tf_op jit(solution)/shard_map/dot_general | solution.py:33
  5.6 3.1 %collective-permute-start = (bf16[3,1024]{1,0:T(4,128)(2,1)S(1)}, bf16[3,1024]{1,0:T(4,128)(2,1)S(1)}, u32[]{:S(2)}, u32[]{:S(2)}) collective-permute-start(bf16[3,1024]{1,0:T(4,128)(2,1)S(1)} %pad_maximum_fusion.3), channel_id=1, source_target_pairs={{0,8},{8,16},{16,24},{24,32},{32,40},{40,48},{48,56},{56,64},{64,7... | collective-permute-start | bytes 18440 | tf_op jit(solution)/shard_map/ppermute | solution.py:27
  9.5 1.9 %fusion.28 = f32[384,4]{0,1:T(4,128)S(1)} fusion(bf16[384,2048]{1,0:T(8,128)(2,1)} %param.21, bf16[2048,4]{0,1:T(4,128)(2,1)S(1)} %copy-done.14), kind=kOutput, calls=%fused_computation.72 | convolution fusion | flops 6296064 | bytes 1595392 | tf_op jit(solution)/shard_map/dot_general | solution.py:86
  11.5 1.9 %reduce_window_sum.11 = f32[6,4,64]{2,1,0:T(4,128)S(1)} reduce-window(f32[6,4,64]{2,1,0:T(4,128)S(1)} %copy.69, f32[]{:T(128)} %constant.18.clone.1), window={size=1x1x64 pad=0_0x0_0x63_0}, to_apply=%region_0.1 | reduce-window | flops 96768 | bytes 12292 | tf_op jit(solution)/shard_map/jit(cumsum)/reduce_window_sum | solution.py:115
  14.0 1.2 divide_multiply_fusion.1
  15.3 1.2 reshape.82
  18.9 2.3 %convolution_multiply_fusion.1 = f32[6,4,64,64]{3,2,1,0:T(8,128)} fusion(f32[6,4,64,128]{3,2,0,1:T(8,128)S(1)} %bitcast.296, f32[6,64,4,128]{3,1,0,2:T(8,128)S(1)} %bitcast.294, f32[6,4,64]{2,1,0:T(4,128)S(1)} %reduce_window_sum.11, pred[64,64]{1,0:T(8,128)(4,1)S(1)} %get-tuple-element.36), kind=kOutput, calls=%fused_computation.13 | convolution fusion | flops 151388160 | bytes 1976320 | tf_op jit(solution)/shard_map/...sd,...td->...st/dot_general | solution.py:134
  21.2 1.4 multiply_subtract_fusion.1
  22.7 0.9 fusion.53
  23.6 1.0 convolution_subtract_fusion.4
  24.6 0.9 fusion.51
  25.5 0.9 convolution_subtract_fusion.3
  26.5 0.9 fusion.49
  27.4 1.0 convolution_subtract_fusion.2
  28.4 1.1 fusion.47
  29.5 1.0 convolution_subtract_fusion.1
  30.5 0.9 fusion.45
  31.4 1.8 %convolution_subtract_fusion = f32[6,4,64,64]{3,2,1,0:T(8,128)} fusion(f32[6,4,64,64]{3,2,1,0:T(8,128)S(1)} %convolution_subtract_fusion.1, f32[6,4,64,64]{3,2,1,0:T(8,128)S(1)} %fusion.45), kind=kOutput, calls=%fused_computation.2 | convolution fusion | flops 75595776 | bytes 1179648 | tf_op jit(solution)/shard_map/...st,...tu->...su/dot_general | solution.py:108
  33.2 1.4 divide_multiply_fusion
  34.6 2.3 %reshape_reshape.11 = f32[6,64,4,128]{3,2,1,0:T(4,128)} reshape(f32[384,512]{1,0:T(8,128)} %divide_multiply_fusion) | data formatting | bytes 1572864 | tf_op jit(solution)/shard_map/reshape;reshape | solution.py:92
  36.9 2.4 %fusion.40 = f32[6,4,64,128]{3,2,1,0:T(8,128)S(1)} fusion(f32[6,4,64,64]{3,2,1,0:T(8,128)} %convolution_subtract_fusion, f32[6,64,4,128]{3,2,1,0:T(4,128)} %reshape_reshape.11, f32[6,4,64]{2,1,0:T(4,128)S(1)} %bitcast.304), kind=kOutput, calls=%fused_computation.87 | convolution fusion | flops 151191552 | bytes 1972224 | tf_op jit(solution)/shard_map/...st,...td->...sd/dot_general | solution.py:131
  40.4 0.9 fusion.43
  41.4 0.9 fusion.105
  42.3 2.6 %fusion.55 = f32[6,4,128,128]{3,2,1,0:T(8,128)S(1)} fusion(f32[6,4,64,128]{3,2,1,0:T(8,128)S(1)} %fusion.40, f32[6,4,64,128]{3,2,0,1:T(8,128)S(1)} %get-tuple-element.5), kind=kOutput, calls=%fused_computation.107 | convolution fusion | flops 301989888 | bytes 3145728 | tf_op jit(solution)/shard_map/...sd,...se->...de/dot_general | solution.py:140
  44.9 1.0 convolution_subtract_fusion.5
  46.5 3.0 %multiply_subtract_fusion = f32[6,4,128,128]{3,2,1,0:T(8,128)S(1)} fusion(f32[6,4,64,128]{3,2,1,0:T(8,128)S(1)} %fusion.43, f32[128,128]{1,0:T(8,128)S(1)} %fusion.96, f32[6,4]{1,0:T(8,128)S(1)} %copy.81, f32[6,4,64,128]{3,2,0,1:T(8,128)S(1)} %get-tuple-element.5), kind=kOutput, calls=%fused_computation.1 | convolution fusion | flops 302776320 | bytes 3211360 | tf_op jit(solution)/shard_map/...sd,...se->...de/dot_general | solution.py:137
  55.4 3.1 %collective-permute-start.4 = (f32[4,128,128]{2,1,0:T(8,128)S(1)}, f32[4,128,128]{2,1,0:T(8,128)S(1)}, u32[]{:S(2)}, u32[]{:S(2)}) collective-permute-start(f32[4,128,128]{2,1,0:T(8,128)S(1)} %convolution_add_fusion.4), channel_id=1, source_target_pairs={{0,8},{8,16},{16,24},{24,32},{32,40},{40,48},{48,56},{56,64},{64,7... | collective-permute-start | bytes 786440 | tf_op jit(solution)/shard_map/ppermute | solution.py:27
  58.9 2.8 %collective-permute-start.1 = (f32[4,128,128]{2,1,0:T(8,128)S(1)}, f32[4,128,128]{2,1,0:T(8,128)S(1)}, u32[]{:S(2)}, u32[]{:S(2)}) collective-permute-start(f32[4,128,128]{2,1,0:T(8,128)S(1)} %fusion.91), channel_id=1, source_target_pairs={{0,8},{8,16},{16,24},{24,32},{32,40},{40,48},{48,56},{56,64},{64,7... | collective-permute-start | bytes 786440 | tf_op jit(solution)/shard_map/ppermute | solution.py:27
  62.1 4.2 %collective-permute-done.4 = f32[4,128,128]{2,1,0:T(8,128)S(1)} collective-permute-done((f32[4,128,128]{2,1,0:T(8,128)S(1)}, f32[4,128,128]{2,1,0:T(8,128)S(1)}, u32[]{:S(2)}, u32[]{:S(2)}) %collective-permute-start.4) | collective-permute-done | bytes 262176 | tf_op jit(solution)/shard_map/ppermute | solution.py:27
  66.6 2.2 %collective-permute-start.5 = (f32[4,128,128]{2,1,0:T(8,128)S(1)}, f32[4,128,128]{2,1,0:T(8,128)S(1)}, u32[]{:S(2)}, u32[]{:S(2)}) collective-permute-start(f32[4,128,128]{2,1,0:T(8,128)S(1)} %fusion.7), channel_id=1, source_target_pairs={{0,16},{8,24},{16,32},{24,40},{32,48},{40,56},{48,64},{56,72},{64,... | collective-permute-start | bytes 786440 | tf_op jit(solution)/shard_map/ppermute | solution.py:27
  69.3 2.6 %collective-permute-done.1 = f32[4,128,128]{2,1,0:T(8,128)S(1)} collective-permute-done((f32[4,128,128]{2,1,0:T(8,128)S(1)}, f32[4,128,128]{2,1,0:T(8,128)S(1)}, u32[]{:S(2)}, u32[]{:S(2)}) %collective-permute-start.1) | collective-permute-done | bytes 262176 | tf_op jit(solution)/shard_map/ppermute | solution.py:27
  72.3 2.7 %collective-permute-start.2 = (f32[4,128,128]{2,1,0:T(8,128)S(1)}, f32[4,128,128]{2,1,0:T(8,128)S(1)}, u32[]{:S(2)}, u32[]{:S(2)}) collective-permute-start(f32[4,128,128]{2,1,0:T(8,128)S(1)} %convolution_select_fusion.2), channel_id=1, source_target_pairs={{0,16},{8,24},{16,32},{24,40},{32,48},{40,56},{48,64},{56,72},{64,... | collective-permute-start | bytes 786440 | tf_op jit(solution)/shard_map/ppermute | solution.py:27
  74.9 1.2 collective-permute-done.5
  76.6 2.9 %collective-permute-start.6 = (f32[4,128,128]{2,1,0:T(8,128)S(1)}, f32[4,128,128]{2,1,0:T(8,128)S(1)}, u32[]{:S(2)}, u32[]{:S(2)}) collective-permute-start(f32[4,128,128]{2,1,0:T(8,128)S(1)} %fusion.6), channel_id=1, source_target_pairs={{0,32},{8,40},{16,48},{24,56},{32,64},{40,72},{48,80},{56,88},{64,... | collective-permute-start | bytes 786440 | tf_op jit(solution)/shard_map/ppermute | solution.py:27
  79.8 4.6 %collective-permute-done.2 = f32[4,128,128]{2,1,0:T(8,128)S(1)} collective-permute-done((f32[4,128,128]{2,1,0:T(8,128)S(1)}, f32[4,128,128]{2,1,0:T(8,128)S(1)}, u32[]{:S(2)}, u32[]{:S(2)}) %collective-permute-start.2) | collective-permute-done | bytes 262176 | tf_op jit(solution)/shard_map/ppermute | solution.py:27
  84.8 2.9 %collective-permute-start.3 = (f32[4,128,128]{2,1,0:T(8,128)S(1)}, f32[4,128,128]{2,1,0:T(8,128)S(1)}, u32[]{:S(2)}, u32[]{:S(2)}) collective-permute-start(f32[4,128,128]{2,1,0:T(8,128)S(1)} %convolution_select_fusion.1), channel_id=1, source_target_pairs={{0,32},{8,40},{16,48},{24,56},{32,64},{40,72},{48,80},{56,88},{64,... | collective-permute-start | bytes 786440 | tf_op jit(solution)/shard_map/ppermute | solution.py:27
  87.8 2.5 %collective-permute-done.6 = f32[4,128,128]{2,1,0:T(8,128)S(1)} collective-permute-done((f32[4,128,128]{2,1,0:T(8,128)S(1)}, f32[4,128,128]{2,1,0:T(8,128)S(1)}, u32[]{:S(2)}, u32[]{:S(2)}) %collective-permute-start.6) | collective-permute-done | bytes 262176 | tf_op jit(solution)/shard_map/ppermute | solution.py:27
  90.7 1.3 collective-permute-start.7
  92.3 3.5 %collective-permute-done.3 = f32[4,128,128]{2,1,0:T(8,128)S(1)} collective-permute-done((f32[4,128,128]{2,1,0:T(8,128)S(1)}, f32[4,128,128]{2,1,0:T(8,128)S(1)}, u32[]{:S(2)}, u32[]{:S(2)}) %collective-permute-start.3) | collective-permute-done | bytes 262176 | tf_op jit(solution)/shard_map/ppermute | solution.py:27
  96.3 3.3 %collective-permute-done.7 = f32[4,128,128]{2,1,0:T(8,128)S(1)} collective-permute-done((f32[4,128,128]{2,1,0:T(8,128)S(1)}, f32[4,128,128]{2,1,0:T(8,128)S(1)}, u32[]{:S(2)}, u32[]{:S(2)}) %collective-permute-start.7) | collective-permute-done | bytes 262176 | tf_op jit(solution)/shard_map/ppermute | solution.py:27
  100.0 2.2 %collective-permute-start.8 = (f32[4,128,128]{2,1,0:T(8,128)S(1)}, f32[4,128,128]{2,1,0:T(8,128)S(1)}, u32[]{:S(2)}, u32[]{:S(2)}) collective-permute-start(f32[4,128,128]{2,1,0:T(8,128)S(1)} %fusion.4), channel_id=1, source_target_pairs={{0,8},{8,16},{16,24},{24,32},{32,40},{40,48},{48,56},{56,64},{64,7... | collective-permute-start | bytes 786440 | tf_op jit(solution)/shard_map/ppermute | solution.py:27
  102.9 6.3 %collective-permute-done.8 = f32[4,128,128]{2,1,0:T(8,128)S(1)} collective-permute-done((f32[4,128,128]{2,1,0:T(8,128)S(1)}, f32[4,128,128]{2,1,0:T(8,128)S(1)}, u32[]{:S(2)}, u32[]{:S(2)}) %collective-permute-start.8) | collective-permute-done | bytes 262176 | tf_op jit(solution)/shard_map/ppermute | solution.py:27
  109.2 1.0 multiply_reduce_fusion
  110.4 1.4 copy.86
  112.3 5.4 %convolution_convert_fusion.part_ref = bf16[384,2048]{1,0:T(8,128)(2,1)} fusion(bf16[512,2048]{1,0:T(8,128)(2,1)S(1)} %copy-done, f32[48,8,4,128]{3,2,1,0:T(4,128)S(1)} %bitcast.300, f32[48,8,4,128]{3,2,1,0:T(4,128)} %bitcast.299, bf16[384,2048]{1,0:T(8,128)(2,1)} %param.21, bf16[2048,512]{1,0:T(8,128)(2,1)} %param.25, f32[512]{0:T(512)S(1)} %broadcast_bitcast_fusion), kind=kOutput, calls=%fused_computation | convolution fusion | flops 1613365248 | bytes 8914944 | tf_op jit(solution)/shard_map/dot_general | solution.py:316
  117.6 30.0 %shard_map.199 = bf16[48,2048]{1,0:T(8,128)(2,1)} custom-call(bf16[384,2048]{1,0:T(8,128)(2,1)} %convolution_convert_fusion.part_ref), custom_call_target="tpu_custom_call" | custom-call | tf_op jit(solution)/shard_map/pallas_call | solution.py:215
  147.6 1.6 %copy.134 = bf16[48,2048]{1,0:T(8,128)(2,1)} copy(bf16[48,2048]{1,0:T(8,128)(2,1)} %shard_map.199) | data formatting | bytes 393216
  (123 shorter events, 18.3 us)
Async XLA Ops:
  0.0 112.3 %copy-start = (bf16[512,2048]{1,0:T(8,128)(2,1)S(1)}, bf16[512,2048]{1,0:T(8,128)(2,1)}, u32[]{:S(2)}) copy-start(bf16[512,2048]{1,0:T(8,128)(2,1)} %param.34) | copy-start | bytes 6291460
  0.0 2.4 %copy-start.1 = (bf16[384,2048]{1,0:T(8,128)(2,1)S(1)}, bf16[384,2048]{1,0:T(8,128)(2,1)}, u32[]{:S(2)}) copy-start(bf16[384,2048]{1,0:T(8,128)(2,1)} %param.21) | copy-start | bytes 4718596
  0.0 3.0 %copy-start.20 = (bf16[2048,512]{1,0:T(8,128)(2,1)S(1)}, bf16[2048,512]{1,0:T(8,128)(2,1)}, u32[]{:S(2)}) copy-start(bf16[2048,512]{1,0:T(8,128)(2,1)} %param.24) | copy-start | bytes 6291460
  3.0 1.9 %copy-start.6 = (bf16[2048,256]{1,0:T(8,128)(2,1)S(1)}, bf16[2048,256]{1,0:T(8,128)(2,1)}, u32[]{:S(2)}) copy-start(bf16[2048,256]{1,0:T(8,128)(2,1)} %param.22) | copy-start | bytes 3145732
  4.9 3.8 %copy-start.16 = (bf16[4,256]{1,0:T(4,128)(2,1)S(1)}, bf16[4,256]{1,0:T(4,128)(2,1)}, u32[]{:S(2)}) copy-start(bf16[4,256]{1,0:T(4,128)(2,1)} %param.29) | copy-start | bytes 6148
  4.9 3.8 %copy-start.17 = (bf16[4,256]{1,0:T(4,128)(2,1)S(1)}, bf16[4,256]{1,0:T(4,128)(2,1)}, u32[]{:S(2)}) copy-start(bf16[4,256]{1,0:T(4,128)(2,1)} %param.28) | copy-start | bytes 6148
  4.9 3.9 %copy-start.21 = (f32[4]{0:T(128)S(1)}, f32[4]{0:T(128)}, u32[]{:S(2)}) copy-start(f32[4]{0:T(128)} %param.31) | copy-start | bytes 52
  4.9 3.9 %copy-start.13 = (bf16[2048,4]{0,1:T(4,128)(2,1)S(1)}, bf16[2048,4]{0,1:T(4,128)(2,1)}, u32[]{:S(2)}) copy-start(bf16[2048,4]{0,1:T(4,128)(2,1)} %param.26) | copy-start | bytes 49156
  4.9 3.9 %copy-start.18 = (f32[4]{0:T(128)S(1)}, f32[4]{0:T(128)}, u32[]{:S(2)}) copy-start(f32[4]{0:T(128)} %param.32) | copy-start | bytes 52
  5.5 3.9 %copy-start.14 = (bf16[2048,4]{0,1:T(4,128)(2,1)S(1)}, bf16[2048,4]{0,1:T(4,128)(2,1)}, u32[]{:S(2)}) copy-start(bf16[2048,4]{0,1:T(4,128)(2,1)} %param.27) | copy-start | bytes 49156
  5.6 8.5 %collective-permute-start = (bf16[3,1024]{1,0:T(4,128)(2,1)S(1)}, bf16[3,1024]{1,0:T(4,128)(2,1)S(1)}, u32[]{:S(2)}, u32[]{:S(2)}) collective-permute-start(bf16[3,1024]{1,0:T(4,128)(2,1)S(1)} %pad_maximum_fusion.3), channel_id=1, source_target_pairs={{0,8},{8,16},{16,24},{24,32},{32,40},{40,48},{48,56},{56,64},{64,7... | collective-permute-start | bytes 18440 | tf_op jit(solution)/shard_map/ppermute | solution.py:27
  8.8 2.7 %copy-start.15 = (bf16[4,512]{1,0:T(4,128)(2,1)S(1)}, bf16[4,512]{1,0:T(4,128)(2,1)}, u32[]{:S(2)}) copy-start(bf16[4,512]{1,0:T(4,128)(2,1)} %param.30) | copy-start | bytes 12292
  8.8 5.0 %copy-start.19 = (f32[128]{0:T(128)S(1)}, f32[128]{0:T(128)}, u32[]{:S(2)}) copy-start(f32[128]{0:T(128)} %param.33) | copy-start | bytes 1540
  18.8 2.4 %copy-start.3 = (f32[384,2,2,128]{3,0,2,1:T(8,128)}, f32[384,2,2,128]{3,0,2,1:T(8,128)S(1)}, u32[]{:S(2)}) copy-start(f32[384,2,2,128]{3,0,2,1:T(8,128)S(1)} %broadcast_in_dim.101) | copy-start | bytes 2359300
  18.8 2.4 %copy-start.22 = (f32[64,64]{1,0:T(8,128)S(1)}, f32[64,64]{1,0:T(8,128)}, u32[]{:S(2)}) copy-start(f32[64,64]{1,0:T(8,128)} %constant.53.clone) | copy-start | bytes 49156
  18.8 2.4 %copy-start.23 = (f32[64,64]{1,0:T(8,128)S(1)}, f32[64,64]{1,0:T(8,128)}, u32[]{:S(2)}) copy-start(f32[64,64]{1,0:T(8,128)} %constant.54.clone) | copy-start | bytes 49156
  21.2 1.5 copy-start.12
  23.6 1.0 copy-start.11
  25.5 0.9 copy-start.10
  27.4 1.0 copy-start.9
  29.5 1.0 copy-start.8
  31.4 1.8 %copy-start.7 = (f32[384,512]{1,0:T(8,128)S(1)}, f32[384,512]{1,0:T(8,128)}, u32[]{:S(2)}) copy-start(f32[384,512]{1,0:T(8,128)} %get-tuple-element.29) | copy-start | bytes 2359300
  36.9 2.4 %copy-start.4 = (f32[384,2,2,128]{3,0,2,1:T(8,128)S(1)}, f32[384,2,2,128]{3,0,2,1:T(8,128)}, u32[]{:S(2)}) copy-start(f32[384,2,2,128]{3,0,2,1:T(8,128)} %copy-done.3) | copy-start | bytes 2359300
  39.3 1.1 copy-start.5
  39.8 1.6 %copy-start.2 = (f32[6,4,64,64]{3,2,1,0:T(8,128)S(1)}, f32[6,4,64,64]{3,2,1,0:T(8,128)}, u32[]{:S(2)}) copy-start(f32[6,4,64,64]{3,2,1,0:T(8,128)} %convolution_multiply_fusion.1) | copy-start | bytes 1179652
  55.4 10.9 %collective-permute-start.4 = (f32[4,128,128]{2,1,0:T(8,128)S(1)}, f32[4,128,128]{2,1,0:T(8,128)S(1)}, u32[]{:S(2)}, u32[]{:S(2)}) collective-permute-start(f32[4,128,128]{2,1,0:T(8,128)S(1)} %convolution_add_fusion.4), channel_id=1, source_target_pairs={{0,8},{8,16},{16,24},{24,32},{32,40},{40,48},{48,56},{56,64},{64,7... | collective-permute-start | bytes 786440 | tf_op jit(solution)/shard_map/ppermute | solution.py:27
  58.9 13.0 %collective-permute-start.1 = (f32[4,128,128]{2,1,0:T(8,128)S(1)}, f32[4,128,128]{2,1,0:T(8,128)S(1)}, u32[]{:S(2)}, u32[]{:S(2)}) collective-permute-start(f32[4,128,128]{2,1,0:T(8,128)S(1)} %fusion.91), channel_id=1, source_target_pairs={{0,8},{8,16},{16,24},{24,32},{32,40},{40,48},{48,56},{56,64},{64,7... | collective-permute-start | bytes 786440 | tf_op jit(solution)/shard_map/ppermute | solution.py:27
  66.6 9.5 %collective-permute-start.5 = (f32[4,128,128]{2,1,0:T(8,128)S(1)}, f32[4,128,128]{2,1,0:T(8,128)S(1)}, u32[]{:S(2)}, u32[]{:S(2)}) collective-permute-start(f32[4,128,128]{2,1,0:T(8,128)S(1)} %fusion.7), channel_id=1, source_target_pairs={{0,16},{8,24},{16,32},{24,40},{32,48},{40,56},{48,64},{56,72},{64,... | collective-permute-start | bytes 786440 | tf_op jit(solution)/shard_map/ppermute | solution.py:27
  72.3 12.2 %collective-permute-start.2 = (f32[4,128,128]{2,1,0:T(8,128)S(1)}, f32[4,128,128]{2,1,0:T(8,128)S(1)}, u32[]{:S(2)}, u32[]{:S(2)}) collective-permute-start(f32[4,128,128]{2,1,0:T(8,128)S(1)} %convolution_select_fusion.2), channel_id=1, source_target_pairs={{0,16},{8,24},{16,32},{24,40},{32,48},{40,56},{48,64},{56,72},{64,... | collective-permute-start | bytes 786440 | tf_op jit(solution)/shard_map/ppermute | solution.py:27
  76.6 13.7 %collective-permute-start.6 = (f32[4,128,128]{2,1,0:T(8,128)S(1)}, f32[4,128,128]{2,1,0:T(8,128)S(1)}, u32[]{:S(2)}, u32[]{:S(2)}) collective-permute-start(f32[4,128,128]{2,1,0:T(8,128)S(1)} %fusion.6), channel_id=1, source_target_pairs={{0,32},{8,40},{16,48},{24,56},{32,64},{40,72},{48,80},{56,88},{64,... | collective-permute-start | bytes 786440 | tf_op jit(solution)/shard_map/ppermute | solution.py:27
  84.8 11.0 %collective-permute-start.3 = (f32[4,128,128]{2,1,0:T(8,128)S(1)}, f32[4,128,128]{2,1,0:T(8,128)S(1)}, u32[]{:S(2)}, u32[]{:S(2)}) collective-permute-start(f32[4,128,128]{2,1,0:T(8,128)S(1)} %convolution_select_fusion.1), channel_id=1, source_target_pairs={{0,32},{8,40},{16,48},{24,56},{32,64},{40,72},{48,80},{56,88},{64,... | collective-permute-start | bytes 786440 | tf_op jit(solution)/shard_map/ppermute | solution.py:27
  90.7 8.9 %collective-permute-start.7 = (f32[4,128,128]{2,1,0:T(8,128)S(1)}, f32[4,128,128]{2,1,0:T(8,128)S(1)}, u32[]{:S(2)}, u32[]{:S(2)}) collective-permute-start(f32[4,128,128]{2,1,0:T(8,128)S(1)} %fusion.5), channel_id=1, source_target_pairs={{0,64},{8,72},{16,80},{24,88},{32,96},{40,104},{48,112},{56,120},{... | collective-permute-start | bytes 786440 | tf_op jit(solution)/shard_map/ppermute | solution.py:27
  100.0 9.2 %collective-permute-start.8 = (f32[4,128,128]{2,1,0:T(8,128)S(1)}, f32[4,128,128]{2,1,0:T(8,128)S(1)}, u32[]{:S(2)}, u32[]{:S(2)}) collective-permute-start(f32[4,128,128]{2,1,0:T(8,128)S(1)} %fusion.4), channel_id=1, source_target_pairs={{0,8},{8,16},{16,24},{24,32},{32,40},{40,48},{48,56},{56,64},{64,7... | collective-permute-start | bytes 786440 | tf_op jit(solution)/shard_map/ppermute | solution.py:27

commit v3 on v2

--- a/solution.py
+++ b/solution.py
@@ -164,6 +164,99 @@
     return jnp.einsum("hde,hef->hdf", trans_mat, state_now, precision=highest) + written
 
 
+def shard_scan_kernel(shard_count, a_ref, b_ref, out_ref, cur_a, cur_b, got_a, got_b, send_sems, recv_sems):
+    me = lax.axis_index("seq")
+    hg_me = lax.axis_index("hg")
+    head_count = a_ref.shape[0]
+    distances = []
+    distance = 1
+    while distance < shard_count:
+        distances.append(distance)
+        distance *= 2
+    barrier = pltpu.get_barrier_semaphore()
+    for distance in distances:
+        for target in (lax.rem(me + distance, shard_count), lax.rem(me + shard_count - distance, shard_count)):
+            pl.semaphore_signal(barrier, inc=1, device_id=(target, hg_me), device_id_type=MESH)
+    pl.semaphore_wait(barrier, 2 * len(distances))
+    cur_a[0] = a_ref[...]
+    cur_b[0] = b_ref[...]
+    sem_index = 0
+    for round_index, distance in enumerate(distances):
+        target = lax.rem(me + distance, shard_count)
+        sends_a = round_index + 1 < len(distances)
+        copies = [
+            pltpu.make_async_remote_copy(
+                src_ref=cur_b.at[round_index],
+                dst_ref=got_b.at[round_index],
+                send_sem=send_sems.at[sem_index],
+                recv_sem=recv_sems.at[sem_index],
+                device_id=(target, hg_me),
+                device_id_type=MESH,
+            )
+        ]
+        if sends_a:
+            copies.append(
+                pltpu.make_async_remote_copy(
+                    src_ref=cur_a.at[round_index],
+                    dst_ref=got_a.at[round_index],
+                    send_sem=send_sems.at[sem_index + 1],
+                    recv_sem=recv_sems.at[sem_index + 1],
+                    device_id=(target, hg_me),
+                    device_id_type=MESH,
+                )
+            )
+        sem_index += len(copies)
+        for copy in copies:
+            copy.start()
+        for copy in copies:
+            copy.wait()
+        has_prev = me >= distance
+        for head in range(head_count):
+            own_a = cur_a[round_index, head]
+            own_b = cur_b[round_index, head]
+            joined_b = (
+                jnp.dot(own_a, got_b[round_index, head], precision=highest,
+                        preferred_element_type=jnp.float32)
+                + own_b
+            )
+            cur_b[round_index + 1, head] = jnp.where(has_prev, joined_b, own_b)
+            if sends_a:
+                joined_a = jnp.dot(own_a, got_a[round_index, head], precision=highest,
+                                   preferred_element_type=jnp.float32)
+                cur_a[round_index + 1, head] = jnp.where(has_prev, joined_a, own_a)
+    last = len(distances)
+    shift = pltpu.make_async_remote_copy(
+        src_ref=cur_b.at[last],
+        dst_ref=got_b.at[last],
+        send_sem=send_sems.at[sem_index],
+        recv_sem=recv_sems.at[sem_index],
+        device_id=(lax.rem(me + 1, shard_count), hg_me),
+        device_id_type=MESH,
+    )
+    shift.start()
+    shift.wait()
+    out_ref[...] = jnp.where(me >= 1, got_b[last], 0.0)
+
+
+def shard_scan(shard_a, shard_b, shard_count):
+    rounds = max(1, (shard_count - 1).bit_length())
+    return pl.pallas_call(
+        functools.partial(shard_scan_kernel, shard_count),
+        out_shape=jax.ShapeDtypeStruct(shard_b.shape, jnp.float32),
+        in_specs=[pl.BlockSpec(memory_space=pltpu.VMEM)] * 2,
+        out_specs=pl.BlockSpec(memory_space=pltpu.VMEM),
+        scratch_shapes=[
+            pltpu.VMEM((rounds + 1,) + shard_a.shape, jnp.float32),
+            pltpu.VMEM((rounds + 1,) + shard_b.shape, jnp.float32),
+            pltpu.VMEM((rounds + 1,) + shard_a.shape, jnp.float32),
+            pltpu.VMEM((rounds + 1,) + shard_b.shape, jnp.float32),
+            pltpu.SemaphoreType.DMA((2 * rounds + 1,)),
+            pltpu.SemaphoreType.DMA((2 * rounds + 1,)),
+        ],
+        compiler_params=pltpu.CompilerParams(collective_id=1, has_side_effects=True),
+    )(shard_a, shard_b)
+
+
 def group_sum_kernel(group_count, part_ref, out_ref, landed, send_sems, recv_sems, own_sem):
     me = lax.axis_index("hg")
     seq_me = lax.axis_index("seq")
@@ -292,24 +385,7 @@
         compose, (identity, empty_state), terms, unroll=True
     )
 
-    shard_count = lax.axis_size("seq")
-    shard_index = lax.axis_index("seq")
-    acc_a, acc_b = shard_a, shard_b
-    distance = 1
-    while distance < shard_count:
-        has_prev = shard_index >= distance
-        prev_b = passed_along(acc_b, "seq", distance)
-        new_b = jnp.where(has_prev, apply_shard(acc_a, prev_b, acc_b), acc_b)
-        if 2 * distance < shard_count:
-            prev_a = passed_along(acc_a, "seq", distance)
-            acc_a = jnp.where(
-                has_prev,
-                jnp.einsum("hde,hef->hdf", acc_a, prev_a, precision=highest),
-                acc_a,
-            )
-        acc_b = new_b
-        distance *= 2
-    state_in = passed_along(acc_b, "seq", 1)
+    state_in = shard_scan(shard_a, shard_b, lax.axis_size("seq"))
     produced = local_mix + jnp.einsum("jhsd,hde->jhse", entry_map, state_in, precision=highest)
     produced = produced.transpose(0, 2, 1, 3).reshape(tok_rows, head_count, DV)
     gated = gated_output(produced, zgate, norm_gain)

time: 152 us -> 164 us (1.079)
  the two profiles are of different devices: /device:TPU:17 before, /device:TPU:1 now
where the time goes in v3:
time: 164 us; the launch traced here: 162 us
  Pallas kernels  85.4 us (52%)
  matrix products  54.3 us (33%)
  local copies, waits for them, and re-layouts  9.36 us (6%)
  other arithmetic  7.41 us (5%)
  starting transfers between devices  3.94 us (2%)
    pallas_call x1, Pallas kernels, shard_scan(): pl.pallas_call(functools.partial(shard_scan_kernel, shard_count), out_sha...  55 us
    pallas_call x1, Pallas kernels, group_sum(): pl.pallas_call(functools.partial(group_sum_kernel, group_count), out_shap...  30.4 us
    dot_general x6, matrix products, compose(): jnp.einsum('hsd,hde->hse', step_carry, prefix_a, precision=highest)  6.08 us
    dot_general x5, matrix products, unit_lower_inverse(): jnp.einsum('...st,...tu->...su', step, inverse, precision=highest)  5.62 us
    dot_general x1, matrix products, on_device(): jnp.dot(gated, w_out, preferred_element_type=jnp.float32)  5.38 us
    dot_general x5, matrix products, unit_lower_inverse(): jnp.einsum('...st,...tu->...su', inverse, off_blocks, precision=highest)  4.77 us
    ppermute x1, starting transfers between devices, passed_along(): return lax.ppermute(block, axis, route)  3.94 us
  transfers between devices with their start and end apart: 1, of which 0 were waited for; matrix products, arithmetic and copies ran while one was open for 3% of the time, Pallas kernels for 0%

profile of v3, /device:TPU:1, one launch (start us, length us, event | category | flops | bytes accessed | tf_op | source)
XLA Modules:
  0.0 161.5 jit_solution(5511474740291564905)
XLA Ops:
  0.0 2.4 %fusion.98 = (f32[384,256]{1,0:T(8,128)S(1)}, bf16[384,256]{1,0:T(8,128)(2,1)S(1)}) fusion(bf16[384,2048]{1,0:T(8,128)(2,1)} %param.21, bf16[2048,256]{1,0:T(8,128)(2,1)} %param.23), kind=kOutput, calls=%fused_computation.210 | convolution fusion | flops 402849792 | bytes 3211264 | tf_op jit(solution)/shard_map/dot_general | solution.py:32
  2.4 0.6 copy-done.21
  3.0 1.9 %fusion.100 = (f32[384,512]{1,0:T(8,128)}, bf16[384,512]{1,0:T(8,128)(2,1)S(1)}) fusion(bf16[384,2048]{1,0:T(8,128)(2,1)S(1)} %copy-done.1, bf16[2048,512]{1,0:T(8,128)(2,1)S(1)} %copy-done.21), kind=kOutput, calls=%fused_computation.212 | convolution fusion | flops 805699584 | bytes 4849664 | tf_op jit(solution)/shard_map/dot_general | solution.py:33
  5.0 0.6 fusion.99
  5.6 3.9 %collective-permute-start = (bf16[3,1024]{1,0:T(4,128)(2,1)S(1)}, bf16[3,1024]{1,0:T(4,128)(2,1)S(1)}, u32[]{:S(2)}, u32[]{:S(2)}) collective-permute-start(bf16[3,1024]{1,0:T(4,128)(2,1)S(1)} %pad_maximum_fusion.3), channel_id=1, source_target_pairs={{0,8},{8,16},{16,24},{24,32},{32,40},{40,48},{48,56},{56,64},{64,7... | collective-permute-start | bytes 18440 | tf_op jit(solution)/shard_map/ppermute | solution.py:27
  9.7 0.5 fusion.94
  10.3 1.9 %fusion.24 = f32[384,4]{0,1:T(4,128)S(1)} fusion(bf16[384,2048]{1,0:T(8,128)(2,1)} %param.21, bf16[2048,4]{0,1:T(4,128)(2,1)S(1)} %copy-done.15), kind=kOutput, calls=%fused_computation.61 | convolution fusion | flops 6296064 | bytes 1595392 | tf_op jit(solution)/shard_map/dot_general | solution.py:86
  12.4 1.9 %reduce_window_sum.11 = f32[6,4,64]{2,1,0:T(4,128)S(1)} reduce-window(f32[6,4,64]{2,1,0:T(4,128)S(1)} %copy.69, f32[]{:T(128)} %constant.16.clone.1), window={size=1x1x64 pad=0_0x0_0x63_0}, to_apply=%region_0.1 | reduce-window | flops 96768 | bytes 12292 | tf_op jit(solution)/shard_map/jit(cumsum)/reduce_window_sum | solution.py:115
  14.9 1.2 divide_multiply_fusion.1
  16.1 1.2 reshape.82
  17.3 0.5 multiply_reduce_fusion.1
  18.6 0.5 multiply_reduce_fusion.2
  19.7 2.3 %convolution_multiply_fusion.1 = f32[6,4,64,64]{3,2,1,0:T(8,128)} fusion(f32[6,4,64,128]{3,2,0,1:T(8,128)S(1)} %bitcast.282, f32[6,64,4,128]{3,1,0,2:T(8,128)S(1)} %bitcast.280, f32[6,4,64]{2,1,0:T(4,128)S(1)} %reduce_window_sum.11, pred[64,64]{1,0:T(8,128)(4,1)S(1)} %get-tuple-element.36), kind=kOutput, calls=%fused_computation.13 | convolution fusion | flops 151388160 | bytes 1976320 | tf_op jit(solution)/shard_map/...sd,...td->...st/dot_general | solution.py:134
  22.0 1.4 multiply_subtract_fusion.1
  23.5 0.9 fusion.49
  24.4 1.0 convolution_subtract_fusion.4
  25.4 0.9 fusion.47
  26.4 0.9 convolution_subtract_fusion.3
  27.3 0.9 fusion.45
  28.2 1.0 convolution_subtract_fusion.2
  29.2 1.1 fusion.43
  30.3 1.0 convolution_subtract_fusion.1
  31.3 0.9 fusion.41
  32.2 1.8 %convolution_subtract_fusion = f32[6,4,64,64]{3,2,1,0:T(8,128)} fusion(f32[6,4,64,64]{3,2,1,0:T(8,128)S(1)} %convolution_subtract_fusion.1, f32[6,4,64,64]{3,2,1,0:T(8,128)S(1)} %fusion.41), kind=kOutput, calls=%fused_computation.2 | convolution fusion | flops 75595776 | bytes 1179648 | tf_op jit(solution)/shard_map/...st,...tu->...su/dot_general | solution.py:108
  34.1 1.4 divide_multiply_fusion
  35.4 2.3 %reshape_reshape.11 = f32[6,64,4,128]{3,2,1,0:T(4,128)} reshape(f32[384,512]{1,0:T(8,128)} %divide_multiply_fusion) | data formatting | bytes 1572864 | tf_op jit(solution)/shard_map/reshape;reshape | solution.py:92
  37.7 2.4 %fusion.36 = f32[6,4,64,128]{3,2,1,0:T(8,128)S(1)} fusion(f32[6,4,64,64]{3,2,1,0:T(8,128)} %convolution_subtract_fusion, f32[6,64,4,128]{3,2,1,0:T(4,128)} %reshape_reshape.11, f32[6,4,64]{2,1,0:T(4,128)S(1)} %bitcast.290), kind=kOutput, calls=%fused_computation.76 | convolution fusion | flops 151191552 | bytes 1972224 | tf_op jit(solution)/shard_map/...st,...td->...sd/dot_general | solution.py:131
  40.2 0.5 broadcast_multiply_fusion
  40.6 0.6 copy-done.5
  41.3 0.9 fusion.39
  42.2 0.9 fusion.101
  43.2 2.6 %fusion.51 = f32[6,4,128,128]{3,2,1,0:T(8,128)S(1)} fusion(f32[6,4,64,128]{3,2,1,0:T(8,128)S(1)} %fusion.36, f32[6,4,64,128]{3,2,0,1:T(8,128)S(1)} %get-tuple-element.5), kind=kOutput, calls=%fused_computation.96 | convolution fusion | flops 301989888 | bytes 3145728 | tf_op jit(solution)/shard_map/...sd,...se->...de/dot_general | solution.py:140
  45.8 1.0 convolution_subtract_fusion.5
  47.0 1.0 fusion.9
  48.0 3.0 %multiply_subtract_fusion = f32[6,4,128,128]{3,2,1,0:T(8,128)S(1)} fusion(f32[6,4,64,128]{3,2,1,0:T(8,128)S(1)} %fusion.39, f32[128,128]{1,0:T(8,128)S(1)} %fusion.92, f32[6,4]{1,0:T(8,128)S(1)} %copy.81, f32[6,4,64,128]{3,2,0,1:T(8,128)S(1)} %get-tuple-element.5), kind=kOutput, calls=%fused_computation.1 | convolution fusion | flops 302776320 | bytes 3211360 | tf_op jit(solution)/shard_map/...sd,...se->...de/dot_general | solution.py:137
  54.8 1.1 convolution_add_fusion.b_ref
  56.7 1.0 fusion.8
  58.1 1.0 fusion.7
  59.6 1.0 fusion.6
  61.0 1.0 fusion.5
  62.0 1.1 fusion.87.a_ref
  63.1 1.0 fusion.4
  64.2 55.0 %shard_map.199 = f32[4,128,128]{2,1,0:T(8,128)} custom-call(f32[4,128,128]{2,1,0:T(8,128)} %fusion.87.a_ref, f32[4,128,128]{2,1,0:T(8,128)} %convolution_add_fusion.b_ref), custom_call_target="tpu_custom_call" | custom-call | tf_op jit(solution)/shard_map/pallas_call | solution.py:243
  119.1 2.4 %multiply_reduce_fusion = (f32[6,64,4]{1,2,0:T(4,128)S(1)}, f32[6,64,4,128]{3,1,2,0:T(8,128)S(1)}) fusion(f32[6,4,64,128]{3,2,1,0:T(8,128)} %copy-done.6, f32[6,4,64,128]{3,2,1,0:T(8,128)} %fusion.4, f32[4,128,128]{2,1,0:T(8,128)} %shard_map.199), kind=kOutput, calls=%fused_computation.82 | convolution fusion | flops 302578176 | bytes 2627584 | tf_op jit(solution)/shard_map/jhsd,hde->jhse/dot_general | solution.py:389
  122.0 1.4 copy.86
  123.9 5.4 %convolution_convert_fusion.part_ref = bf16[384,2048]{1,0:T(8,128)(2,1)} fusion(bf16[512,2048]{1,0:T(8,128)(2,1)S(1)} %copy-done, f32[48,8,4,128]{3,2,1,0:T(4,128)S(1)} %bitcast.286, f32[48,8,4,128]{3,2,1,0:T(4,128)} %bitcast.285, bf16[384,2048]{1,0:T(8,128)(2,1)} %param.21, bf16[2048,512]{1,0:T(8,128)(2,1)} %param.25, f32[512]{0:T(512)S(1)} %broadcast_bitcast_fusion), kind=kOutput, calls=%fused_computation | convolution fusion | flops 1613365248 | bytes 8914944 | tf_op jit(solution)/shard_map/dot_general | solution.py:392
  129.2 30.4 %shard_map.200 = bf16[48,2048]{1,0:T(8,128)(2,1)} custom-call(bf16[384,2048]{1,0:T(8,128)(2,1)} %convolution_convert_fusion.part_ref), custom_call_target="tpu_custom_call" | custom-call | tf_op jit(solution)/shard_map/pallas_call | solution.py:308
  159.7 1.6 %copy.134 = bf16[48,2048]{1,0:T(8,128)(2,1)} copy(bf16[48,2048]{1,0:T(8,128)(2,1)} %shard_map.200) | data formatting | bytes 393216
  (103 shorter events, 9.1 us)
Async XLA Ops:
  0.0 123.8 %copy-start = (bf16[512,2048]{1,0:T(8,128)(2,1)S(1)}, bf16[512,2048]{1,0:T(8,128)(2,1)}, u32[]{:S(2)}) copy-start(bf16[512,2048]{1,0:T(8,128)(2,1)} %param.34) | copy-start | bytes 6291460
  0.0 2.4 %copy-start.1 = (bf16[384,2048]{1,0:T(8,128)(2,1)S(1)}, bf16[384,2048]{1,0:T(8,128)(2,1)}, u32[]{:S(2)}) copy-start(bf16[384,2048]{1,0:T(8,128)(2,1)} %param.21) | copy-start | bytes 4718596
  0.0 3.0 %copy-start.21 = (bf16[2048,512]{1,0:T(8,128)(2,1)S(1)}, bf16[2048,512]{1,0:T(8,128)(2,1)}, u32[]{:S(2)}) copy-start(bf16[2048,512]{1,0:T(8,128)(2,1)} %param.24) | copy-start | bytes 6291460
  3.0 1.9 %copy-start.7 = (bf16[2048,256]{1,0:T(8,128)(2,1)S(1)}, bf16[2048,256]{1,0:T(8,128)(2,1)}, u32[]{:S(2)}) copy-start(bf16[2048,256]{1,0:T(8,128)(2,1)} %param.22) | copy-start | bytes 3145732
  4.9 4.7 %copy-start.17 = (bf16[4,256]{1,0:T(4,128)(2,1)S(1)}, bf16[4,256]{1,0:T(4,128)(2,1)}, u32[]{:S(2)}) copy-start(bf16[4,256]{1,0:T(4,128)(2,1)} %param.29) | copy-start | bytes 6148
  4.9 4.7 %copy-start.18 = (bf16[4,256]{1,0:T(4,128)(2,1)S(1)}, bf16[4,256]{1,0:T(4,128)(2,1)}, u32[]{:S(2)}) copy-start(bf16[4,256]{1,0:T(4,128)(2,1)} %param.28) | copy-start | bytes 6148
  4.9 4.7 %copy-start.22 = (f32[4]{0:T(128)S(1)}, f32[4]{0:T(128)}, u32[]{:S(2)}) copy-start(f32[4]{0:T(128)} %param.31) | copy-start | bytes 52
  5.0 4.7 %copy-start.14 = (bf16[2048,4]{0,1:T(4,128)(2,1)S(1)}, bf16[2048,4]{0,1:T(4,128)(2,1)}, u32[]{:S(2)}) copy-start(bf16[2048,4]{0,1:T(4,128)(2,1)} %param.26) | copy-start | bytes 49156
  5.0 4.7 %copy-start.19 = (f32[4]{0:T(128)S(1)}, f32[4]{0:T(128)}, u32[]{:S(2)}) copy-start(f32[4]{0:T(128)} %param.32) | copy-start | bytes 52
  5.6 4.8 %copy-start.15 = (bf16[2048,4]{0,1:T(4,128)(2,1)S(1)}, bf16[2048,4]{0,1:T(4,128)(2,1)}, u32[]{:S(2)}) copy-start(bf16[2048,4]{0,1:T(4,128)(2,1)} %param.27) | copy-start | bytes 49156
  5.6 9.3 %collective-permute-start = (bf16[3,1024]{1,0:T(4,128)(2,1)S(1)}, bf16[3,1024]{1,0:T(4,128)(2,1)S(1)}, u32[]{:S(2)}, u32[]{:S(2)}) collective-permute-start(bf16[3,1024]{1,0:T(4,128)(2,1)S(1)} %pad_maximum_fusion.3), channel_id=1, source_target_pairs={{0,8},{8,16},{16,24},{24,32},{32,40},{40,48},{48,56},{56,64},{64,7... | collective-permute-start | bytes 18440 | tf_op jit(solution)/shard_map/ppermute | solution.py:27
  9.7 2.7 %copy-start.16 = (bf16[4,512]{1,0:T(4,128)(2,1)S(1)}, bf16[4,512]{1,0:T(4,128)(2,1)}, u32[]{:S(2)}) copy-start(bf16[4,512]{1,0:T(4,128)(2,1)} %param.30) | copy-start | bytes 12292
  9.7 5.0 %copy-start.20 = (f32[128]{0:T(128)S(1)}, f32[128]{0:T(128)}, u32[]{:S(2)}) copy-start(f32[128]{0:T(128)} %param.33) | copy-start | bytes 1540
  19.6 2.4 %copy-start.3 = (f32[384,2,2,128]{3,0,2,1:T(8,128)}, f32[384,2,2,128]{3,0,2,1:T(8,128)S(1)}, u32[]{:S(2)}) copy-start(f32[384,2,2,128]{3,0,2,1:T(8,128)S(1)} %broadcast_in_dim.101) | copy-start | bytes 2359300
  19.7 2.4 %copy-start.23 = (f32[64,64]{1,0:T(8,128)S(1)}, f32[64,64]{1,0:T(8,128)}, u32[]{:S(2)}) copy-start(f32[64,64]{1,0:T(8,128)} %constant.39.clone) | copy-start | bytes 49156
  19.7 2.4 %copy-start.24 = (f32[64,64]{1,0:T(8,128)S(1)}, f32[64,64]{1,0:T(8,128)}, u32[]{:S(2)}) copy-start(f32[64,64]{1,0:T(8,128)} %constant.40.clone) | copy-start | bytes 49156
  22.0 1.5 copy-start.13
  24.4 1.0 copy-start.12
  26.3 0.9 copy-start.11
  28.2 1.0 copy-start.10
  30.3 1.0 copy-start.9
  32.2 1.8 %copy-start.8 = (f32[384,512]{1,0:T(8,128)S(1)}, f32[384,512]{1,0:T(8,128)}, u32[]{:S(2)}) copy-start(f32[384,512]{1,0:T(8,128)} %get-tuple-element.29) | copy-start | bytes 2359300
  37.7 2.4 %copy-start.4 = (f32[384,2,2,128]{3,0,2,1:T(8,128)S(1)}, f32[384,2,2,128]{3,0,2,1:T(8,128)}, u32[]{:S(2)}) copy-start(f32[384,2,2,128]{3,0,2,1:T(8,128)} %copy-done.3) | copy-start | bytes 2359300
  40.1 1.1 copy-start.5
  40.6 1.6 copy-start.2
  56.3 3.3 %copy-start.6 = (f32[6,4,64,128]{3,2,1,0:T(8,128)}, f32[6,4,64,128]{3,2,1,0:T(8,128)S(1)}, u32[]{:S(2)}) copy-start(f32[6,4,64,128]{3,2,1,0:T(8,128)S(1)} %fusion.11) | copy-start | bytes 2359300

commit v4 on v3

--- a/solution.py
+++ b/solution.py
@@ -164,7 +164,9 @@
     return jnp.einsum("hde,hef->hdf", trans_mat, state_now, precision=highest) + written
 
 
-def shard_scan_kernel(shard_count, a_ref, b_ref, out_ref, cur_a, cur_b, got_a, got_b, send_sems, recv_sems):
+def shard_scan_kernel(
+    shard_count, a_ref, b_ref, out_ref, cur_a, cur_b, out_a, out_b, got_a, got_b, send_sems, recv_sems
+):
     me = lax.axis_index("seq")
     hg_me = lax.axis_index("hg")
     head_count = a_ref.shape[0]
@@ -180,13 +182,15 @@
     pl.semaphore_wait(barrier, 2 * len(distances))
     cur_a[0] = a_ref[...]
     cur_b[0] = b_ref[...]
+    out_a[0] = a_ref[...].astype(out_a.dtype)
+    out_b[0] = b_ref[...].astype(out_b.dtype)
     sem_index = 0
     for round_index, distance in enumerate(distances):
         target = lax.rem(me + distance, shard_count)
         sends_a = round_index + 1 < len(distances)
         copies = [
             pltpu.make_async_remote_copy(
-                src_ref=cur_b.at[round_index],
+                src_ref=out_b.at[round_index],
                 dst_ref=got_b.at[round_index],
                 send_sem=send_sems.at[sem_index],
                 recv_sem=recv_sems.at[sem_index],
@@ -197,7 +201,7 @@
         if sends_a:
             copies.append(
                 pltpu.make_async_remote_copy(
-                    src_ref=cur_a.at[round_index],
+                    src_ref=out_a.at[round_index],
                     dst_ref=got_a.at[round_index],
                     send_sem=send_sems.at[sem_index + 1],
                     recv_sem=recv_sems.at[sem_index + 1],
@@ -215,18 +219,22 @@
             own_a = cur_a[round_index, head]
             own_b = cur_b[round_index, head]
             joined_b = (
-                jnp.dot(own_a, got_b[round_index, head], precision=highest,
+                jnp.dot(own_a, got_b[round_index, head].astype(jnp.float32), precision=highest,
                         preferred_element_type=jnp.float32)
                 + own_b
             )
-            cur_b[round_index + 1, head] = jnp.where(has_prev, joined_b, own_b)
+            next_b = jnp.where(has_prev, joined_b, own_b)
+            cur_b[round_index + 1, head] = next_b
+            out_b[round_index + 1, head] = next_b.astype(out_b.dtype)
             if sends_a:
-                joined_a = jnp.dot(own_a, got_a[round_index, head], precision=highest,
-                                   preferred_element_type=jnp.float32)
-                cur_a[round_index + 1, head] = jnp.where(has_prev, joined_a, own_a)
+                joined_a = jnp.dot(own_a, got_a[round_index, head].astype(jnp.float32),
+                                   precision=highest, preferred_element_type=jnp.float32)
+                next_a = jnp.where(has_prev, joined_a, own_a)
+                cur_a[round_index + 1, head] = next_a
+                out_a[round_index + 1, head] = next_a.astype(out_a.dtype)
     last = len(distances)
     shift = pltpu.make_async_remote_copy(
-        src_ref=cur_b.at[last],
+        src_ref=out_b.at[last],
         dst_ref=got_b.at[last],
         send_sem=send_sems.at[sem_index],
         recv_sem=recv_sems.at[sem_index],
@@ -235,7 +243,7 @@
     )
     shift.start()
     shift.wait()
-    out_ref[...] = jnp.where(me >= 1, got_b[last], 0.0)
+    out_ref[...] = jnp.where(me >= 1, got_b[last].astype(jnp.float32), 0.0)
 
 
 def shard_scan(shard_a, shard_b, shard_count):
@@ -248,8 +256,10 @@
         scratch_shapes=[
             pltpu.VMEM((rounds + 1,) + shard_a.shape, jnp.float32),
             pltpu.VMEM((rounds + 1,) + shard_b.shape, jnp.float32),
-            pltpu.VMEM((rounds + 1,) + shard_a.shape, jnp.float32),
-            pltpu.VMEM((rounds + 1,) + shard_b.shape, jnp.float32),
+            pltpu.VMEM((rounds + 1,) + shard_a.shape, jnp.bfloat16),
+            pltpu.VMEM((rounds + 1,) + shard_b.shape, jnp.bfloat16),
+            pltpu.VMEM((rounds + 1,) + shard_a.shape, jnp.bfloat16),
+            pltpu.VMEM((rounds + 1,) + shard_b.shape, jnp.bfloat16),
             pltpu.SemaphoreType.DMA((2 * rounds + 1,)),
             pltpu.SemaphoreType.DMA((2 * rounds + 1,)),
         ],

time: 164 us -> 145 us (0.88)
  Pallas kernels: 85.4 us -> 65.7 us
    pallas_call x1, Pallas kernels: 55 us -> 35.4 us  [shard_scan(): pl.pallas_call(functools.partial(shard_scan_kernel, shard_count), out_sha...]
  transfers between devices with their start and end apart: 1 -> 1, of which waited for: 0 -> 0; matrix products, arithmetic and copies ran while one was open for 3% -> 4% of each run, Pallas kernels for 0% -> 0%
where the time goes in v4:
time: 145 us; the launch traced here: 142 us
  Pallas kernels  65.7 us (45%)
  matrix products  54.6 us (38%)
  local copies, waits for them, and re-layouts  9.36 us (6%)
  other arithmetic  7.16 us (5%)
  starting transfers between devices  3.94 us (3%)
    pallas_call x1, Pallas kernels, shard_scan(): pl.pallas_call(functools.partial(shard_scan_kernel, shard_count), out_sha...  35.4 us
    pallas_call x1, Pallas kernels, group_sum(): pl.pallas_call(functools.partial(group_sum_kernel, group_count), out_shap...  30.4 us
    dot_general x6, matrix products, compose(): jnp.einsum('hsd,hde->hse', step_carry, prefix_a, precision=highest)  6.08 us
    dot_general x5, matrix products, unit_lower_inverse(): jnp.einsum('...st,...tu->...su', step, inverse, precision=highest)  5.62 us
    dot_general x1, matrix products, on_device(): jnp.dot(gated, w_out, preferred_element_type=jnp.float32)  5.39 us
    dot_general x5, matrix products, unit_lower_inverse(): jnp.einsum('...st,...tu->...su', inverse, off_blocks, precision=highest)  4.77 us
    ppermute x1, starting transfers between devices, passed_along(): return lax.ppermute(block, axis, route)  3.94 us
    dot_general x6, matrix products, apply_shard(): jnp.einsum('hde,hef->hdf', trans_mat, state_now, precision=highest)  3.08 us
  transfers between devices with their start and end apart: 1, of which 0 were waited for; matrix products, arithmetic and copies ran while one was open for 4% of the time, Pallas kernels for 0%

profile of v4, /device:TPU:1, one launch (start us, length us, event | category | flops | bytes accessed | tf_op | source)
XLA Modules:
  0.0 141.9 jit_solution(2482375182014496870)
XLA Ops:
  0.0 2.4 %fusion.98 = (f32[384,256]{1,0:T(8,128)S(1)}, bf16[384,256]{1,0:T(8,128)(2,1)S(1)}) fusion(bf16[384,2048]{1,0:T(8,128)(2,1)} %param.21, bf16[2048,256]{1,0:T(8,128)(2,1)} %param.23), kind=kOutput, calls=%fused_computation.210 | convolution fusion | flops 402849792 | bytes 3211264 | tf_op jit(solution)/shard_map/dot_general | solution.py:32
  2.4 0.6 copy-done.21
  3.0 1.9 %fusion.100 = (f32[384,512]{1,0:T(8,128)}, bf16[384,512]{1,0:T(8,128)(2,1)S(1)}) fusion(bf16[384,2048]{1,0:T(8,128)(2,1)S(1)} %copy-done.1, bf16[2048,512]{1,0:T(8,128)(2,1)S(1)} %copy-done.21), kind=kOutput, calls=%fused_computation.212 | convolution fusion | flops 805699584 | bytes 4849664 | tf_op jit(solution)/shard_map/dot_general | solution.py:33
  5.0 0.6 fusion.99
  5.6 3.9 %collective-permute-start = (bf16[3,1024]{1,0:T(4,128)(2,1)S(1)}, bf16[3,1024]{1,0:T(4,128)(2,1)S(1)}, u32[]{:S(2)}, u32[]{:S(2)}) collective-permute-start(bf16[3,1024]{1,0:T(4,128)(2,1)S(1)} %pad_maximum_fusion.3), channel_id=1, source_target_pairs={{0,8},{8,16},{16,24},{24,32},{32,40},{40,48},{48,56},{56,64},{64,7... | collective-permute-start | bytes 18440 | tf_op jit(solution)/shard_map/ppermute | solution.py:27
  9.7 0.5 fusion.94
  10.3 1.9 %fusion.24 = f32[384,4]{0,1:T(4,128)S(1)} fusion(bf16[384,2048]{1,0:T(8,128)(2,1)} %param.21, bf16[2048,4]{0,1:T(4,128)(2,1)S(1)} %copy-done.15), kind=kOutput, calls=%fused_computation.61 | convolution fusion | flops 6296064 | bytes 1595392 | tf_op jit(solution)/shard_map/dot_general | solution.py:86
  12.4 1.9 %reduce_window_sum.11 = f32[6,4,64]{2,1,0:T(4,128)S(1)} reduce-window(f32[6,4,64]{2,1,0:T(4,128)S(1)} %copy.69, f32[]{:T(128)} %constant.16.clone.1), window={size=1x1x64 pad=0_0x0_0x63_0}, to_apply=%region_0.1 | reduce-window | flops 96768 | bytes 12292 | tf_op jit(solution)/shard_map/jit(cumsum)/reduce_window_sum | solution.py:115
  14.9 1.2 divide_multiply_fusion.1
  16.1 1.2 reshape.82
  17.3 0.5 multiply_reduce_fusion.1
  18.6 0.5 multiply_reduce_fusion.2
  19.7 2.3 %convolution_multiply_fusion.1 = f32[6,4,64,64]{3,2,1,0:T(8,128)} fusion(f32[6,4,64,128]{3,2,0,1:T(8,128)S(1)} %bitcast.282, f32[6,64,4,128]{3,1,0,2:T(8,128)S(1)} %bitcast.280, f32[6,4,64]{2,1,0:T(4,128)S(1)} %reduce_window_sum.11, pred[64,64]{1,0:T(8,128)(4,1)S(1)} %get-tuple-element.36), kind=kOutput, calls=%fused_computation.13 | convolution fusion | flops 151388160 | bytes 1976320 | tf_op jit(solution)/shard_map/...sd,...td->...st/dot_general | solution.py:134
  22.0 1.4 %multiply_subtract_fusion.1 = (f32[6,4,64,64]{3,2,1,0:T(8,128)S(1)}, f32[6,4,64,64]{3,2,1,0:T(8,128)S(1)}) fusion(f32[64,64]{1,0:T(8,128)S(1)} %copy-done.23, f32[64,64]{1,0:T(8,128)S(1)} %copy-done.24, f32[6,4,64,128]{3,2,0,1:T(8,128)S(1)} %bitcast.283, f32[6,4,64]{2,1,0:T(4,128)S(1)} %reduce_window_sum.11, pred[64,64]{1,0:T(8,128)(4,1)S(1)} %get-tuple-element.36, ...), kind=kOutput, calls=%fused_computation.94 | convolution fusion | flops 151781376 | bytes 1626112 | tf_op jit(solution)/shard_map/...sd,...td->...st/dot_general | solution.py:122
  23.5 0.9 fusion.49
  24.4 1.0 convolution_subtract_fusion.4
  25.4 0.9 fusion.47
  26.4 0.9 convolution_subtract_fusion.3
  27.3 0.9 fusion.45
  28.2 1.0 convolution_subtract_fusion.2
  29.2 1.1 fusion.43
  30.3 1.0 convolution_subtract_fusion.1
  31.3 0.9 fusion.41
  32.2 1.8 %convolution_subtract_fusion = f32[6,4,64,64]{3,2,1,0:T(8,128)} fusion(f32[6,4,64,64]{3,2,1,0:T(8,128)S(1)} %convolution_subtract_fusion.1, f32[6,4,64,64]{3,2,1,0:T(8,128)S(1)} %fusion.41), kind=kOutput, calls=%fused_computation.2 | convolution fusion | flops 75595776 | bytes 1179648 | tf_op jit(solution)/shard_map/...st,...tu->...su/dot_general | solution.py:108
  34.1 1.4 divide_multiply_fusion
  35.4 2.3 %reshape_reshape.11 = f32[6,64,4,128]{3,2,1,0:T(4,128)} reshape(f32[384,512]{1,0:T(8,128)} %divide_multiply_fusion) | data formatting | bytes 1572864 | tf_op jit(solution)/shard_map/reshape;reshape | solution.py:92
  37.7 2.4 %fusion.36 = f32[6,4,64,128]{3,2,1,0:T(8,128)S(1)} fusion(f32[6,4,64,64]{3,2,1,0:T(8,128)} %convolution_subtract_fusion, f32[6,64,4,128]{3,2,1,0:T(4,128)} %reshape_reshape.11, f32[6,4,64]{2,1,0:T(4,128)S(1)} %bitcast.290), kind=kOutput, calls=%fused_computation.76 | convolution fusion | flops 151191552 | bytes 1972224 | tf_op jit(solution)/shard_map/...st,...td->...sd/dot_general | solution.py:131
  40.2 0.5 broadcast_multiply_fusion
  40.6 0.6 copy-done.5
  41.3 0.9 fusion.39
  42.2 0.9 fusion.101
  43.2 2.6 %fusion.51 = f32[6,4,128,128]{3,2,1,0:T(8,128)S(1)} fusion(f32[6,4,64,128]{3,2,1,0:T(8,128)S(1)} %fusion.36, f32[6,4,64,128]{3,2,0,1:T(8,128)S(1)} %get-tuple-element.5), kind=kOutput, calls=%fused_computation.96 | convolution fusion | flops 301989888 | bytes 3145728 | tf_op jit(solution)/shard_map/...sd,...se->...de/dot_general | solution.py:140
  45.8 1.0 convolution_subtract_fusion.5
  47.0 1.0 fusion.9
  48.0 3.0 %multiply_subtract_fusion = f32[6,4,128,128]{3,2,1,0:T(8,128)S(1)} fusion(f32[6,4,64,128]{3,2,1,0:T(8,128)S(1)} %fusion.39, f32[128,128]{1,0:T(8,128)S(1)} %fusion.92, f32[6,4]{1,0:T(8,128)S(1)} %copy.81, f32[6,4,64,128]{3,2,0,1:T(8,128)S(1)} %get-tuple-element.5), kind=kOutput, calls=%fused_computation.1 | convolution fusion | flops 302776320 | bytes 3211360 | tf_op jit(solution)/shard_map/...sd,...se->...de/dot_general | solution.py:137
  54.8 1.1 convolution_add_fusion.b_ref
  56.7 1.0 fusion.8
  58.1 1.0 fusion.7
  59.6 1.0 fusion.6
  61.0 1.0 fusion.5
  62.0 1.1 fusion.87.a_ref
  63.1 1.0 fusion.4
  64.2 35.4 %shard_map.199 = f32[4,128,128]{2,1,0:T(8,128)} custom-call(f32[4,128,128]{2,1,0:T(8,128)} %fusion.87.a_ref, f32[4,128,128]{2,1,0:T(8,128)} %convolution_add_fusion.b_ref), custom_call_target="tpu_custom_call" | custom-call | tf_op jit(solution)/shard_map/pallas_call | solution.py:251
  99.5 2.7 %multiply_reduce_fusion = (f32[6,64,4]{1,2,0:T(4,128)S(1)}, f32[6,64,4,128]{3,1,2,0:T(8,128)S(1)}) fusion(f32[6,4,64,128]{3,2,1,0:T(8,128)} %copy-done.6, f32[6,4,64,128]{3,2,1,0:T(8,128)} %fusion.4, f32[4,128,128]{2,1,0:T(8,128)} %shard_map.199), kind=kOutput, calls=%fused_computation.82 | convolution fusion | flops 302578176 | bytes 2627584 | tf_op jit(solution)/shard_map/jhsd,hde->jhse/dot_general | solution.py:399
  102.4 1.4 copy.86
  104.2 5.4 %convolution_convert_fusion.part_ref = bf16[384,2048]{1,0:T(8,128)(2,1)} fusion(bf16[512,2048]{1,0:T(8,128)(2,1)S(1)} %copy-done, f32[48,8,4,128]{3,2,1,0:T(4,128)S(1)} %bitcast.286, f32[48,8,4,128]{3,2,1,0:T(4,128)} %bitcast.285, bf16[384,2048]{1,0:T(8,128)(2,1)} %param.21, bf16[2048,512]{1,0:T(8,128)(2,1)} %param.25, f32[512]{0:T(512)S(1)} %broadcast_bitcast_fusion), kind=kOutput, calls=%fused_computation | convolution fusion | flops 1613365248 | bytes 8914944 | tf_op jit(solution)/shard_map/dot_general | solution.py:402
  109.6 30.4 %shard_map.200 = bf16[48,2048]{1,0:T(8,128)(2,1)} custom-call(bf16[384,2048]{1,0:T(8,128)(2,1)} %convolution_convert_fusion.part_ref), custom_call_target="tpu_custom_call" | custom-call | tf_op jit(solution)/shard_map/pallas_call | solution.py:318
  140.0 1.6 %copy.134 = bf16[48,2048]{1,0:T(8,128)(2,1)} copy(bf16[48,2048]{1,0:T(8,128)(2,1)} %shard_map.200) | data formatting | bytes 393216
  (103 shorter events, 8.8 us)
Async XLA Ops:
  0.0 104.2 %copy-start = (bf16[512,2048]{1,0:T(8,128)(2,1)S(1)}, bf16[512,2048]{1,0:T(8,128)(2,1)}, u32[]{:S(2)}) copy-start(bf16[512,2048]{1,0:T(8,128)(2,1)} %param.34) | copy-start | bytes 6291460
  0.0 2.4 %copy-start.1 = (bf16[384,2048]{1,0:T(8,128)(2,1)S(1)}, bf16[384,2048]{1,0:T(8,128)(2,1)}, u32[]{:S(2)}) copy-start(bf16[384,2048]{1,0:T(8,128)(2,1)} %param.21) | copy-start | bytes 4718596
  0.0 3.0 %copy-start.21 = (bf16[2048,512]{1,0:T(8,128)(2,1)S(1)}, bf16[2048,512]{1,0:T(8,128)(2,1)}, u32[]{:S(2)}) copy-start(bf16[2048,512]{1,0:T(8,128)(2,1)} %param.24) | copy-start | bytes 6291460
  3.0 1.9 %copy-start.7 = (bf16[2048,256]{1,0:T(8,128)(2,1)S(1)}, bf16[2048,256]{1,0:T(8,128)(2,1)}, u32[]{:S(2)}) copy-start(bf16[2048,256]{1,0:T(8,128)(2,1)} %param.22) | copy-start | bytes 3145732
  4.9 4.7 %copy-start.17 = (bf16[4,256]{1,0:T(4,128)(2,1)S(1)}, bf16[4,256]{1,0:T(4,128)(2,1)}, u32[]{:S(2)}) copy-start(bf16[4,256]{1,0:T(4,128)(2,1)} %param.29) | copy-start | bytes 6148
  4.9 4.7 %copy-start.18 = (bf16[4,256]{1,0:T(4,128)(2,1)S(1)}, bf16[4,256]{1,0:T(4,128)(2,1)}, u32[]{:S(2)}) copy-start(bf16[4,256]{1,0:T(4,128)(2,1)} %param.28) | copy-start | bytes 6148
  4.9 4.7 %copy-start.22 = (f32[4]{0:T(128)S(1)}, f32[4]{0:T(128)}, u32[]{:S(2)}) copy-start(f32[4]{0:T(128)} %param.31) | copy-start | bytes 52
  5.0 4.7 %copy-start.14 = (bf16[2048,4]{0,1:T(4,128)(2,1)S(1)}, bf16[2048,4]{0,1:T(4,128)(2,1)}, u32[]{:S(2)}) copy-start(bf16[2048,4]{0,1:T(4,128)(2,1)} %param.26) | copy-start | bytes 49156
  5.0 4.7 %copy-start.19 = (f32[4]{0:T(128)S(1)}, f32[4]{0:T(128)}, u32[]{:S(2)}) copy-start(f32[4]{0:T(128)} %param.32) | copy-start | bytes 52
  5.6 4.8 %copy-start.15 = (bf16[2048,4]{0,1:T(4,128)(2,1)S(1)}, bf16[2048,4]{0,1:T(4,128)(2,1)}, u32[]{:S(2)}) copy-start(bf16[2048,4]{0,1:T(4,128)(2,1)} %param.27) | copy-start | bytes 49156
  5.6 9.3 %collective-permute-start = (bf16[3,1024]{1,0:T(4,128)(2,1)S(1)}, bf16[3,1024]{1,0:T(4,128)(2,1)S(1)}, u32[]{:S(2)}, u32[]{:S(2)}) collective-permute-start(bf16[3,1024]{1,0:T(4,128)(2,1)S(1)} %pad_maximum_fusion.3), channel_id=1, source_target_pairs={{0,8},{8,16},{16,24},{24,32},{32,40},{40,48},{48,56},{56,64},{64,7... | collective-permute-start | bytes 18440 | tf_op jit(solution)/shard_map/ppermute | solution.py:27
  9.7 2.7 %copy-start.16 = (bf16[4,512]{1,0:T(4,128)(2,1)S(1)}, bf16[4,512]{1,0:T(4,128)(2,1)}, u32[]{:S(2)}) copy-start(bf16[4,512]{1,0:T(4,128)(2,1)} %param.30) | copy-start | bytes 12292
  9.7 5.0 %copy-start.20 = (f32[128]{0:T(128)S(1)}, f32[128]{0:T(128)}, u32[]{:S(2)}) copy-start(f32[128]{0:T(128)} %param.33) | copy-start | bytes 1540
  19.6 2.4 %copy-start.3 = (f32[384,2,2,128]{3,0,2,1:T(8,128)}, f32[384,2,2,128]{3,0,2,1:T(8,128)S(1)}, u32[]{:S(2)}) copy-start(f32[384,2,2,128]{3,0,2,1:T(8,128)S(1)} %broadcast_in_dim.101) | copy-start | bytes 2359300
  19.7 2.4 %copy-start.23 = (f32[64,64]{1,0:T(8,128)S(1)}, f32[64,64]{1,0:T(8,128)}, u32[]{:S(2)}) copy-start(f32[64,64]{1,0:T(8,128)} %constant.39.clone) | copy-start | bytes 49156
  19.7 2.4 %copy-start.24 = (f32[64,64]{1,0:T(8,128)S(1)}, f32[64,64]{1,0:T(8,128)}, u32[]{:S(2)}) copy-start(f32[64,64]{1,0:T(8,128)} %constant.40.clone) | copy-start | bytes 49156
  22.0 1.5 %copy-start.13 = (f32[64,64]{1,0:T(8,128)S(1)}, f32[64,64]{1,0:T(8,128)}, u32[]{:S(2)}) copy-start(f32[64,64]{1,0:T(8,128)} %constant.41.clone) | copy-start | bytes 49156
  24.4 1.0 copy-start.12
  26.3 0.9 copy-start.11
  28.2 1.0 copy-start.10
  30.3 1.0 copy-start.9
  32.2 1.8 %copy-start.8 = (f32[384,512]{1,0:T(8,128)S(1)}, f32[384,512]{1,0:T(8,128)}, u32[]{:S(2)}) copy-start(f32[384,512]{1,0:T(8,128)} %get-tuple-element.29) | copy-start | bytes 2359300
  37.7 2.4 %copy-start.4 = (f32[384,2,2,128]{3,0,2,1:T(8,128)S(1)}, f32[384,2,2,128]{3,0,2,1:T(8,128)}, u32[]{:S(2)}) copy-start(f32[384,2,2,128]{3,0,2,1:T(8,128)} %copy-done.3) | copy-start | bytes 2359300
  40.1 1.1 copy-start.5
  40.6 1.6 %copy-start.2 = (f32[6,4,64,64]{3,2,1,0:T(8,128)S(1)}, f32[6,4,64,64]{3,2,1,0:T(8,128)}, u32[]{:S(2)}) copy-start(f32[6,4,64,64]{3,2,1,0:T(8,128)} %convolution_multiply_fusion.1) | copy-start | bytes 1179652
  56.3 3.3 %copy-start.6 = (f32[6,4,64,128]{3,2,1,0:T(8,128)}, f32[6,4,64,128]{3,2,1,0:T(8,128)S(1)}, u32[]{:S(2)}) copy-start(f32[6,4,64,128]{3,2,1,0:T(8,128)S(1)} %fusion.11) | copy-start | bytes 2359300

commit v5 on v4

--- a/solution.py
+++ b/solution.py
@@ -17,7 +17,7 @@
 SPAN = 64
 
 
-highest = lax.Precision.HIGHEST
+highest = lax.Precision.HIGH
 norm_eps = 1e-06
 
 

time: 145 us -> 129 us (0.89); the launches traced: 142 us -> 128 us
  matrix products: 54.6 us -> 41.4 us
    dot_general x5, matrix products: 4.77 us -> 2.43 us  [unit_lower_inverse(): jnp.einsum('...st,...tu->...su', inverse, off_blocks, precision=highest)]
    dot_general x5, matrix products: 5.62 us -> 3.44 us  [unit_lower_inverse(): jnp.einsum('...st,...tu->...su', step, inverse, precision=highest)]
where the time goes in v5:
time: 129 us; the launch traced here: 128 us
  Pallas kernels  65.2 us (51%)
  matrix products  41.4 us (32%)
  local copies, waits for them, and re-layouts  10.3 us (8%)
  other arithmetic  6.79 us (5%)
  starting transfers between devices  3.94 us (3%)
    pallas_call x1, Pallas kernels, shard_scan(): pl.pallas_call(functools.partial(shard_scan_kernel, shard_count), out_sha...  34.6 us
    pallas_call x1, Pallas kernels, group_sum(): pl.pallas_call(functools.partial(group_sum_kernel, group_count), out_shap...  30.6 us
    dot_general x6, matrix products, compose(): jnp.einsum('hsd,hde->hse', step_carry, prefix_a, precision=highest)  5.39 us
    dot_general x1, matrix products, on_device(): jnp.dot(gated, w_out, preferred_element_type=jnp.float32)  5.39 us
    ppermute x1, starting transfers between devices, passed_along(): return lax.ppermute(block, axis, route)  3.94 us
    unnamed x51, local copies, waits for them, and re-layouts  3.84 us
    dot_general x5, matrix products, unit_lower_inverse(): jnp.einsum('...st,...tu->...su', step, inverse, precision=highest)  3.44 us
    mul x2, other arithmetic, conv_silu(): return jax.nn.silu(summed)  2.61 us
  transfers between devices with their start and end apart: 1, of which 0 were waited for; matrix products, arithmetic and copies ran while one was open for 4% of the time, Pallas kernels for 0%

profile of v5, /device:TPU:1, one launch (start us, length us, event | category | flops | bytes accessed | tf_op | source)
XLA Modules:
  0.0 128.4 jit_solution(9052268885931595099)
XLA Ops:
  0.0 2.4 %fusion.98 = (f32[384,256]{1,0:T(8,128)S(1)}, bf16[384,256]{1,0:T(8,128)(2,1)S(1)}) fusion(bf16[384,2048]{1,0:T(8,128)(2,1)} %param.21, bf16[2048,256]{1,0:T(8,128)(2,1)} %param.23), kind=kOutput, calls=%fused_computation.210 | convolution fusion | flops 402849792 | bytes 3211264 | tf_op jit(solution)/shard_map/dot_general | solution.py:32
  2.5 0.6 copy-done.21
  3.0 1.9 %fusion.100 = (f32[384,512]{1,0:T(8,128)}, bf16[384,512]{1,0:T(8,128)(2,1)S(1)}) fusion(bf16[384,2048]{1,0:T(8,128)(2,1)S(1)} %copy-done.1, bf16[2048,512]{1,0:T(8,128)(2,1)S(1)} %copy-done.21), kind=kOutput, calls=%fused_computation.212 | convolution fusion | flops 805699584 | bytes 4849664 | tf_op jit(solution)/shard_map/dot_general | solution.py:33
  5.0 0.6 fusion.99
  5.6 3.9 %collective-permute-start = (bf16[3,1024]{1,0:T(4,128)(2,1)S(1)}, bf16[3,1024]{1,0:T(4,128)(2,1)S(1)}, u32[]{:S(2)}, u32[]{:S(2)}) collective-permute-start(bf16[3,1024]{1,0:T(4,128)(2,1)S(1)} %pad_maximum_fusion.3), channel_id=1, source_target_pairs={{0,8},{8,16},{16,24},{24,32},{32,40},{40,48},{48,56},{56,64},{64,7... | collective-permute-start | bytes 18440 | tf_op jit(solution)/shard_map/ppermute | solution.py:27
  9.7 0.5 fusion.94
  10.3 1.9 %fusion.24 = f32[384,4]{0,1:T(4,128)S(1)} fusion(bf16[384,2048]{1,0:T(8,128)(2,1)} %param.21, bf16[2048,4]{0,1:T(4,128)(2,1)S(1)} %copy-done.15), kind=kOutput, calls=%fused_computation.61 | convolution fusion | flops 6296064 | bytes 1595392 | tf_op jit(solution)/shard_map/dot_general | solution.py:86
  12.4 1.6 %reduce_window_sum.11 = f32[6,4,64]{2,1,0:T(4,128)S(1)} reduce-window(f32[6,4,64]{2,1,0:T(4,128)S(1)} %copy.69, f32[]{:T(128)} %constant.16.clone.1), window={size=1x1x64 pad=0_0x0_0x63_0}, to_apply=%region_0.1 | reduce-window | flops 96768 | bytes 12292 | tf_op jit(solution)/shard_map/jit(cumsum)/reduce_window_sum | solution.py:115
  14.5 1.2 divide_multiply_fusion.1
  15.7 1.2 reshape.82
  16.9 0.5 multiply_reduce_fusion.1
  18.2 0.5 multiply_reduce_fusion.2
  19.4 1.7 %convolution_multiply_fusion.1 = f32[6,4,64,64]{3,2,1,0:T(8,128)} fusion(f32[6,4,64,128]{3,2,0,1:T(8,128)S(1)} %bitcast.282, f32[6,64,4,128]{3,1,0,2:T(8,128)S(1)} %bitcast.280, f32[6,4,64]{2,1,0:T(4,128)S(1)} %reduce_window_sum.11, pred[64,64]{1,0:T(8,128)(4,1)S(1)} %get-tuple-element.36), kind=kOutput, calls=%fused_computation.13 | convolution fusion | flops 75890688 | bytes 1976320 | tf_op jit(solution)/shard_map/...sd,...td->...st/dot_general | solution.py:134
  21.1 0.8 multiply_subtract_fusion.1
  21.9 0.5 fusion.49
  22.4 0.5 convolution_subtract_fusion.4
  23.2 0.5 fusion.47
  23.7 0.5 convolution_subtract_fusion.3
  24.4 0.5 fusion.45
  24.9 0.5 convolution_subtract_fusion.2
  25.7 0.5 fusion.43
  26.2 0.5 convolution_subtract_fusion.1
  26.9 0.5 fusion.41
  27.4 1.4 %convolution_subtract_fusion = f32[6,4,64,64]{3,2,1,0:T(8,128)} fusion(f32[6,4,64,64]{3,2,1,0:T(8,128)S(1)} %convolution_subtract_fusion.1, f32[6,4,64,64]{3,2,1,0:T(8,128)S(1)} %fusion.41), kind=kOutput, calls=%fused_computation.2 | convolution fusion | flops 37847040 | bytes 1179648 | tf_op jit(solution)/shard_map/...st,...tu->...su/dot_general | solution.py:108
  28.8 1.4 %divide_multiply_fusion = f32[384,512]{1,0:T(8,128)} fusion(f32[384,512]{1,0:T(8,128)S(1)} %copy-done.8, f32[3,512]{1,0:T(4,128)S(1)} %slice_convert_fusion, f32[512]{0:T(512)S(1)} %bitcast.294, f32[512]{0:T(512)S(1)} %bitcast.295, f32[512]{0:T(512)S(1)} %bitcast.293, f32[512]{0:T(512)S(1)} %bitcast.292), kind=kLoop, calls=%fused_computation.83 | loop fusion | flops 2752512 | bytes 1587200 | tf_op jit(solution)/shard_map/jit(silu)/mul | solution.py:44
  30.2 2.3 %reshape_reshape.11 = f32[6,64,4,128]{3,2,1,0:T(4,128)} reshape(f32[384,512]{1,0:T(8,128)} %divide_multiply_fusion) | data formatting | bytes 1572864 | tf_op jit(solution)/shard_map/reshape;reshape | solution.py:92
  32.5 2.0 %fusion.36 = f32[6,4,64,128]{3,2,1,0:T(8,128)S(1)} fusion(f32[6,4,64,64]{3,2,1,0:T(8,128)} %convolution_subtract_fusion, f32[6,64,4,128]{3,2,1,0:T(4,128)} %reshape_reshape.11, f32[6,4,64]{2,1,0:T(4,128)S(1)} %bitcast.290), kind=kOutput, calls=%fused_computation.76 | convolution fusion | flops 75694080 | bytes 1972224 | tf_op jit(solution)/shard_map/...st,...td->...sd/dot_general | solution.py:131
  34.6 0.5 broadcast_multiply_fusion
  35.1 0.6 copy-done.5
  35.7 0.5 fusion.39
  36.2 0.7 fusion.101
  36.9 1.4 %fusion.51 = f32[6,4,128,128]{3,2,1,0:T(8,128)S(1)} fusion(f32[6,4,64,128]{3,2,1,0:T(8,128)S(1)} %fusion.36, f32[6,4,64,128]{3,2,0,1:T(8,128)S(1)} %get-tuple-element.5), kind=kOutput, calls=%fused_computation.96 | convolution fusion | flops 150994944 | bytes 3145728 | tf_op jit(solution)/shard_map/...sd,...se->...de/dot_general | solution.py:140
  38.4 0.5 convolution_subtract_fusion.5
  39.1 0.9 fusion.9
  39.9 1.5 %multiply_subtract_fusion = f32[6,4,128,128]{3,2,1,0:T(8,128)S(1)} fusion(f32[6,4,64,128]{3,2,1,0:T(8,128)S(1)} %fusion.39, f32[128,128]{1,0:T(8,128)S(1)} %fusion.92, f32[6,4]{1,0:T(8,128)S(1)} %copy.81, f32[6,4,64,128]{3,2,0,1:T(8,128)S(1)} %get-tuple-element.5), kind=kOutput, calls=%fused_computation.1 | convolution fusion | flops 151781376 | bytes 3211360 | tf_op jit(solution)/shard_map/...sd,...se->...de/dot_general | solution.py:137
  44.1 1.0 convolution_add_fusion.b_ref
  45.7 0.9 fusion.8
  46.9 0.9 fusion.7
  48.0 0.9 fusion.6
  49.2 0.9 fusion.5
  50.1 1.0 fusion.87.a_ref
  51.1 0.9 fusion.4
  52.0 34.6 %shard_map.199 = f32[4,128,128]{2,1,0:T(8,128)} custom-call(f32[4,128,128]{2,1,0:T(8,128)} %fusion.87.a_ref, f32[4,128,128]{2,1,0:T(8,128)} %convolution_add_fusion.b_ref), custom_call_target="tpu_custom_call" | custom-call | tf_op jit(solution)/shard_map/pallas_call | solution.py:251
  86.6 2.1 %multiply_reduce_fusion = (f32[6,64,4]{1,2,0:T(4,128)S(1)}, f32[6,64,4,128]{3,1,2,0:T(8,128)S(1)}) fusion(f32[6,4,64,128]{3,2,1,0:T(8,128)} %copy-done.6, f32[6,4,64,128]{3,2,1,0:T(8,128)} %fusion.4, f32[4,128,128]{2,1,0:T(8,128)} %shard_map.199), kind=kOutput, calls=%fused_computation.82 | convolution fusion | flops 151583232 | bytes 2627584 | tf_op jit(solution)/shard_map/jhsd,hde->jhse/dot_general | solution.py:399
  88.9 1.4 %copy.86 = f32[6,64,4,128]{3,2,1,0:T(4,128)} copy(f32[6,64,4,128]{3,1,2,0:T(8,128)S(1)} %get-tuple-element.32) | data formatting | bytes 1572864 | tf_op jit(solution)/shard_map/transpose | solution.py:400
  90.8 5.4 %convolution_convert_fusion.part_ref = bf16[384,2048]{1,0:T(8,128)(2,1)} fusion(bf16[512,2048]{1,0:T(8,128)(2,1)S(1)} %copy-done, f32[48,8,4,128]{3,2,1,0:T(4,128)S(1)} %bitcast.286, f32[48,8,4,128]{3,2,1,0:T(4,128)} %bitcast.285, bf16[384,2048]{1,0:T(8,128)(2,1)} %param.21, bf16[2048,512]{1,0:T(8,128)(2,1)} %param.25, f32[512]{0:T(512)S(1)} %broadcast_bitcast_fusion), kind=kOutput, calls=%fused_computation | convolution fusion | flops 1613365248 | bytes 8914944 | tf_op jit(solution)/shard_map/dot_general | solution.py:402
  96.2 30.6 %shard_map.200 = bf16[48,2048]{1,0:T(8,128)(2,1)} custom-call(bf16[384,2048]{1,0:T(8,128)(2,1)} %convolution_convert_fusion.part_ref), custom_call_target="tpu_custom_call" | custom-call | tf_op jit(solution)/shard_map/pallas_call | solution.py:318
  126.7 1.6 %copy.134 = bf16[48,2048]{1,0:T(8,128)(2,1)} copy(bf16[48,2048]{1,0:T(8,128)(2,1)} %shard_map.200) | data formatting | bytes 393216
  (103 shorter events, 7.9 us)
Async XLA Ops:
  0.0 90.8 %copy-start = (bf16[512,2048]{1,0:T(8,128)(2,1)S(1)}, bf16[512,2048]{1,0:T(8,128)(2,1)}, u32[]{:S(2)}) copy-start(bf16[512,2048]{1,0:T(8,128)(2,1)} %param.34) | copy-start | bytes 6291460
  0.0 2.4 %copy-start.1 = (bf16[384,2048]{1,0:T(8,128)(2,1)S(1)}, bf16[384,2048]{1,0:T(8,128)(2,1)}, u32[]{:S(2)}) copy-start(bf16[384,2048]{1,0:T(8,128)(2,1)} %param.21) | copy-start | bytes 4718596
  0.0 3.0 %copy-start.21 = (bf16[2048,512]{1,0:T(8,128)(2,1)S(1)}, bf16[2048,512]{1,0:T(8,128)(2,1)}, u32[]{:S(2)}) copy-start(bf16[2048,512]{1,0:T(8,128)(2,1)} %param.24) | copy-start | bytes 6291460
  3.0 1.9 %copy-start.7 = (bf16[2048,256]{1,0:T(8,128)(2,1)S(1)}, bf16[2048,256]{1,0:T(8,128)(2,1)}, u32[]{:S(2)}) copy-start(bf16[2048,256]{1,0:T(8,128)(2,1)} %param.22) | copy-start | bytes 3145732
  4.9 4.7 %copy-start.17 = (bf16[4,256]{1,0:T(4,128)(2,1)S(1)}, bf16[4,256]{1,0:T(4,128)(2,1)}, u32[]{:S(2)}) copy-start(bf16[4,256]{1,0:T(4,128)(2,1)} %param.29) | copy-start | bytes 6148
  4.9 4.7 %copy-start.18 = (bf16[4,256]{1,0:T(4,128)(2,1)S(1)}, bf16[4,256]{1,0:T(4,128)(2,1)}, u32[]{:S(2)}) copy-start(bf16[4,256]{1,0:T(4,128)(2,1)} %param.28) | copy-start | bytes 6148
  4.9 4.7 %copy-start.22 = (f32[4]{0:T(128)S(1)}, f32[4]{0:T(128)}, u32[]{:S(2)}) copy-start(f32[4]{0:T(128)} %param.31) | copy-start | bytes 52
  4.9 4.7 %copy-start.14 = (bf16[2048,4]{0,1:T(4,128)(2,1)S(1)}, bf16[2048,4]{0,1:T(4,128)(2,1)}, u32[]{:S(2)}) copy-start(bf16[2048,4]{0,1:T(4,128)(2,1)} %param.26) | copy-start | bytes 49156
  5.0 4.7 %copy-start.19 = (f32[4]{0:T(128)S(1)}, f32[4]{0:T(128)}, u32[]{:S(2)}) copy-start(f32[4]{0:T(128)} %param.32) | copy-start | bytes 52
  5.6 4.8 %copy-start.15 = (bf16[2048,4]{0,1:T(4,128)(2,1)S(1)}, bf16[2048,4]{0,1:T(4,128)(2,1)}, u32[]{:S(2)}) copy-start(bf16[2048,4]{0,1:T(4,128)(2,1)} %param.27) | copy-start | bytes 49156
  5.6 8.9 %collective-permute-start = (bf16[3,1024]{1,0:T(4,128)(2,1)S(1)}, bf16[3,1024]{1,0:T(4,128)(2,1)S(1)}, u32[]{:S(2)}, u32[]{:S(2)}) collective-permute-start(bf16[3,1024]{1,0:T(4,128)(2,1)S(1)} %pad_maximum_fusion.3), channel_id=1, source_target_pairs={{0,8},{8,16},{16,24},{24,32},{32,40},{40,48},{48,56},{56,64},{64,7... | collective-permute-start | bytes 18440 | tf_op jit(solution)/shard_map/ppermute | solution.py:27
  9.7 2.7 %copy-start.16 = (bf16[4,512]{1,0:T(4,128)(2,1)S(1)}, bf16[4,512]{1,0:T(4,128)(2,1)}, u32[]{:S(2)}) copy-start(bf16[4,512]{1,0:T(4,128)(2,1)} %param.30) | copy-start | bytes 12292
  9.7 4.7 %copy-start.20 = (f32[128]{0:T(128)S(1)}, f32[128]{0:T(128)}, u32[]{:S(2)}) copy-start(f32[128]{0:T(128)} %param.33) | copy-start | bytes 1540
  19.3 1.8 %copy-start.3 = (f32[384,2,2,128]{3,0,2,1:T(8,128)}, f32[384,2,2,128]{3,0,2,1:T(8,128)S(1)}, u32[]{:S(2)}) copy-start(f32[384,2,2,128]{3,0,2,1:T(8,128)S(1)} %broadcast_in_dim.101) | copy-start | bytes 2359300
  19.3 1.8 %copy-start.23 = (f32[64,64]{1,0:T(8,128)S(1)}, f32[64,64]{1,0:T(8,128)}, u32[]{:S(2)}) copy-start(f32[64,64]{1,0:T(8,128)} %constant.39.clone) | copy-start | bytes 49156
  19.3 1.8 %copy-start.24 = (f32[64,64]{1,0:T(8,128)S(1)}, f32[64,64]{1,0:T(8,128)}, u32[]{:S(2)}) copy-start(f32[64,64]{1,0:T(8,128)} %constant.40.clone) | copy-start | bytes 49156
  21.0 0.8 copy-start.13
  22.4 0.8 copy-start.12
  23.6 0.8 copy-start.11
  24.9 0.8 copy-start.10
  26.2 0.8 copy-start.9
  27.4 1.4 %copy-start.8 = (f32[384,512]{1,0:T(8,128)S(1)}, f32[384,512]{1,0:T(8,128)}, u32[]{:S(2)}) copy-start(f32[384,512]{1,0:T(8,128)} %get-tuple-element.29) | copy-start | bytes 2359300
  32.5 2.1 %copy-start.4 = (f32[384,2,2,128]{3,0,2,1:T(8,128)S(1)}, f32[384,2,2,128]{3,0,2,1:T(8,128)}, u32[]{:S(2)}) copy-start(f32[384,2,2,128]{3,0,2,1:T(8,128)} %copy-done.3) | copy-start | bytes 2359300
  34.6 1.1 copy-start.5
  35.0 1.2 copy-start.2
  45.4 2.7 %copy-start.6 = (f32[6,4,64,128]{3,2,1,0:T(8,128)}, f32[6,4,64,128]{3,2,1,0:T(8,128)S(1)}, u32[]{:S(2)}) copy-start(f32[6,4,64,128]{3,2,1,0:T(8,128)S(1)} %fusion.11) | copy-start | bytes 2359300

commit v6 on v2

--- a/solution.py
+++ b/solution.py
@@ -17,7 +17,7 @@
 SPAN = 64
 
 
-highest = lax.Precision.HIGHEST
+highest = lax.Precision.HIGH
 norm_eps = 1e-06
 
 
@@ -164,6 +164,122 @@
     return jnp.einsum("hde,hef->hdf", trans_mat, state_now, precision=highest) + written
 
 
+def scan_plan(shard_count):
+    plan = []
+    cover = 0
+    while cover < shard_count - 1:
+        if cover == 0:
+            distances = [d for d in range(1, 5) if d < shard_count]
+            new_cover = 4
+        else:
+            distances = [cover * k for k in range(1, 4) if cover * k < shard_count]
+            new_cover = cover * 4
+        last = new_cover >= shard_count - 1
+        plan.append([(d, (not last) or d != distances[-1]) for d in distances])
+        cover = new_cover
+    return plan
+
+
+def shard_scan_kernel(
+    shard_count, a_ref, b_ref, out_ref, own_a, own_b, sent_a, sent_b, got_a, got_b, send_sems, recv_sems
+):
+    me = lax.axis_index("seq")
+    hg_me = lax.axis_index("hg")
+    head_count = a_ref.shape[0]
+    plan = scan_plan(shard_count)
+    distances = sorted({d for round_plan in plan for d, _ in round_plan})
+    barrier = pltpu.get_barrier_semaphore()
+    for distance in distances:
+        for target in (lax.rem(me + distance, shard_count), lax.rem(me + shard_count - distance, shard_count)):
+            pl.semaphore_signal(barrier, inc=1, device_id=(target, hg_me), device_id_type=MESH)
+    pl.semaphore_wait(barrier, 2 * len(distances))
+    own_a[...] = a_ref[...]
+    own_b[...] = b_ref[...]
+    eye = jnp.eye(a_ref.shape[1], dtype=jnp.float32)
+    slot = 0
+    copy_index = 0
+    result = jnp.zeros(out_ref.shape, jnp.float32)
+    for round_index, round_plan in enumerate(plan):
+        last = round_index == len(plan) - 1
+        sent_a[round_index] = own_a[...].astype(sent_a.dtype)
+        sent_b[round_index] = own_b[...].astype(sent_b.dtype)
+        copies = []
+        slots = []
+        for distance, send_a in round_plan:
+            target = (lax.rem(me + distance, shard_count), hg_me)
+            pair = [(sent_b, got_b)] + ([(sent_a, got_a)] if send_a else [])
+            for source, landing in pair:
+                copies.append(
+                    pltpu.make_async_remote_copy(
+                        src_ref=source.at[round_index],
+                        dst_ref=landing.at[slot],
+                        send_sem=send_sems.at[copy_index],
+                        recv_sem=recv_sems.at[copy_index],
+                        device_id=target,
+                        device_id_type=MESH,
+                    )
+                )
+                copy_index += 1
+            slots.append(slot)
+            slot += 1
+        for copy in copies:
+            copy.start()
+        for copy in copies:
+            copy.wait()
+        for head in range(head_count):
+            acc_a = None
+            acc_b = None
+            for (distance, send_a), got in reversed(list(zip(round_plan, slots))):
+                valid = me >= distance
+                in_b = got_b[got, head].astype(jnp.float32)
+                in_a = got_a[got, head].astype(jnp.float32) if send_a else None
+                if acc_b is None:
+                    acc_b = jnp.where(valid, in_b, 0.0)
+                    if not last:
+                        acc_a = jnp.where(valid, in_a, eye)
+                    continue
+                joined_b = jnp.dot(in_a, acc_b, precision=highest, preferred_element_type=jnp.float32) + in_b
+                acc_b = jnp.where(valid, joined_b, acc_b)
+                if not last:
+                    joined_a = jnp.dot(in_a, acc_a, precision=highest, preferred_element_type=jnp.float32)
+                    acc_a = jnp.where(valid, joined_a, acc_a)
+            if round_index > 0:
+                mine_a = own_a[head]
+                acc_b = jnp.dot(mine_a, acc_b, precision=highest, preferred_element_type=jnp.float32) + own_b[head]
+                if not last:
+                    acc_a = jnp.dot(mine_a, acc_a, precision=highest, preferred_element_type=jnp.float32)
+            if last:
+                out_ref[head] = acc_b
+            else:
+                own_a[head] = acc_a
+                own_b[head] = acc_b
+
+
+def shard_scan(shard_a, shard_b, shard_count):
+    plan = scan_plan(shard_count)
+    if not plan:
+        return jnp.zeros(shard_b.shape, jnp.float32)
+    slots = sum(len(round_plan) for round_plan in plan)
+    copies = sum(1 + int(send_a) for round_plan in plan for _, send_a in round_plan)
+    return pl.pallas_call(
+        functools.partial(shard_scan_kernel, shard_count),
+        out_shape=jax.ShapeDtypeStruct(shard_b.shape, jnp.float32),
+        in_specs=[pl.BlockSpec(memory_space=pltpu.VMEM)] * 2,
+        out_specs=pl.BlockSpec(memory_space=pltpu.VMEM),
+        scratch_shapes=[
+            pltpu.VMEM(shard_a.shape, jnp.float32),
+            pltpu.VMEM(shard_b.shape, jnp.float32),
+            pltpu.VMEM((len(plan),) + shard_a.shape, jnp.bfloat16),
+            pltpu.VMEM((len(plan),) + shard_b.shape, jnp.bfloat16),
+            pltpu.VMEM((slots,) + shard_a.shape, jnp.bfloat16),
+            pltpu.VMEM((slots,) + shard_b.shape, jnp.bfloat16),
+            pltpu.SemaphoreType.DMA((copies,)),
+            pltpu.SemaphoreType.DMA((copies,)),
+        ],
+        compiler_params=pltpu.CompilerParams(collective_id=1, has_side_effects=True),
+    )(shard_a, shard_b)
+
+
 def group_sum_kernel(group_count, part_ref, out_ref, landed, send_sems, recv_sems, own_sem):
     me = lax.axis_index("hg")
     seq_me = lax.axis_index("seq")
@@ -210,6 +326,8 @@
 
 
 def group_sum(part, group_count):
+    if group_count == 1:
+        return part
     rows = part.shape[0] // group_count
     cols = part.shape[1]
     return pl.pallas_call(
@@ -292,24 +410,7 @@
         compose, (identity, empty_state), terms, unroll=True
     )
 
-    shard_count = lax.axis_size("seq")
-    shard_index = lax.axis_index("seq")
-    acc_a, acc_b = shard_a, shard_b
-    distance = 1
-    while distance < shard_count:
-        has_prev = shard_index >= distance
-        prev_b = passed_along(acc_b, "seq", distance)
-        new_b = jnp.where(has_prev, apply_shard(acc_a, prev_b, acc_b), acc_b)
-        if 2 * distance < shard_count:
-            prev_a = passed_along(acc_a, "seq", distance)
-            acc_a = jnp.where(
-                has_prev,
-                jnp.einsum("hde,hef->hdf", acc_a, prev_a, precision=highest),
-                acc_a,
-            )
-        acc_b = new_b
-        distance *= 2
-    state_in = passed_along(acc_b, "seq", 1)
+    state_in = shard_scan(shard_a, shard_b, lax.axis_size("seq"))
     produced = local_mix + jnp.einsum("jhsd,hde->jhse", entry_map, state_in, precision=highest)
     produced = produced.transpose(0, 2, 1, 3).reshape(tok_rows, head_count, DV)
     gated = gated_output(produced, zgate, norm_gain)

time: 152 us -> 135 us (0.89)
  the two profiles are of different devices: /device:TPU:17 before, /device:TPU:1 now
where the time goes in v6:
time: 135 us; the launch traced here: 134 us
  Pallas kernels  70.9 us (53%)
  matrix products  41.4 us (31%)
  local copies, waits for them, and re-layouts  10.3 us (8%)
  other arithmetic  6.79 us (5%)
  starting transfers between devices  3.94 us (3%)
    pallas_call x1, Pallas kernels, shard_scan(): pl.pallas_call(functools.partial(shard_scan_kernel, shard_count), out_sha...  44.1 us
    pallas_call x1, Pallas kernels, group_sum(): pl.pallas_call(functools.partial(group_sum_kernel, group_count), out_shap...  26.9 us
    dot_general x1, matrix products, on_device(): jnp.dot(gated, w_out, preferred_element_type=jnp.float32)  5.39 us
    dot_general x6, matrix products, compose(): jnp.einsum('hsd,hde->hse', step_carry, prefix_a, precision=highest)  5.39 us
    ppermute x1, starting transfers between devices, passed_along(): return lax.ppermute(block, axis, route)  3.94 us
    unnamed x51, local copies, waits for them, and re-layouts  3.84 us
    dot_general x5, matrix products, unit_lower_inverse(): jnp.einsum('...st,...tu->...su', step, inverse, precision=highest)  3.44 us
  transfers between devices with their start and end apart: 1, of which 0 were waited for; matrix products, arithmetic and copies ran while one was open for 4% of the time, Pallas kernels for 0%

profile of v6, /device:TPU:1, one launch (start us, length us, event | category | flops | bytes accessed | tf_op | source)
XLA Modules:
  0.0 134.1 jit_solution(2826318713101842862)
XLA Ops:
  0.0 2.4 %fusion.98 = (f32[384,256]{1,0:T(8,128)S(1)}, bf16[384,256]{1,0:T(8,128)(2,1)S(1)}) fusion(bf16[384,2048]{1,0:T(8,128)(2,1)} %param.21, bf16[2048,256]{1,0:T(8,128)(2,1)} %param.23), kind=kOutput, calls=%fused_computation.210 | convolution fusion | flops 402849792 | bytes 3211264 | tf_op jit(solution)/shard_map/dot_general | solution.py:32
  2.5 0.6 copy-done.21
  3.0 1.9 %fusion.100 = (f32[384,512]{1,0:T(8,128)}, bf16[384,512]{1,0:T(8,128)(2,1)S(1)}) fusion(bf16[384,2048]{1,0:T(8,128)(2,1)S(1)} %copy-done.1, bf16[2048,512]{1,0:T(8,128)(2,1)S(1)} %copy-done.21), kind=kOutput, calls=%fused_computation.212 | convolution fusion | flops 805699584 | bytes 4849664 | tf_op jit(solution)/shard_map/dot_general | solution.py:33
  5.0 0.6 fusion.99
  5.6 3.9 %collective-permute-start = (bf16[3,1024]{1,0:T(4,128)(2,1)S(1)}, bf16[3,1024]{1,0:T(4,128)(2,1)S(1)}, u32[]{:S(2)}, u32[]{:S(2)}) collective-permute-start(bf16[3,1024]{1,0:T(4,128)(2,1)S(1)} %pad_maximum_fusion.3), channel_id=1, source_target_pairs={{0,8},{8,16},{16,24},{24,32},{32,40},{40,48},{48,56},{56,64},{64,7... | collective-permute-start | bytes 18440 | tf_op jit(solution)/shard_map/ppermute | solution.py:27
  9.7 0.5 fusion.94
  10.3 1.9 %fusion.24 = f32[384,4]{0,1:T(4,128)S(1)} fusion(bf16[384,2048]{1,0:T(8,128)(2,1)} %param.21, bf16[2048,4]{0,1:T(4,128)(2,1)S(1)} %copy-done.15), kind=kOutput, calls=%fused_computation.61 | convolution fusion | flops 6296064 | bytes 1595392 | tf_op jit(solution)/shard_map/dot_general | solution.py:86
  12.4 1.6 %reduce_window_sum.11 = f32[6,4,64]{2,1,0:T(4,128)S(1)} reduce-window(f32[6,4,64]{2,1,0:T(4,128)S(1)} %copy.69, f32[]{:T(128)} %constant.16.clone.1), window={size=1x1x64 pad=0_0x0_0x63_0}, to_apply=%region_0.1 | reduce-window | flops 96768 | bytes 12292 | tf_op jit(solution)/shard_map/jit(cumsum)/reduce_window_sum | solution.py:115
  14.5 1.2 divide_multiply_fusion.1
  15.7 1.2 reshape.82
  16.9 0.5 multiply_reduce_fusion.1
  18.2 0.5 multiply_reduce_fusion.2
  19.4 1.7 %convolution_multiply_fusion.1 = f32[6,4,64,64]{3,2,1,0:T(8,128)} fusion(f32[6,4,64,128]{3,2,0,1:T(8,128)S(1)} %bitcast.282, f32[6,64,4,128]{3,1,0,2:T(8,128)S(1)} %bitcast.280, f32[6,4,64]{2,1,0:T(4,128)S(1)} %reduce_window_sum.11, pred[64,64]{1,0:T(8,128)(4,1)S(1)} %get-tuple-element.36), kind=kOutput, calls=%fused_computation.13 | convolution fusion | flops 75890688 | bytes 1976320 | tf_op jit(solution)/shard_map/...sd,...td->...st/dot_general | solution.py:134
  21.1 0.8 multiply_subtract_fusion.1
  21.9 0.5 fusion.49
  22.4 0.5 convolution_subtract_fusion.4
  23.2 0.5 fusion.47
  23.7 0.5 convolution_subtract_fusion.3
  24.4 0.5 fusion.45
  24.9 0.5 convolution_subtract_fusion.2
  25.7 0.5 fusion.43
  26.2 0.5 convolution_subtract_fusion.1
  26.9 0.5 fusion.41
  27.4 1.4 %convolution_subtract_fusion = f32[6,4,64,64]{3,2,1,0:T(8,128)} fusion(f32[6,4,64,64]{3,2,1,0:T(8,128)S(1)} %convolution_subtract_fusion.1, f32[6,4,64,64]{3,2,1,0:T(8,128)S(1)} %fusion.41), kind=kOutput, calls=%fused_computation.2 | convolution fusion | flops 37847040 | bytes 1179648 | tf_op jit(solution)/shard_map/...st,...tu->...su/dot_general | solution.py:108
  28.8 1.4 %divide_multiply_fusion = f32[384,512]{1,0:T(8,128)} fusion(f32[384,512]{1,0:T(8,128)S(1)} %copy-done.8, f32[3,512]{1,0:T(4,128)S(1)} %slice_convert_fusion, f32[512]{0:T(512)S(1)} %bitcast.294, f32[512]{0:T(512)S(1)} %bitcast.295, f32[512]{0:T(512)S(1)} %bitcast.293, f32[512]{0:T(512)S(1)} %bitcast.292), kind=kLoop, calls=%fused_computation.83 | loop fusion | flops 2752512 | bytes 1587200 | tf_op jit(solution)/shard_map/jit(silu)/mul | solution.py:44
  30.2 2.3 %reshape_reshape.11 = f32[6,64,4,128]{3,2,1,0:T(4,128)} reshape(f32[384,512]{1,0:T(8,128)} %divide_multiply_fusion) | data formatting | bytes 1572864 | tf_op jit(solution)/shard_map/reshape;reshape | solution.py:92
  32.5 2.0 %fusion.36 = f32[6,4,64,128]{3,2,1,0:T(8,128)S(1)} fusion(f32[6,4,64,64]{3,2,1,0:T(8,128)} %convolution_subtract_fusion, f32[6,64,4,128]{3,2,1,0:T(4,128)} %reshape_reshape.11, f32[6,4,64]{2,1,0:T(4,128)S(1)} %bitcast.290), kind=kOutput, calls=%fused_computation.76 | convolution fusion | flops 75694080 | bytes 1972224 | tf_op jit(solution)/shard_map/...st,...td->...sd/dot_general | solution.py:131
  34.6 0.5 broadcast_multiply_fusion
  35.1 0.6 copy-done.5
  35.7 0.5 fusion.39
  36.2 0.7 fusion.101
  36.9 1.4 %fusion.51 = f32[6,4,128,128]{3,2,1,0:T(8,128)S(1)} fusion(f32[6,4,64,128]{3,2,1,0:T(8,128)S(1)} %fusion.36, f32[6,4,64,128]{3,2,0,1:T(8,128)S(1)} %get-tuple-element.5), kind=kOutput, calls=%fused_computation.96 | convolution fusion | flops 150994944 | bytes 3145728 | tf_op jit(solution)/shard_map/...sd,...se->...de/dot_general | solution.py:140
  38.4 0.5 convolution_subtract_fusion.5
  39.1 0.9 fusion.9
  39.9 1.5 %multiply_subtract_fusion = f32[6,4,128,128]{3,2,1,0:T(8,128)S(1)} fusion(f32[6,4,64,128]{3,2,1,0:T(8,128)S(1)} %fusion.39, f32[128,128]{1,0:T(8,128)S(1)} %fusion.92, f32[6,4]{1,0:T(8,128)S(1)} %copy.81, f32[6,4,64,128]{3,2,0,1:T(8,128)S(1)} %get-tuple-element.5), kind=kOutput, calls=%fused_computation.1 | convolution fusion | flops 151781376 | bytes 3211360 | tf_op jit(solution)/shard_map/...sd,...se->...de/dot_general | solution.py:137
  44.1 1.0 convolution_add_fusion.b_ref
  45.7 0.9 fusion.8
  46.9 0.9 fusion.7
  48.0 0.9 fusion.6
  49.2 0.9 fusion.5
  50.1 1.0 fusion.87.a_ref
  51.1 0.9 fusion.4
  52.0 44.1 %shard_map.199 = f32[4,128,128]{2,1,0:T(8,128)} custom-call(f32[4,128,128]{2,1,0:T(8,128)} %fusion.87.a_ref, f32[4,128,128]{2,1,0:T(8,128)} %convolution_add_fusion.b_ref), custom_call_target="tpu_custom_call" | custom-call | tf_op jit(solution)/shard_map/pallas_call | solution.py:264
  96.1 2.1 %multiply_reduce_fusion = (f32[6,64,4]{1,2,0:T(4,128)S(1)}, f32[6,64,4,128]{3,1,2,0:T(8,128)S(1)}) fusion(f32[6,4,64,128]{3,2,1,0:T(8,128)} %copy-done.6, f32[6,4,64,128]{3,2,1,0:T(8,128)} %fusion.4, f32[4,128,128]{2,1,0:T(8,128)} %shard_map.199), kind=kOutput, calls=%fused_computation.82 | convolution fusion | flops 151583232 | bytes 2627584 | tf_op jit(solution)/shard_map/jhsd,hde->jhse/dot_general | solution.py:414
  98.3 1.4 %copy.86 = f32[6,64,4,128]{3,2,1,0:T(4,128)} copy(f32[6,64,4,128]{3,1,2,0:T(8,128)S(1)} %get-tuple-element.32) | data formatting | bytes 1572864 | tf_op jit(solution)/shard_map/transpose | solution.py:415
  100.2 5.4 %convolution_convert_fusion.part_ref = bf16[384,2048]{1,0:T(8,128)(2,1)} fusion(bf16[512,2048]{1,0:T(8,128)(2,1)S(1)} %copy-done, f32[48,8,4,128]{3,2,1,0:T(4,128)S(1)} %bitcast.286, f32[48,8,4,128]{3,2,1,0:T(4,128)} %bitcast.285, bf16[384,2048]{1,0:T(8,128)(2,1)} %param.21, bf16[2048,512]{1,0:T(8,128)(2,1)} %param.25, f32[512]{0:T(512)S(1)} %broadcast_bitcast_fusion), kind=kOutput, calls=%fused_computation | convolution fusion | flops 1613365248 | bytes 8914944 | tf_op jit(solution)/shard_map/dot_general | solution.py:417
  105.6 26.9 %shard_map.200 = bf16[48,2048]{1,0:T(8,128)(2,1)} custom-call(bf16[384,2048]{1,0:T(8,128)(2,1)} %convolution_convert_fusion.part_ref), custom_call_target="tpu_custom_call" | custom-call | tf_op jit(solution)/shard_map/pallas_call | solution.py:333
  132.5 1.6 %copy.134 = bf16[48,2048]{1,0:T(8,128)(2,1)} copy(bf16[48,2048]{1,0:T(8,128)(2,1)} %shard_map.200) | data formatting | bytes 393216
  (103 shorter events, 7.9 us)
Async XLA Ops:
  0.0 100.2 %copy-start = (bf16[512,2048]{1,0:T(8,128)(2,1)S(1)}, bf16[512,2048]{1,0:T(8,128)(2,1)}, u32[]{:S(2)}) copy-start(bf16[512,2048]{1,0:T(8,128)(2,1)} %param.34) | copy-start | bytes 6291460
  0.0 2.4 %copy-start.1 = (bf16[384,2048]{1,0:T(8,128)(2,1)S(1)}, bf16[384,2048]{1,0:T(8,128)(2,1)}, u32[]{:S(2)}) copy-start(bf16[384,2048]{1,0:T(8,128)(2,1)} %param.21) | copy-start | bytes 4718596
  0.0 3.0 %copy-start.21 = (bf16[2048,512]{1,0:T(8,128)(2,1)S(1)}, bf16[2048,512]{1,0:T(8,128)(2,1)}, u32[]{:S(2)}) copy-start(bf16[2048,512]{1,0:T(8,128)(2,1)} %param.24) | copy-start | bytes 6291460
  3.0 1.9 %copy-start.7 = (bf16[2048,256]{1,0:T(8,128)(2,1)S(1)}, bf16[2048,256]{1,0:T(8,128)(2,1)}, u32[]{:S(2)}) copy-start(bf16[2048,256]{1,0:T(8,128)(2,1)} %param.22) | copy-start | bytes 3145732
  4.9 4.7 %copy-start.17 = (bf16[4,256]{1,0:T(4,128)(2,1)S(1)}, bf16[4,256]{1,0:T(4,128)(2,1)}, u32[]{:S(2)}) copy-start(bf16[4,256]{1,0:T(4,128)(2,1)} %param.29) | copy-start | bytes 6148
  4.9 4.7 %copy-start.18 = (bf16[4,256]{1,0:T(4,128)(2,1)S(1)}, bf16[4,256]{1,0:T(4,128)(2,1)}, u32[]{:S(2)}) copy-start(bf16[4,256]{1,0:T(4,128)(2,1)} %param.28) | copy-start | bytes 6148
  4.9 4.7 %copy-start.22 = (f32[4]{0:T(128)S(1)}, f32[4]{0:T(128)}, u32[]{:S(2)}) copy-start(f32[4]{0:T(128)} %param.31) | copy-start | bytes 52
  4.9 4.7 %copy-start.14 = (bf16[2048,4]{0,1:T(4,128)(2,1)S(1)}, bf16[2048,4]{0,1:T(4,128)(2,1)}, u32[]{:S(2)}) copy-start(bf16[2048,4]{0,1:T(4,128)(2,1)} %param.26) | copy-start | bytes 49156
  5.0 4.7 %copy-start.19 = (f32[4]{0:T(128)S(1)}, f32[4]{0:T(128)}, u32[]{:S(2)}) copy-start(f32[4]{0:T(128)} %param.32) | copy-start | bytes 52
  5.6 4.8 %copy-start.15 = (bf16[2048,4]{0,1:T(4,128)(2,1)S(1)}, bf16[2048,4]{0,1:T(4,128)(2,1)}, u32[]{:S(2)}) copy-start(bf16[2048,4]{0,1:T(4,128)(2,1)} %param.27) | copy-start | bytes 49156
  5.6 8.9 %collective-permute-start = (bf16[3,1024]{1,0:T(4,128)(2,1)S(1)}, bf16[3,1024]{1,0:T(4,128)(2,1)S(1)}, u32[]{:S(2)}, u32[]{:S(2)}) collective-permute-start(bf16[3,1024]{1,0:T(4,128)(2,1)S(1)} %pad_maximum_fusion.3), channel_id=1, source_target_pairs={{0,8},{8,16},{16,24},{24,32},{32,40},{40,48},{48,56},{56,64},{64,7... | collective-permute-start | bytes 18440 | tf_op jit(solution)/shard_map/ppermute | solution.py:27
  9.7 2.7 %copy-start.16 = (bf16[4,512]{1,0:T(4,128)(2,1)S(1)}, bf16[4,512]{1,0:T(4,128)(2,1)}, u32[]{:S(2)}) copy-start(bf16[4,512]{1,0:T(4,128)(2,1)} %param.30) | copy-start | bytes 12292
  9.7 4.7 %copy-start.20 = (f32[128]{0:T(128)S(1)}, f32[128]{0:T(128)}, u32[]{:S(2)}) copy-start(f32[128]{0:T(128)} %param.33) | copy-start | bytes 1540
  19.3 1.8 %copy-start.3 = (f32[384,2,2,128]{3,0,2,1:T(8,128)}, f32[384,2,2,128]{3,0,2,1:T(8,128)S(1)}, u32[]{:S(2)}) copy-start(f32[384,2,2,128]{3,0,2,1:T(8,128)S(1)} %broadcast_in_dim.101) | copy-start | bytes 2359300
  19.3 1.8 %copy-start.23 = (f32[64,64]{1,0:T(8,128)S(1)}, f32[64,64]{1,0:T(8,128)}, u32[]{:S(2)}) copy-start(f32[64,64]{1,0:T(8,128)} %constant.39.clone) | copy-start | bytes 49156
  19.3 1.8 %copy-start.24 = (f32[64,64]{1,0:T(8,128)S(1)}, f32[64,64]{1,0:T(8,128)}, u32[]{:S(2)}) copy-start(f32[64,64]{1,0:T(8,128)} %constant.40.clone) | copy-start | bytes 49156
  21.0 0.8 copy-start.13
  22.4 0.8 copy-start.12
  23.6 0.8 copy-start.11
  24.9 0.8 copy-start.10
  26.2 0.8 copy-start.9
  27.4 1.4 %copy-start.8 = (f32[384,512]{1,0:T(8,128)S(1)}, f32[384,512]{1,0:T(8,128)}, u32[]{:S(2)}) copy-start(f32[384,512]{1,0:T(8,128)} %get-tuple-element.29) | copy-start | bytes 2359300
  32.5 2.1 %copy-start.4 = (f32[384,2,2,128]{3,0,2,1:T(8,128)S(1)}, f32[384,2,2,128]{3,0,2,1:T(8,128)}, u32[]{:S(2)}) copy-start(f32[384,2,2,128]{3,0,2,1:T(8,128)} %copy-done.3) | copy-start | bytes 2359300
  34.6 1.1 copy-start.5
  35.0 1.2 copy-start.2
  45.4 2.7 %copy-start.6 = (f32[6,4,64,128]{3,2,1,0:T(8,128)}, f32[6,4,64,128]{3,2,1,0:T(8,128)S(1)}, u32[]{:S(2)}) copy-start(f32[6,4,64,128]{3,2,1,0:T(8,128)S(1)} %fusion.11) | copy-start | bytes 2359300

commit v7 on v5

--- a/solution.py
+++ b/solution.py
@@ -267,6 +267,88 @@
     )(shard_a, shard_b)
 
 
+def span_kernel(q_ref, k_ref, v_ref, gc_ref, gr_ref, bc_ref, trans_ref, written_ref, carry_ref, local_ref):
+    queries = q_ref[...]
+    key_vecs = k_ref[...]
+    values = v_ref[...]
+    decay_col = gc_ref[...]
+    decay_row = gr_ref[...]
+    rate = bc_ref[...]
+    block_len = queries.shape[1]
+    row_ids = lax.broadcasted_iota(jnp.int32, (1, block_len, block_len), 1)
+    col_ids = lax.broadcasted_iota(jnp.int32, (1, block_len, block_len), 2)
+    inclusive = row_ids >= col_ids
+    strict = row_ids > col_ids
+    cum_col = jnp.sum(jnp.where(inclusive, decay_row, 0.0), axis=2, keepdims=True)
+    cum_row = jnp.sum(jnp.where(row_ids <= col_ids, decay_col, 0.0), axis=1, keepdims=True)
+    gap_mat = cum_col - cum_row
+    falloff = jnp.where(inclusive, jnp.exp(jnp.where(inclusive, gap_mat, 0.0)), 0.0)
+    key_dots = jnp.einsum("bsd,btd->bst", key_vecs, key_vecs, precision=highest,
+                          preferred_element_type=jnp.float32)
+    lower_part = jnp.where(strict, rate * falloff * key_dots, 0.0)
+    inverse = jnp.where((row_ids // 2 == col_ids // 2) & strict, -lower_part, 0.0) + jnp.where(
+        row_ids == col_ids, 1.0, 0.0
+    )
+    size = 2
+    while size < block_len:
+        band = (row_ids // (2 * size) == col_ids // (2 * size)) & (row_ids // size != col_ids // size)
+        off_blocks = jnp.where(band, lower_part, 0.0)
+        step = jnp.einsum("bst,btu->bsu", inverse, off_blocks, precision=highest,
+                          preferred_element_type=jnp.float32)
+        inverse = inverse - jnp.einsum("bst,btu->bsu", step, inverse, precision=highest,
+                                       preferred_element_type=jnp.float32)
+        size *= 2
+    grow = jnp.exp(cum_col)
+    wy_keys = jnp.einsum("bst,btd->bsd", inverse, (rate * grow) * key_vecs, precision=highest,
+                         preferred_element_type=jnp.float32)
+    wy_values = jnp.einsum("bst,btd->bsd", inverse, rate * values, precision=highest,
+                           preferred_element_type=jnp.float32)
+    scores = falloff * jnp.einsum("bsd,btd->bst", queries, key_vecs, precision=highest,
+                                  preferred_element_type=jnp.float32)
+    last = cum_row[:, :, block_len - 1 :]
+    tail_keys_t = jnp.swapaxes(jnp.exp(last - cum_col) * key_vecs, 1, 2)
+    width = key_vecs.shape[2]
+    eye_rows = lax.broadcasted_iota(jnp.int32, (1, width, width), 1)
+    eye_cols = lax.broadcasted_iota(jnp.int32, (1, width, width), 2)
+    trans_ref[...] = jnp.where(eye_rows == eye_cols, jnp.exp(last), 0.0) - jnp.einsum(
+        "bds,bse->bde", tail_keys_t, wy_keys, precision=highest, preferred_element_type=jnp.float32
+    )
+    written_ref[...] = jnp.einsum("bds,bse->bde", tail_keys_t, wy_values, precision=highest,
+                                  preferred_element_type=jnp.float32)
+    carry_ref[...] = grow * queries - jnp.einsum("bst,btd->bsd", scores, wy_keys, precision=highest,
+                                                 preferred_element_type=jnp.float32)
+    local_ref[...] = jnp.einsum("bst,bte->bse", scores, wy_values, precision=highest,
+                                preferred_element_type=jnp.float32)
+
+
+def span_terms_kernel(queries, key_vecs, values, log_decay, write_rate):
+    lead = queries.shape[:2]
+    block_len, width = queries.shape[2], queries.shape[3]
+    flat = lambda x: x.reshape((-1,) + x.shape[2:])
+    pairs = lead[0] * lead[1]
+    decay = log_decay.reshape(pairs, block_len)
+    rate = write_rate.reshape(pairs, block_len)
+    outs = pl.pallas_call(
+        span_kernel,
+        out_shape=[
+            jax.ShapeDtypeStruct((pairs, width, width), jnp.float32),
+            jax.ShapeDtypeStruct((pairs, width, values.shape[3]), jnp.float32),
+            jax.ShapeDtypeStruct((pairs, block_len, width), jnp.float32),
+            jax.ShapeDtypeStruct((pairs, block_len, values.shape[3]), jnp.float32),
+        ],
+        in_specs=[pl.BlockSpec(memory_space=pltpu.VMEM)] * 6,
+        out_specs=[pl.BlockSpec(memory_space=pltpu.VMEM)] * 4,
+    )(
+        flat(queries),
+        flat(key_vecs),
+        flat(values),
+        decay[:, :, None],
+        decay[:, None, :],
+        rate[:, :, None],
+    )
+    return tuple(out.reshape(lead + out.shape[1:]) for out in outs)
+
+
 def group_sum_kernel(group_count, part_ref, out_ref, landed, send_sems, recv_sems, own_sem):
     me = lax.axis_index("hg")
     seq_me = lax.axis_index("seq")
@@ -313,6 +395,8 @@
 
 
 def group_sum(part, group_count):
+    if group_count == 1:
+        return part
     rows = part.shape[0] // group_count
     cols = part.shape[1]
     return pl.pallas_call(
@@ -369,7 +453,7 @@
         a_log,
         dt_bias,
     )
-    terms = span_terms(
+    terms = span_terms_kernel(
         to_blocks(queries),
         to_blocks(key_vecs),
         to_blocks(values),

time: 129 us -> 128 us (level)
  matrix products: 41.4 us -> 28.3 us
  Pallas kernels: 65.2 us -> 76.3 us
  local copies, waits for them, and re-layouts: 10.3 us -> 14.2 us
  other arithmetic: 6.79 us -> 3.75 us
    dot_general x18 -> x0, matrix products: 15.1 us -> none  [the longest x5 3.44 us: unit_lower_inverse(): jnp.einsum('...st,...tu->...su', step, inverse, precision=highest)]
    pallas_call x0 -> x1, Pallas kernels: none -> 11.1 us  [span_terms_kernel(): pl.pallas_call(span_kernel, out_shape=[jax.ShapeDtypeStruct((pairs, width...]
    dot_general x6, matrix products: 5.39 us -> 1.44 us  [compose(): jnp.einsum('hsd,hde->hse', step_carry, prefix_a, precision=highest)]
    dot_general x6, matrix products: 1.42 us -> 5.31 us  [compose(): jnp.einsum('hsd,hde->hse', step_carry, prefix_b, precision=highest)]
    dot_general x6, matrix products: 2.32 us -> 5.53 us  [apply_shard(): jnp.einsum('hde,hef->hdf', trans_mat, state_now, precision=highest)]
    another operation x0 -> x2, local copies, waits for them, and re-layouts: none -> 2.44 us  [the longest x1 1.22 us: span_terms_kernel(): rate[:, :, None]]
    dot_general x1, matrix products: 1.88 us -> 4.07 us  [project_inputs(): jnp.dot(hidden_in, w_value, preferred_element_type=jnp.float32)]
    transpose x0 -> x4, local copies, waits for them, and re-layouts: none -> 1.91 us  [to_blocks(): array_3d.reshape(tok_rows // SPAN, SPAN, head_count, -1)]
  transfers between devices with their start and end apart: 1 -> 1, of which waited for: 0 -> 0; matrix products, arithmetic and copies ran while one was open for 4% -> 3% of each run, Pallas kernels for 0% -> 0%
where the time goes in v7:
time: 128 us; the launch traced here: 127 us
  Pallas kernels  76.3 us (60%)
  matrix products  28.3 us (22%)
  local copies, waits for them, and re-layouts  14.2 us (11%)
  starting transfers between devices  3.94 us (3%)
  other arithmetic  3.75 us (3%)
    pallas_call x1, Pallas kernels, shard_scan(): pl.pallas_call(functools.partial(shard_scan_kernel, shard_count), out_sha...  34.6 us
    pallas_call x1, Pallas kernels, group_sum(): pl.pallas_call(functools.partial(group_sum_kernel, group_count), out_shap...  30.6 us
    pallas_call x1, Pallas kernels, span_terms_kernel(): pl.pallas_call(span_kernel, out_shape=[jax.ShapeDtypeStruct((pairs, width...  11.1 us
    dot_general x6, matrix products, apply_shard(): jnp.einsum('hde,hef->hdf', trans_mat, state_now, precision=highest)  5.53 us
    dot_general x1, matrix products, on_device(): jnp.dot(gated, w_out, preferred_element_type=jnp.float32)  5.38 us
    dot_general x6, matrix products, compose(): jnp.einsum('hsd,hde->hse', step_carry, prefix_b, precision=highest)  5.31 us
    dot_general x1, matrix products, project_inputs(): jnp.dot(hidden_in, w_value, preferred_element_type=jnp.float32)  4.07 us
    ppermute x1, starting transfers between devices, passed_along(): return lax.ppermute(block, axis, route)  3.94 us
  transfers between devices with their start and end apart: 1, of which 0 were waited for; matrix products, arithmetic and copies ran while one was open for 3% of the time, Pallas kernels for 0%

profile of v7, /device:TPU:1, one launch (start us, length us, event | category | flops | bytes accessed | tf_op | source)
XLA Modules:
  0.0 127.1 jit_solution(11744522042816498315)
XLA Ops:
  0.0 4.1 %fusion.66 = (f32[384,512]{1,0:T(8,128)}, bf16[384,512]{1,0:T(8,128)(2,1)S(1)}) fusion(bf16[384,2048]{1,0:T(8,128)(2,1)} %param.14, bf16[2048,512]{1,0:T(8,128)(2,1)} %param.17), kind=kOutput, calls=%fused_computation.133 | convolution fusion | flops 805699584 | bytes 4849664 | tf_op jit(solution)/shard_map/dot_general | solution.py:33
  4.1 0.6 fusion.64
  4.7 0.6 copy-done.7
  5.4 0.6 fusion.65
  6.0 3.9 %collective-permute-start = (bf16[3,1024]{1,0:T(4,128)(2,1)S(1)}, bf16[3,1024]{1,0:T(4,128)(2,1)S(1)}, u32[]{:S(2)}, u32[]{:S(2)}) collective-permute-start(bf16[3,1024]{1,0:T(4,128)(2,1)S(1)} %pad_maximum_fusion.3), channel_id=1, source_target_pairs={{0,8},{8,16},{16,24},{24,32},{32,40},{40,48},{48,56},{56,64},{64,7... | collective-permute-start | bytes 18440 | tf_op jit(solution)/shard_map/ppermute | solution.py:27
  10.1 0.5 fusion.23
  10.6 0.5 fusion.60
  11.3 1.2 copy.52.gc_ref
  12.6 1.2 copy.53.bc_ref
  13.8 1.2 divide_multiply_fusion.1
  15.1 1.2 reshape.109
  16.3 0.5 multiply_reduce_fusion.1
  16.8 0.5 broadcast_multiply_fusion
  17.4 0.9 copy.47
  18.5 0.5 multiply_reduce_fusion.2
  19.0 0.5 multiply_multiply_fusion
  19.6 0.9 copy.45
  20.6 0.3 copy-done.9
  20.9 0.5 divide_multiply_fusion
  21.4 1.2 reshape_reshape.11
  22.6 2.2 %copy.48 = f32[6,64,4,128]{3,1,2,0:T(8,128)} copy(f32[6,64,4,128]{3,2,1,0:T(4,128)} %reshape_reshape.11) | data formatting | bytes 1572864 | tf_op jit(solution)/shard_map/reshape;reshape | solution.py:92
  24.7 11.1 %shard_map.136 = (f32[24,128,128]{2,1,0:T(8,128)}, f32[24,128,128]{2,1,0:T(8,128)}, f32[24,64,128]{2,1,0:T(8,128)}, f32[24,64,128]{2,1,0:T(8,128)}) custom-call(f32[24,64,128]{2,1,0:T(8,128)} %bitcast.174, f32[24,64,128]{2,1,0:T(8,128)} %bitcast.173, f32[24,64,128]{2,1,0:T(8,128)} %bitcast.175, f32[24,64,1]{2,1,0:T(8,128)} %copy.52.gc_ref, ...), custom_call_target="tpu_custom_call" | custom-call | tf_op jit(solution)/shard_map/pallas_call | solution.py:331
  35.9 1.4 %convolution_add_fusion.5 = f32[4,128,128]{2,1,0:T(8,128)S(1)} fusion(f32[24,128,128]{2,1,0:T(8,128)} %get-tuple-element.11, f32[24,128,128]{2,1,0:T(8,128)} %get-tuple-element.12), kind=kOutput, calls=%fused_computation.14 | convolution fusion | flops 50397184 | bytes 2097152 | tf_op jit(solution)/shard_map/eval_jaxpr/hde,hef->hdf/dot_general | solution.py:164
  37.3 1.4 %convolution_add_fusion.4 = f32[4,128,128]{2,1,0:T(8,128)S(1)} fusion(f32[24,128,128]{2,1,0:T(8,128)} %get-tuple-element.11, f32[4,128,128]{2,1,0:T(8,128)S(1)} %convolution_add_fusion.5, f32[24,128,128]{2,1,0:T(8,128)} %get-tuple-element.12), kind=kOutput, calls=%fused_computation.13 | convolution fusion | flops 50397184 | bytes 2359296 | tf_op jit(solution)/shard_map/eval_jaxpr/hde,hef->hdf/dot_general | solution.py:164
  38.7 1.2 convolution_add_fusion.3
  39.9 0.3 convolution_add_fusion.2
  40.2 0.3 convolution_add_fusion.1
  40.5 1.0 convolution_add_fusion.b_ref
  41.5 0.3 fusion.55
  41.7 0.3 fusion.67
  42.0 0.3 fusion.68
  42.3 0.3 fusion.69
  42.6 0.3 fusion.70
  42.8 1.0 fusion.71.a_ref
  44.0 0.2 fusion.7
  45.4 0.8 fusion.20
  46.2 0.9 fusion.18
  47.1 0.9 fusion.16
  48.0 0.9 fusion.14
  48.9 0.9 fusion.12
  49.8 0.9 fusion.10
  50.7 34.6 %shard_map.137 = f32[4,128,128]{2,1,0:T(8,128)} custom-call(f32[4,128,128]{2,1,0:T(8,128)} %fusion.71.a_ref, f32[4,128,128]{2,1,0:T(8,128)} %convolution_add_fusion.b_ref), custom_call_target="tpu_custom_call" | custom-call | tf_op jit(solution)/shard_map/pallas_call | solution.py:251
  85.3 2.1 %multiply_reduce_fusion = (f32[6,64,4]{1,2,0:T(4,128)S(1)}, f32[6,64,4,128]{3,1,2,0:T(8,128)S(1)}) fusion(f32[6,4,64,128]{3,2,1,0:T(8,128)} %fusion.10, f32[6,4,64,128]{3,2,1,0:T(8,128)} %copy-done.5, f32[4,128,128]{2,1,0:T(8,128)} %shard_map.137), kind=kOutput, calls=%fused_computation.65 | convolution fusion | flops 151583232 | bytes 2627584 | tf_op jit(solution)/shard_map/jhsd,hde->jhse/dot_general | solution.py:483
  87.6 1.4 %copy.54 = f32[6,64,4,128]{3,2,1,0:T(4,128)} copy(f32[6,64,4,128]{3,1,2,0:T(8,128)S(1)} %get-tuple-element.34) | data formatting | bytes 1572864 | tf_op jit(solution)/shard_map/transpose | solution.py:484
  89.0 0.5 mul.302
  89.4 5.4 %convolution_convert_fusion.part_ref = bf16[384,2048]{1,0:T(8,128)(2,1)} fusion(bf16[512,2048]{1,0:T(8,128)(2,1)S(1)} %copy-done, f32[48,8,4,128]{3,2,1,0:T(4,128)S(1)} %bitcast.177, f32[48,8,4,128]{3,2,1,0:T(4,128)} %bitcast.176, bf16[384,2048]{1,0:T(8,128)(2,1)} %param.14, bf16[2048,512]{1,0:T(8,128)(2,1)} %param.18, f32[512]{0:T(512)S(1)} %broadcast_bitcast_fusion), kind=kOutput, calls=%fused_computation | convolution fusion | flops 1613365248 | bytes 8914944 | tf_op jit(solution)/shard_map/dot_general | solution.py:486
  94.8 30.6 %shard_map.138 = bf16[48,2048]{1,0:T(8,128)(2,1)} custom-call(bf16[384,2048]{1,0:T(8,128)(2,1)} %convolution_convert_fusion.part_ref), custom_call_target="tpu_custom_call" | custom-call | tf_op jit(solution)/shard_map/pallas_call | solution.py:402
  125.4 1.6 %copy.78 = bf16[48,2048]{1,0:T(8,128)(2,1)} copy(bf16[48,2048]{1,0:T(8,128)(2,1)} %shard_map.138) | data formatting | bytes 393216
  (67 shorter events, 2.2 us)
Async XLA Ops:
  0.0 89.4 %copy-start = (bf16[512,2048]{1,0:T(8,128)(2,1)S(1)}, bf16[512,2048]{1,0:T(8,128)(2,1)}, u32[]{:S(2)}) copy-start(bf16[512,2048]{1,0:T(8,128)(2,1)} %param.27) | copy-start | bytes 6291460
  0.0 4.1 %copy-start.2 = (bf16[384,2048]{1,0:T(8,128)(2,1)S(1)}, bf16[384,2048]{1,0:T(8,128)(2,1)}, u32[]{:S(2)}) copy-start(bf16[384,2048]{1,0:T(8,128)(2,1)} %param.14) | copy-start | bytes 4718596
  0.0 4.1 %copy-start.6 = (bf16[2048,256]{1,0:T(8,128)(2,1)S(1)}, bf16[2048,256]{1,0:T(8,128)(2,1)}, u32[]{:S(2)}) copy-start(bf16[2048,256]{1,0:T(8,128)(2,1)} %param.15) | copy-start | bytes 3145732
  4.1 1.2 copy-start.7
  5.3 4.6 %copy-start.14 = (bf16[4,256]{1,0:T(4,128)(2,1)S(1)}, bf16[4,256]{1,0:T(4,128)(2,1)}, u32[]{:S(2)}) copy-start(bf16[4,256]{1,0:T(4,128)(2,1)} %param.21) | copy-start | bytes 6148
  5.3 4.6 %copy-start.15 = (bf16[4,256]{1,0:T(4,128)(2,1)S(1)}, bf16[4,256]{1,0:T(4,128)(2,1)}, u32[]{:S(2)}) copy-start(bf16[4,256]{1,0:T(4,128)(2,1)} %param.22) | copy-start | bytes 6148
  5.3 4.7 %copy-start.13 = (bf16[4,512]{1,0:T(4,128)(2,1)S(1)}, bf16[4,512]{1,0:T(4,128)(2,1)}, u32[]{:S(2)}) copy-start(bf16[4,512]{1,0:T(4,128)(2,1)} %param.23) | copy-start | bytes 12292
  5.3 4.7 %copy-start.18 = (f32[4]{0:T(128)S(1)}, f32[4]{0:T(128)}, u32[]{:S(2)}) copy-start(f32[4]{0:T(128)} %param.24) | copy-start | bytes 52
  5.3 4.7 %copy-start.11 = (bf16[2048,4]{0,1:T(4,128)(2,1)S(1)}, bf16[2048,4]{0,1:T(4,128)(2,1)}, u32[]{:S(2)}) copy-start(bf16[2048,4]{0,1:T(4,128)(2,1)} %param.20) | copy-start | bytes 49156
  5.9 4.7 %copy-start.17 = (f32[128]{0:T(128)S(1)}, f32[128]{0:T(128)}, u32[]{:S(2)}) copy-start(f32[128]{0:T(128)} %param.26) | copy-start | bytes 1540
  5.9 4.7 %copy-start.12 = (bf16[2048,4]{0,1:T(4,128)(2,1)S(1)}, bf16[2048,4]{0,1:T(4,128)(2,1)}, u32[]{:S(2)}) copy-start(bf16[2048,4]{0,1:T(4,128)(2,1)} %param.19) | copy-start | bytes 49156
  6.0 4.7 %copy-start.16 = (f32[4]{0:T(128)S(1)}, f32[4]{0:T(128)}, u32[]{:S(2)}) copy-start(f32[4]{0:T(128)} %param.25) | copy-start | bytes 52
  6.0 7.8 %collective-permute-start = (bf16[3,1024]{1,0:T(4,128)(2,1)S(1)}, bf16[3,1024]{1,0:T(4,128)(2,1)S(1)}, u32[]{:S(2)}, u32[]{:S(2)}) collective-permute-start(bf16[3,1024]{1,0:T(4,128)(2,1)S(1)} %pad_maximum_fusion.3), channel_id=1, source_target_pairs={{0,8},{8,16},{16,24},{24,32},{32,40},{40,48},{48,56},{56,64},{64,7... | collective-permute-start | bytes 18440 | tf_op jit(solution)/shard_map/ppermute | solution.py:27
  11.3 3.8 %copy-start.10 = (f32[6,4,64,1]{2,1,0,3:T(4,128)}, f32[6,4,64,1]{2,1,0,3:T(4,128)S(1)}, u32[]{:S(2)}) copy-start(f32[6,4,64,1]{2,1,0,3:T(4,128)S(1)} %copy.49) | copy-start | bytes 18436
  19.5 1.4 %copy-start.9 = (f32[384,512]{1,0:T(8,128)S(1)}, f32[384,512]{1,0:T(8,128)}, u32[]{:S(2)}) copy-start(f32[384,512]{1,0:T(8,128)} %get-tuple-element.31) | copy-start | bytes 2359300
  35.9 2.8 %copy-start.1 = (f32[24,128,128]{2,1,0:T(8,128)S(1)}, f32[24,128,128]{2,1,0:T(8,128)}, u32[]{:S(2)}) copy-start(f32[24,128,128]{2,1,0:T(8,128)} %get-tuple-element.11) | copy-start | bytes 4718596
  37.3 2.7 %copy-start.4 = (f32[24,128,128]{2,1,0:T(8,128)S(1)}, f32[24,128,128]{2,1,0:T(8,128)}, u32[]{:S(2)}) copy-start(f32[24,128,128]{2,1,0:T(8,128)} %get-tuple-element.12) | copy-start | bytes 4718596
  42.3 1.5 %copy-start.3 = (f32[24,64,128]{2,1,0:T(8,128)S(1)}, f32[24,64,128]{2,1,0:T(8,128)}, u32[]{:S(2)}) copy-start(f32[24,64,128]{2,1,0:T(8,128)} %get-tuple-element.9) | copy-start | bytes 2359300
  44.3 1.1 copy-start.8
  45.3 3.7 %copy-start.5 = (f32[6,4,64,128]{3,2,1,0:T(8,128)}, f32[6,4,64,128]{3,2,1,0:T(8,128)S(1)}, u32[]{:S(2)}) copy-start(f32[6,4,64,128]{3,2,1,0:T(8,128)S(1)} %fusion.3) | copy-start | bytes 2359300

commit v8 on v7

--- a/solution.py
+++ b/solution.py
@@ -267,7 +267,9 @@
     )(shard_a, shard_b)
 
 
-def span_kernel(q_ref, k_ref, v_ref, gc_ref, gr_ref, bc_ref, trans_ref, written_ref, carry_ref, local_ref):
+def span_kernel(
+    head_count, q_ref, k_ref, v_ref, gc_ref, gr_ref, bc_ref, shard_a_ref, shard_b_ref, mix_ref, entry_ref
+):
     queries = q_ref[...]
     key_vecs = k_ref[...]
     values = v_ref[...]
@@ -310,15 +312,35 @@
     width = key_vecs.shape[2]
     eye_rows = lax.broadcasted_iota(jnp.int32, (1, width, width), 1)
     eye_cols = lax.broadcasted_iota(jnp.int32, (1, width, width), 2)
-    trans_ref[...] = jnp.where(eye_rows == eye_cols, jnp.exp(last), 0.0) - jnp.einsum(
+    transition = jnp.where(eye_rows == eye_cols, jnp.exp(last), 0.0) - jnp.einsum(
         "bds,bse->bde", tail_keys_t, wy_keys, precision=highest, preferred_element_type=jnp.float32
     )
-    written_ref[...] = jnp.einsum("bds,bse->bde", tail_keys_t, wy_values, precision=highest,
-                                  preferred_element_type=jnp.float32)
-    carry_ref[...] = grow * queries - jnp.einsum("bst,btd->bsd", scores, wy_keys, precision=highest,
-                                                 preferred_element_type=jnp.float32)
-    local_ref[...] = jnp.einsum("bst,bte->bse", scores, wy_values, precision=highest,
-                                preferred_element_type=jnp.float32)
+    written = jnp.einsum("bds,bse->bde", tail_keys_t, wy_values, precision=highest,
+                         preferred_element_type=jnp.float32)
+    carry_map = grow * queries - jnp.einsum("bst,btd->bsd", scores, wy_keys, precision=highest,
+                                            preferred_element_type=jnp.float32)
+    local_out = jnp.einsum("bst,bte->bse", scores, wy_values, precision=highest,
+                           preferred_element_type=jnp.float32)
+    for span in range(queries.shape[0] // head_count):
+        heads = slice(span * head_count, (span + 1) * head_count)
+        if span == 0:
+            mix_ref[heads] = local_out[heads]
+            entry_ref[heads] = carry_map[heads]
+            prefix_a = transition[heads]
+            prefix_b = written[heads]
+            continue
+        mix_ref[heads] = local_out[heads] + jnp.einsum(
+            "hsd,hde->hse", carry_map[heads], prefix_b, precision=highest,
+            preferred_element_type=jnp.float32)
+        entry_ref[heads] = jnp.einsum("hsd,hde->hse", carry_map[heads], prefix_a, precision=highest,
+                                      preferred_element_type=jnp.float32)
+        prefix_b = written[heads] + jnp.einsum(
+            "hde,hef->hdf", transition[heads], prefix_b, precision=highest,
+            preferred_element_type=jnp.float32)
+        prefix_a = jnp.einsum("hde,hef->hdf", transition[heads], prefix_a, precision=highest,
+                              preferred_element_type=jnp.float32)
+    shard_a_ref[...] = prefix_a
+    shard_b_ref[...] = prefix_b
 
 
 def span_terms_kernel(queries, key_vecs, values, log_decay, write_rate):
@@ -328,13 +350,13 @@
     pairs = lead[0] * lead[1]
     decay = log_decay.reshape(pairs, block_len)
     rate = write_rate.reshape(pairs, block_len)
-    outs = pl.pallas_call(
-        span_kernel,
+    shard_a, shard_b, local_mix, entry_map = pl.pallas_call(
+        functools.partial(span_kernel, lead[1]),
         out_shape=[
-            jax.ShapeDtypeStruct((pairs, width, width), jnp.float32),
-            jax.ShapeDtypeStruct((pairs, width, values.shape[3]), jnp.float32),
+            jax.ShapeDtypeStruct((lead[1], width, width), jnp.float32),
+            jax.ShapeDtypeStruct((lead[1], width, values.shape[3]), jnp.float32),
+            jax.ShapeDtypeStruct((pairs, block_len, values.shape[3]), jnp.float32),
             jax.ShapeDtypeStruct((pairs, block_len, width), jnp.float32),
-            jax.ShapeDtypeStruct((pairs, block_len, values.shape[3]), jnp.float32),
         ],
         in_specs=[pl.BlockSpec(memory_space=pltpu.VMEM)] * 6,
         out_specs=[pl.BlockSpec(memory_space=pltpu.VMEM)] * 4,
@@ -346,7 +368,12 @@
         decay[:, None, :],
         rate[:, :, None],
     )
-    return tuple(out.reshape(lead + out.shape[1:]) for out in outs)
+    return (
+        shard_a,
+        shard_b,
+        local_mix.reshape(lead + local_mix.shape[1:]),
+        entry_map.reshape(lead + entry_map.shape[1:]),
+    )
 
 
 def group_sum_kernel(group_count, part_ref, out_ref, landed, send_sems, recv_sems, own_sem):
@@ -453,7 +480,7 @@
         a_log,
         dt_bias,
     )
-    terms = span_terms_kernel(
+    shard_a, shard_b, local_mix, entry_map = span_terms_kernel(
         to_blocks(queries),
         to_blocks(key_vecs),
         to_blocks(values),
@@ -461,24 +488,6 @@
         to_blocks(write_rate[..., None])[..., 0],
     )
     head_count = values.shape[1]
-    identity = jnp.broadcast_to(jnp.eye(DK, dtype=jnp.float32), (head_count, DK, DK))
-    empty_state = jnp.zeros((head_count, DK, DV), jnp.float32)
-
-    def compose(carried, per_span):
-        prefix_a, prefix_b = carried
-        step_trans, step_written, step_carry, step_local = per_span
-        local_mix = (
-            jnp.einsum("hsd,hde->hse", step_carry, prefix_b, precision=highest) + step_local
-        )
-        entry_map = jnp.einsum("hsd,hde->hse", step_carry, prefix_a, precision=highest)
-        new_a = jnp.einsum("hde,hef->hdf", step_trans, prefix_a, precision=highest)
-        new_b = apply_shard(step_trans, prefix_b, step_written)
-        return ((new_a, new_b), (local_mix, entry_map))
-
-    (shard_a, shard_b), (local_mix, entry_map) = lax.scan(
-        compose, (identity, empty_state), terms, unroll=True
-    )
-
     state_in = shard_scan(shard_a, shard_b, lax.axis_size("seq"))
     produced = local_mix + jnp.einsum("jhsd,hde->jhse", entry_map, state_in, precision=highest)
     produced = produced.transpose(0, 2, 1, 3).reshape(tok_rows, head_count, DV)

time: 128 us -> 115 us (0.90)
  matrix products: 28.3 us -> 13.8 us
  Pallas kernels: 76.3 us -> 78.5 us
    dot_general x24 -> x0, matrix products: 14.6 us -> none  [the longest x6 5.53 us: apply_shard(): jnp.einsum('hde,hef->hdf', trans_mat, state_now, precision=highest)]
    pallas_call x1, Pallas kernels: 11.1 us -> 13.3 us  [span_terms_kernel(): pl.pallas_call(functools.partial(span_kernel, lead[1]), out_shape=[jax.Sh...]
    unnamed x39 -> x29, local copies, waits for them, and re-layouts: 2.8 us -> 2.64 us
where the time goes in v8:
time: 115 us; the launch traced here: 114 us
  Pallas kernels  78.5 us (68%)
  local copies, waits for them, and re-layouts  14.1 us (12%)
  matrix products  13.8 us (12%)
  starting transfers between devices  3.95 us (3%)
  other arithmetic  3.72 us (3%)
    pallas_call x1, Pallas kernels, shard_scan(): pl.pallas_call(functools.partial(shard_scan_kernel, shard_count), out_sha...  34.6 us
    pallas_call x1, Pallas kernels, group_sum(): pl.pallas_call(functools.partial(group_sum_kernel, group_count), out_shap...  30.6 us
    pallas_call x1, Pallas kernels, span_terms_kernel(): pl.pallas_call(functools.partial(span_kernel, lead[1]), out_shape=[jax.Sh...  13.3 us
    dot_general x1, matrix products, on_device(): jnp.dot(gated, w_out, preferred_element_type=jnp.float32)  5.39 us
    dot_general x1, matrix products, project_inputs(): jnp.dot(hidden_in, w_value, preferred_element_type=jnp.float32)  4.09 us
    ppermute x1, starting transfers between devices, passed_along(): return lax.ppermute(block, axis, route)  3.95 us
    another operation x4, local copies, waits for them, and re-layouts, to_blocks(): array_3d.reshape(tok_rows // SPAN, SPAN, head_count, -1)  3.44 us
    unnamed x29, local copies, waits for them, and re-layouts  2.64 us
  transfers between devices with their start and end apart: 1, of which 0 were waited for; matrix products, arithmetic and copies ran while one was open for 3% of the time, Pallas kernels for 0%

profile of v8, /device:TPU:1, one launch (start us, length us, event | category | flops | bytes accessed | tf_op | source)
XLA Modules:
  0.0 114.4 jit_solution(8396634625520073395)
XLA Ops:
  0.0 0.0 copy-start
  0.0 4.1 %fusion.41 = (f32[384,512]{1,0:T(8,128)}, bf16[384,512]{1,0:T(8,128)(2,1)S(1)}) fusion(bf16[384,2048]{1,0:T(8,128)(2,1)} %param.14, bf16[2048,512]{1,0:T(8,128)(2,1)} %param.17), kind=kOutput, calls=%fused_computation.89 | convolution fusion | flops 805699584 | bytes 4849664 | tf_op jit(solution)/shard_map/dot_general | solution.py:33
  4.1 0.0 copy-done.1
  4.1 0.0 copy-done.2
  4.1 0.0 copy-start.3
  4.1 0.6 fusion.39
  4.7 0.6 copy-done.3
  5.4 0.0 copy-start.6
  5.4 0.6 fusion.40
  6.0 0.0 copy-start.7
  6.0 0.0 copy-start.11
  6.0 3.9 %collective-permute-start = (bf16[3,1024]{1,0:T(4,128)(2,1)S(1)}, bf16[3,1024]{1,0:T(4,128)(2,1)S(1)}, u32[]{:S(2)}, u32[]{:S(2)}) collective-permute-start(bf16[3,1024]{1,0:T(4,128)(2,1)S(1)} %pad_maximum_fusion.3), channel_id=1, source_target_pairs={{0,8},{8,16},{16,24},{24,32},{32,40},{40,48},{48,56},{56,64},{64,7... | collective-permute-start | bytes 18440 | tf_op jit(solution)/shard_map/ppermute | solution.py:27
  10.0 0.0 copy-done.9
  10.1 0.0 copy-start.12
  10.1 0.5 fusion.5
  10.6 0.0 copy-done.7
  10.6 0.0 copy-done.11
  10.6 0.5 fusion.37
  11.2 0.1 reshape_broadcast_in_dim.6
  11.3 1.2 %copy.56.gc_ref = f32[24,64,1]{2,1,0:T(8,128)} copy(f32[24,64,1]{1,0,2:T(8,128)S(1)} %bitcast.92) | data formatting | bytes 12288 | tf_op jit(solution)/shard_map/broadcast_in_dim;reshape;squeeze | solution.py:367
  12.5 0.1 reshape_broadcast_in_dim.7
  12.6 1.3 %copy.57.bc_ref = f32[24,64,1]{2,1,0:T(8,128)} copy(f32[24,64,1]{1,0,2:T(8,128)S(1)} %bitcast.96) | data formatting | bytes 12288 | tf_op jit(solution)/shard_map/broadcast_in_dim;reshape;squeeze | solution.py:369
  13.9 0.0 collective-permute-done
  13.9 1.2 %divide_multiply_fusion.1 = (f32[384,256]{1,0:T(8,128)}, f32[384,256]{1,0:T(8,128)S(1)}) fusion(f32[384,256]{1,0:T(8,128)S(1)} %get-tuple-element.29, f32[3,256]{1,0:T(4,128)S(1)} %get-tuple-element.13, f32[256]{0:T(256)S(1)} %bitcast.107, f32[256]{0:T(256)S(1)} %bitcast.108, f32[256]{0:T(256)S(1)} %bitcast.106, f32[256]{0:T(256)S(1)} %bitcast.105, ...), kind=kLoop, calls=%fused_computation.57 | loop fusion | flops 2752512 | bytes 1587200 | tf_op jit(solution)/shard_map/jit(silu)/mul | solution.py:44
  15.1 1.2 %reshape.63 = f32[384,2,128]{2,1,0:T(2,128)S(1)} reshape(f32[384,256]{1,0:T(8,128)} %get-tuple-element.35) | data formatting | bytes 786432 | tf_op jit(solution)/shard_map/reshape | solution.py:74
  16.3 0.5 multiply_reduce_fusion.1
  16.8 0.5 broadcast_multiply_fusion
  17.3 0.1 broadcast_in_dim.5
  17.4 0.9 copy.51
  18.3 0.2 reshape.61
  18.6 0.5 multiply_reduce_fusion.2
  19.1 0.5 multiply_multiply_fusion
  19.6 0.1 broadcast_in_dim.4
  19.7 1.0 copy.49
  20.6 0.3 copy-done.4
  21.0 0.5 divide_multiply_fusion
  21.4 1.1 %reshape_reshape.11 = f32[6,64,4,128]{3,2,1,0:T(4,128)} reshape(f32[384,512]{1,0:T(8,128)S(1)} %divide_multiply_fusion) | data formatting | bytes 1572864 | tf_op jit(solution)/shard_map/reshape;reshape | solution.py:92
  22.6 2.1 %copy.52 = f32[6,64,4,128]{3,1,2,0:T(8,128)} copy(f32[6,64,4,128]{3,2,1,0:T(4,128)} %reshape_reshape.11) | data formatting | bytes 1572864 | tf_op jit(solution)/shard_map/reshape;reshape | solution.py:92
  24.7 13.3 %shard_map.136 = (f32[4,128,128]{2,1,0:T(8,128)}, f32[4,128,128]{2,1,0:T(8,128)}, f32[24,64,128]{2,1,0:T(8,128)}, f32[24,64,128]{2,1,0:T(8,128)}) custom-call(f32[24,64,128]{2,1,0:T(8,128)} %bitcast.85, f32[24,64,128]{2,1,0:T(8,128)} %bitcast.84, f32[24,64,128]{2,1,0:T(8,128)} %bitcast.86, f32[24,64,1]{2,1,0:T(8,128)} %copy.56.gc_ref, ...), custom_call_target="tpu_custom_call" | custom-call | tf_op jit(solution)/shard_map/pallas_call | solution.py:353
  38.1 34.6 %shard_map.137 = f32[4,128,128]{2,1,0:T(8,128)} custom-call(f32[4,128,128]{2,1,0:T(8,128)} %get-tuple-element.10.a_ref, f32[4,128,128]{2,1,0:T(8,128)} %get-tuple-element.11.b_ref), custom_call_target="tpu_custom_call" | custom-call | tf_op jit(solution)/shard_map/pallas_call | solution.py:251
  72.6 2.1 %multiply_reduce_fusion = (f32[6,64,4]{1,0,2:T(8,128)S(1)}, f32[6,64,4,128]{3,1,0,2:T(8,128)S(1)}) fusion(f32[6,4,64,128]{3,2,1,0:T(8,128)} %bitcast.89, f32[4,128,128]{2,1,0:T(8,128)} %shard_map.137, f32[6,4,64,128]{3,2,1,0:T(8,128)} %bitcast.88), kind=kOutput, calls=%fused_computation.30 | convolution fusion | flops 151583232 | bytes 2627584 | tf_op jit(solution)/shard_map/jhsd,hde->jhse/dot_general | solution.py:492
  74.8 0.1 copy.63
  74.9 1.4 %copy.60 = f32[6,64,4,128]{3,2,1,0:T(4,128)} copy(f32[6,64,4,128]{3,1,0,2:T(8,128)S(1)} %get-tuple-element.34) | data formatting | bytes 1572864 | tf_op jit(solution)/shard_map/transpose | solution.py:493
  76.3 0.5 mul.302
  76.8 0.0 copy-done
  76.8 5.4 %convolution_convert_fusion.part_ref = bf16[384,2048]{1,0:T(8,128)(2,1)} fusion(bf16[512,2048]{1,0:T(8,128)(2,1)S(1)} %copy-done, f32[48,8,4,128]{3,2,1,0:T(4,128)S(1)} %bitcast.90, f32[48,8,4,128]{3,2,1,0:T(4,128)} %bitcast.87, bf16[384,2048]{1,0:T(8,128)(2,1)} %param.14, bf16[2048,512]{1,0:T(8,128)(2,1)} %param.18, f32[512]{0:T(512)S(1)} %broadcast_bitcast_fusion), kind=kOutput, calls=%fused_computation | convolution fusion | flops 1613365248 | bytes 8914944 | tf_op jit(solution)/shard_map/dot_general | solution.py:495
  82.2 30.6 %shard_map.138 = bf16[48,2048]{1,0:T(8,128)(2,1)} custom-call(bf16[384,2048]{1,0:T(8,128)(2,1)} %convolution_convert_fusion.part_ref), custom_call_target="tpu_custom_call" | custom-call | tf_op jit(solution)/shard_map/pallas_call | solution.py:429
  112.8 1.6 %copy.78 = bf16[48,2048]{1,0:T(8,128)(2,1)} copy(bf16[48,2048]{1,0:T(8,128)(2,1)} %shard_map.138) | data formatting | bytes 393216
  (32 shorter events, 0.2 us)
Async XLA Ops:
  0.0 76.8 %copy-start = (bf16[512,2048]{1,0:T(8,128)(2,1)S(1)}, bf16[512,2048]{1,0:T(8,128)(2,1)}, u32[]{:S(2)}) copy-start(bf16[512,2048]{1,0:T(8,128)(2,1)} %param.27) | copy-start | bytes 6291460
  0.0 4.1 %copy-start.1 = (bf16[384,2048]{1,0:T(8,128)(2,1)S(1)}, bf16[384,2048]{1,0:T(8,128)(2,1)}, u32[]{:S(2)}) copy-start(bf16[384,2048]{1,0:T(8,128)(2,1)} %param.14) | copy-start | bytes 4718596
  0.0 4.1 %copy-start.2 = (bf16[2048,256]{1,0:T(8,128)(2,1)S(1)}, bf16[2048,256]{1,0:T(8,128)(2,1)}, u32[]{:S(2)}) copy-start(bf16[2048,256]{1,0:T(8,128)(2,1)} %param.15) | copy-start | bytes 3145732
  4.1 1.2 %copy-start.3 = (bf16[2048,256]{1,0:T(8,128)(2,1)S(1)}, bf16[2048,256]{1,0:T(8,128)(2,1)}, u32[]{:S(2)}) copy-start(bf16[2048,256]{1,0:T(8,128)(2,1)} %param.16) | copy-start | bytes 3145732
  5.4 4.6 %copy-start.9 = (bf16[4,256]{1,0:T(4,128)(2,1)S(1)}, bf16[4,256]{1,0:T(4,128)(2,1)}, u32[]{:S(2)}) copy-start(bf16[4,256]{1,0:T(4,128)(2,1)} %param.21) | copy-start | bytes 6148
  5.4 4.6 %copy-start.10 = (bf16[4,256]{1,0:T(4,128)(2,1)S(1)}, bf16[4,256]{1,0:T(4,128)(2,1)}, u32[]{:S(2)}) copy-start(bf16[4,256]{1,0:T(4,128)(2,1)} %param.22) | copy-start | bytes 6148
  5.4 4.7 %copy-start.8 = (bf16[4,512]{1,0:T(4,128)(2,1)S(1)}, bf16[4,512]{1,0:T(4,128)(2,1)}, u32[]{:S(2)}) copy-start(bf16[4,512]{1,0:T(4,128)(2,1)} %param.23) | copy-start | bytes 12292
  5.4 4.7 %copy-start.13 = (f32[4]{0:T(128)S(1)}, f32[4]{0:T(128)}, u32[]{:S(2)}) copy-start(f32[4]{0:T(128)} %param.24) | copy-start | bytes 52
  5.4 4.7 %copy-start.6 = (bf16[2048,4]{0,1:T(4,128)(2,1)S(1)}, bf16[2048,4]{0,1:T(4,128)(2,1)}, u32[]{:S(2)}) copy-start(bf16[2048,4]{0,1:T(4,128)(2,1)} %param.20) | copy-start | bytes 49156
  6.0 4.7 %copy-start.7 = (bf16[2048,4]{0,1:T(4,128)(2,1)S(1)}, bf16[2048,4]{0,1:T(4,128)(2,1)}, u32[]{:S(2)}) copy-start(bf16[2048,4]{0,1:T(4,128)(2,1)} %param.19) | copy-start | bytes 49156
  6.0 4.7 %copy-start.11 = (f32[4]{0:T(128)S(1)}, f32[4]{0:T(128)}, u32[]{:S(2)}) copy-start(f32[4]{0:T(128)} %param.25) | copy-start | bytes 52
  6.0 7.9 %collective-permute-start = (bf16[3,1024]{1,0:T(4,128)(2,1)S(1)}, bf16[3,1024]{1,0:T(4,128)(2,1)S(1)}, u32[]{:S(2)}, u32[]{:S(2)}) collective-permute-start(bf16[3,1024]{1,0:T(4,128)(2,1)S(1)} %pad_maximum_fusion.3), channel_id=1, source_target_pairs={{0,8},{8,16},{16,24},{24,32},{32,40},{40,48},{48,56},{56,64},{64,7... | collective-permute-start | bytes 18440 | tf_op jit(solution)/shard_map/ppermute | solution.py:27
  10.1 1.1 copy-start.12
  11.3 3.8 %copy-start.5 = (f32[6,4,64,1]{2,1,0,3:T(4,128)}, f32[6,4,64,1]{2,1,0,3:T(4,128)S(1)}, u32[]{:S(2)}) copy-start(f32[6,4,64,1]{2,1,0,3:T(4,128)S(1)} %copy.53) | copy-start | bytes 18436
  19.6 1.4 %copy-start.4 = (f32[384,512]{1,0:T(8,128)S(1)}, f32[384,512]{1,0:T(8,128)}, u32[]{:S(2)}) copy-start(f32[384,512]{1,0:T(8,128)} %get-tuple-element.31) | copy-start | bytes 2359300

commit v9 on v8

--- a/solution.py
+++ b/solution.py
@@ -376,7 +376,7 @@
     )
 
 
-def group_sum_kernel(group_count, part_ref, out_ref, landed, send_sems, recv_sems, own_sem):
+def group_sum_kernel(group_count, gated_ref, w_ref, out_ref, outgoing, landed, send_sems, recv_sems):
     me = lax.axis_index("hg")
     seq_me = lax.axis_index("seq")
     rows = out_ref.shape[0]
@@ -385,11 +385,17 @@
         peer = lax.rem(me + step, group_count)
         pl.semaphore_signal(barrier, inc=1, device_id=(seq_me, peer), device_id_type=MESH)
     pl.semaphore_wait(barrier, group_count - 1)
+
+    def term(owner):
+        block = gated_ref[pl.ds(pl.multiple_of(owner * rows, 16), rows), :]
+        return jnp.dot(block, w_ref[...], preferred_element_type=jnp.float32).astype(out_ref.dtype)
+
     sends = []
     for step in range(1, group_count):
         peer = lax.rem(me + step, group_count)
+        outgoing[step] = term(peer)
         copy = pltpu.make_async_remote_copy(
-            src_ref=part_ref.at[pl.ds(pl.multiple_of(peer * rows, 8), rows)],
+            src_ref=outgoing.at[step],
             dst_ref=landed.at[me],
             send_sem=send_sems.at[step],
             recv_sem=recv_sems.at[me],
@@ -398,47 +404,41 @@
         )
         copy.start()
         sends.append(copy)
-    own = pltpu.make_async_copy(
-        part_ref.at[pl.ds(pl.multiple_of(me * rows, 8), rows)], landed.at[me], own_sem
-    )
-    own.start()
-    own.wait()
+    total = term(me).astype(jnp.float32)
     for step in range(1, group_count):
         source = lax.rem(me + group_count - step, group_count)
         pltpu.make_async_remote_copy(
-            src_ref=part_ref.at[pl.ds(0, rows)],
+            src_ref=outgoing.at[step],
             dst_ref=landed.at[source],
             send_sem=send_sems.at[step],
             recv_sem=recv_sems.at[source],
             device_id=(seq_me, source),
             device_id_type=MESH,
         ).wait_recv()
+        total = total + landed[source].astype(jnp.float32)
     for copy in sends:
         copy.wait_send()
-    total = landed[0].astype(jnp.float32)
-    for slot in range(1, group_count):
-        total = total + landed[slot].astype(jnp.float32)
     out_ref[...] = total.astype(out_ref.dtype)
 
 
-def group_sum(part, group_count):
+def group_sum(gated, w_out, group_count):
     if group_count == 1:
-        return part
-    rows = part.shape[0] // group_count
-    cols = part.shape[1]
+        return jnp.dot(gated, w_out, preferred_element_type=jnp.float32).astype(jnp.bfloat16)
+    rows = gated.shape[0] // group_count
+    cols = w_out.shape[1]
     return pl.pallas_call(
         functools.partial(group_sum_kernel, group_count),
-        out_shape=jax.ShapeDtypeStruct((rows, cols), part.dtype),
-        in_specs=[pl.BlockSpec(memory_space=pltpu.VMEM)],
+        out_shape=jax.ShapeDtypeStruct((rows, cols), jnp.bfloat16),
+        in_specs=[pl.BlockSpec(memory_space=pltpu.VMEM)] * 2,
         out_specs=pl.BlockSpec(memory_space=pltpu.VMEM),
         scratch_shapes=[
-            pltpu.VMEM((group_count, rows, cols), part.dtype),
+            pltpu.VMEM((group_count, rows, cols), jnp.bfloat16),
+            pltpu.VMEM((group_count, rows, cols), jnp.bfloat16),
             pltpu.SemaphoreType.DMA((group_count,)),
             pltpu.SemaphoreType.DMA((group_count,)),
-            pltpu.SemaphoreType.DMA,
         ],
         compiler_params=pltpu.CompilerParams(collective_id=0, has_side_effects=True),
-    )(part)
+    )(gated, w_out)
 
 
 def on_device(
@@ -492,8 +492,7 @@
     produced = local_mix + jnp.einsum("jhsd,hde->jhse", entry_map, state_in, precision=highest)
     produced = produced.transpose(0, 2, 1, 3).reshape(tok_rows, head_count, DV)
     gated = gated_output(produced, zgate, norm_gain)
-    part = jnp.dot(gated, w_out, preferred_element_type=jnp.float32).astype(jnp.bfloat16)
-    return group_sum(part, lax.axis_size("hg"))
+    return group_sum(gated, w_out, lax.axis_size("hg"))
 
 
 def solution(mesh):

time: 115 us -> 114 us (level)
  matrix products: 13.8 us -> 11.1 us
    another operation x4 -> x3, local copies, waits for them, and re-layouts: 3.44 us -> 1.3 us  [to_blocks(): array_3d.reshape(tok_rows // SPAN, SPAN, head_count, -1)]
    transpose x4 -> x5, local copies, waits for them, and re-layouts: 1.91 us -> 4.03 us  [to_blocks(): array_3d.reshape(tok_rows // SPAN, SPAN, head_count, -1)]
    unnamed x29 -> x31, local copies, waits for them, and re-layouts: 2.64 us -> 4.65 us
    dot_general x1, matrix products: 5.39 us -> 3.47 us  [mixer_inputs(): jnp.dot(hidden_in, w_zgate, preferred_element_type=jnp.float32)]
where the time goes in v9:
time: 114 us
  Pallas kernels  79.6 us (70%)
  local copies, waits for them, and re-layouts  15.1 us (13%)
  matrix products  11.1 us (10%)
  starting transfers between devices  3.95 us (3%)
  other arithmetic  3.72 us (3%)
    pallas_call x1, Pallas kernels, shard_scan(): pl.pallas_call(functools.partial(shard_scan_kernel, shard_count), out_sha...  34.6 us
    pallas_call x1, Pallas kernels, group_sum(): pl.pallas_call(functools.partial(group_sum_kernel, group_count), out_shap...  31.7 us
    pallas_call x1, Pallas kernels, span_terms_kernel(): pl.pallas_call(functools.partial(span_kernel, lead[1]), out_shape=[jax.Sh...  13.3 us
    unnamed x31, local copies, waits for them, and re-layouts  4.65 us
    transpose x5, local copies, waits for them, and re-layouts, to_blocks(): array_3d.reshape(tok_rows // SPAN, SPAN, head_count, -1)  4.03 us
    ppermute x1, starting transfers between devices, passed_along(): return lax.ppermute(block, axis, route)  3.95 us
    dot_general x1, matrix products, mixer_inputs(): jnp.dot(hidden_in, w_zgate, preferred_element_type=jnp.float32)  3.47 us
    dot_general x1, matrix products, project_inputs(): jnp.dot(hidden_in, w_value, preferred_element_type=jnp.float32)  3.28 us
  transfers between devices with their start and end apart: 1, of which 0 were waited for; matrix products, arithmetic and copies ran while one was open for 3% of the time, Pallas kernels for 0%

profile of v9, /device:TPU:1, one launch (start us, length us, event | category | flops | bytes accessed | tf_op | source)
XLA Modules:
  0.0 113.8 jit_solution(6269898564740201983)
XLA Ops:
  0.0 0.0 copy-start
  0.0 1.6 %copy-done = bf16[2048,512]{1,0:T(8,128)(2,1)S(1)} copy-done((bf16[2048,512]{1,0:T(8,128)(2,1)S(1)}, bf16[2048,512]{1,0:T(8,128)(2,1)}, u32[]{:S(2)}) %copy-start) | copy-done | bytes 2097176
  1.6 3.3 %fusion.38 = (f32[384,512]{1,0:T(8,128)}, bf16[384,512]{1,0:T(8,128)(2,1)S(1)}) fusion(bf16[384,2048]{1,0:T(8,128)(2,1)} %param.14, bf16[2048,512]{1,0:T(8,128)(2,1)S(1)} %copy-done), kind=kOutput, calls=%fused_computation.85 | convolution fusion | flops 805699584 | bytes 4849664 | tf_op jit(solution)/shard_map/dot_general | solution.py:33
  4.9 0.0 copy-done.1
  4.9 0.0 copy-start.4
  4.9 0.6 fusion.36
  5.5 0.6 copy-done.4
  6.1 0.0 copy-start.7
  6.1 0.6 fusion.37
  6.7 0.0 copy-start.8
  6.7 0.0 copy-start.12
  6.8 3.9 %collective-permute-start = (bf16[3,1024]{1,0:T(4,128)(2,1)S(1)}, bf16[3,1024]{1,0:T(4,128)(2,1)S(1)}, u32[]{:S(2)}, u32[]{:S(2)}) collective-permute-start(bf16[3,1024]{1,0:T(4,128)(2,1)S(1)} %pad_maximum_fusion.3), channel_id=1, source_target_pairs={{0,8},{8,16},{16,24},{24,32},{32,40},{40,48},{48,56},{56,64},{64,7... | collective-permute-start | bytes 18440 | tf_op jit(solution)/shard_map/ppermute | solution.py:27
  10.7 0.0 copy-done.10
  10.8 0.0 copy-done.14
  10.8 0.0 copy-start.13
  10.9 0.5 fusion.5
  11.4 0.5 fusion.35
  12.0 0.1 reshape_broadcast_in_dim.6
  12.1 1.2 %copy.56.gc_ref = f32[24,64,1]{2,1,0:T(8,128)} copy(f32[24,64,1]{1,0,2:T(8,128)S(1)} %bitcast.87) | data formatting | bytes 12288 | tf_op jit(solution)/shard_map/broadcast_in_dim;reshape;squeeze | solution.py:367
  13.3 0.1 reshape_broadcast_in_dim.7
  13.4 1.2 %copy.57.bc_ref = f32[24,64,1]{2,1,0:T(8,128)} copy(f32[24,64,1]{1,0,2:T(8,128)S(1)} %bitcast.91) | data formatting | bytes 12288 | tf_op jit(solution)/shard_map/broadcast_in_dim;reshape;squeeze | solution.py:369
  14.6 0.0 collective-permute-done
  14.6 1.2 %divide_multiply_fusion.1 = (f32[384,256]{1,0:T(8,128)}, f32[384,256]{1,0:T(8,128)S(1)}) fusion(f32[384,256]{1,0:T(8,128)S(1)} %get-tuple-element.29, f32[3,256]{1,0:T(4,128)S(1)} %get-tuple-element.13, f32[256]{0:T(256)S(1)} %bitcast.102, f32[256]{0:T(256)S(1)} %bitcast.103, f32[256]{0:T(256)S(1)} %bitcast.101, f32[256]{0:T(256)S(1)} %bitcast.100, ...), kind=kLoop, calls=%fused_computation.54 | loop fusion | flops 2752512 | bytes 1587200 | tf_op jit(solution)/shard_map/jit(silu)/mul | solution.py:44
  15.9 1.2 %reshape.63 = f32[384,2,128]{2,1,0:T(2,128)S(1)} reshape(f32[384,256]{1,0:T(8,128)} %get-tuple-element.35) | data formatting | bytes 786432 | tf_op jit(solution)/shard_map/reshape | solution.py:74
  17.1 0.5 multiply_reduce_fusion.1
  17.6 0.5 broadcast_multiply_fusion
  18.1 0.1 broadcast_in_dim.5
  18.2 0.9 copy.51
  19.1 0.2 reshape.61
  19.3 0.5 multiply_reduce_fusion.2
  19.8 0.5 multiply_multiply_fusion
  20.3 0.1 broadcast_in_dim.4
  20.4 0.9 copy.49
  21.4 0.4 copy-done.5
  21.7 0.5 divide_multiply_fusion
  22.2 1.1 %reshape_reshape.11 = f32[6,64,4,128]{3,2,1,0:T(4,128)} reshape(f32[384,512]{1,0:T(8,128)S(1)} %divide_multiply_fusion) | data formatting | bytes 1572864 | tf_op jit(solution)/shard_map/reshape;reshape | solution.py:92
  23.3 2.1 %copy.52 = f32[6,4,64,128]{3,2,1,0:T(8,128)} copy(f32[6,4,64,128]{3,1,2,0:T(4,128)} %bitcast.78) | data formatting | bytes 1572864 | tf_op jit(solution)/shard_map/transpose | solution.py:92
  25.5 13.3 %shard_map.136 = (f32[4,128,128]{2,1,0:T(8,128)}, f32[4,128,128]{2,1,0:T(8,128)}, f32[24,64,128]{2,1,0:T(8,128)}, f32[24,64,128]{2,1,0:T(8,128)}) custom-call(f32[24,64,128]{2,1,0:T(8,128)} %bitcast.80, f32[24,64,128]{2,1,0:T(8,128)} %bitcast.79, f32[24,64,128]{2,1,0:T(8,128)} %bitcast.81, f32[24,64,1]{2,1,0:T(8,128)} %copy.56.gc_ref, ...), custom_call_target="tpu_custom_call" | custom-call | tf_op jit(solution)/shard_map/pallas_call | solution.py:353
  38.8 34.6 %shard_map.137 = f32[4,128,128]{2,1,0:T(8,128)} custom-call(f32[4,128,128]{2,1,0:T(8,128)} %get-tuple-element.10.a_ref, f32[4,128,128]{2,1,0:T(8,128)} %get-tuple-element.11.b_ref), custom_call_target="tpu_custom_call" | custom-call | tf_op jit(solution)/shard_map/pallas_call | solution.py:251
  73.4 2.1 %multiply_reduce_fusion = (f32[6,64,4]{1,0,2:T(8,128)S(1)}, f32[6,64,4,128]{3,1,0,2:T(8,128)S(1)}) fusion(f32[6,4,64,128]{3,2,1,0:T(8,128)} %bitcast.84, f32[4,128,128]{2,1,0:T(8,128)} %shard_map.137, f32[6,4,64,128]{3,2,1,0:T(8,128)} %bitcast.83), kind=kOutput, calls=%fused_computation.29 | convolution fusion | flops 151583232 | bytes 2627584 | tf_op jit(solution)/shard_map/jhsd,hde->jhse/dot_general | solution.py:492
  75.5 0.1 copy.63
  75.6 0.0 copy-start.2
  75.6 0.5 copy.60
  76.2 0.5 mul.302
  76.6 0.4 copy-done.2
  77.0 3.5 %fusion.15.gated_ref = bf16[384,512]{1,0:T(8,128)(2,1)} fusion(f32[48,8,4,128]{3,2,1,0:T(4,128)S(1)} %bitcast.85, f32[48,8,4,128]{3,2,1,0:T(4,128)S(1)} %bitcast.82, bf16[384,2048]{1,0:T(8,128)(2,1)S(1)} %copy-done.2, bf16[2048,512]{1,0:T(8,128)(2,1)} %param.18, f32[512]{0:T(512)S(1)} %broadcast_bitcast_fusion), kind=kOutput, calls=%fused_computation.25 | convolution fusion | flops 807272448 | bytes 5638144 | tf_op jit(solution)/shard_map/dot_general | solution.py:83
  80.5 31.7 %shard_map.138 = bf16[48,2048]{1,0:T(8,128)(2,1)} custom-call(bf16[384,512]{1,0:T(8,128)(2,1)} %fusion.15.gated_ref, bf16[512,2048]{1,0:T(8,128)(2,1)} %w_ref.1), custom_call_target="tpu_custom_call" | custom-call | tf_op jit(solution)/shard_map/pallas_call | solution.py:429
  112.2 1.6 %copy.74 = bf16[48,2048]{1,0:T(8,128)(2,1)} copy(bf16[48,2048]{1,0:T(8,128)(2,1)} %shard_map.138) | data formatting | bytes 393216
  (34 shorter events, 0.2 us)
Async XLA Ops:
  0.0 1.6 %copy-start = (bf16[2048,512]{1,0:T(8,128)(2,1)S(1)}, bf16[2048,512]{1,0:T(8,128)(2,1)}, u32[]{:S(2)}) copy-start(bf16[2048,512]{1,0:T(8,128)(2,1)} %param.17) | copy-start | bytes 6291460
  0.0 4.9 %copy-start.1 = (bf16[384,2048]{1,0:T(8,128)(2,1)S(1)}, bf16[384,2048]{1,0:T(8,128)(2,1)}, u32[]{:S(2)}) copy-start(bf16[384,2048]{1,0:T(8,128)(2,1)} %param.14) | copy-start | bytes 4718596
  0.0 4.9 %copy-start.3 = (bf16[2048,256]{1,0:T(8,128)(2,1)S(1)}, bf16[2048,256]{1,0:T(8,128)(2,1)}, u32[]{:S(2)}) copy-start(bf16[2048,256]{1,0:T(8,128)(2,1)} %param.15) | copy-start | bytes 3145732
  4.9 1.2 %copy-start.4 = (bf16[2048,256]{1,0:T(8,128)(2,1)S(1)}, bf16[2048,256]{1,0:T(8,128)(2,1)}, u32[]{:S(2)}) copy-start(bf16[2048,256]{1,0:T(8,128)(2,1)} %param.16) | copy-start | bytes 3145732
  6.1 4.6 %copy-start.10 = (bf16[4,256]{1,0:T(4,128)(2,1)S(1)}, bf16[4,256]{1,0:T(4,128)(2,1)}, u32[]{:S(2)}) copy-start(bf16[4,256]{1,0:T(4,128)(2,1)} %param.21) | copy-start | bytes 6148
  6.1 4.6 %copy-start.11 = (bf16[4,256]{1,0:T(4,128)(2,1)S(1)}, bf16[4,256]{1,0:T(4,128)(2,1)}, u32[]{:S(2)}) copy-start(bf16[4,256]{1,0:T(4,128)(2,1)} %param.22) | copy-start | bytes 6148
  6.1 4.7 %copy-start.9 = (bf16[4,512]{1,0:T(4,128)(2,1)S(1)}, bf16[4,512]{1,0:T(4,128)(2,1)}, u32[]{:S(2)}) copy-start(bf16[4,512]{1,0:T(4,128)(2,1)} %param.23) | copy-start | bytes 12292
  6.1 4.7 %copy-start.14 = (f32[4]{0:T(128)S(1)}, f32[4]{0:T(128)}, u32[]{:S(2)}) copy-start(f32[4]{0:T(128)} %param.24) | copy-start | bytes 52
  6.1 4.7 %copy-start.7 = (bf16[2048,4]{0,1:T(4,128)(2,1)S(1)}, bf16[2048,4]{0,1:T(4,128)(2,1)}, u32[]{:S(2)}) copy-start(bf16[2048,4]{0,1:T(4,128)(2,1)} %param.20) | copy-start | bytes 49156
  6.7 4.7 %copy-start.8 = (bf16[2048,4]{0,1:T(4,128)(2,1)S(1)}, bf16[2048,4]{0,1:T(4,128)(2,1)}, u32[]{:S(2)}) copy-start(bf16[2048,4]{0,1:T(4,128)(2,1)} %param.19) | copy-start | bytes 49156
  6.7 4.7 %copy-start.12 = (f32[4]{0:T(128)S(1)}, f32[4]{0:T(128)}, u32[]{:S(2)}) copy-start(f32[4]{0:T(128)} %param.25) | copy-start | bytes 52
  6.8 7.9 %collective-permute-start = (bf16[3,1024]{1,0:T(4,128)(2,1)S(1)}, bf16[3,1024]{1,0:T(4,128)(2,1)S(1)}, u32[]{:S(2)}, u32[]{:S(2)}) collective-permute-start(bf16[3,1024]{1,0:T(4,128)(2,1)S(1)} %pad_maximum_fusion.3), channel_id=1, source_target_pairs={{0,8},{8,16},{16,24},{24,32},{32,40},{40,48},{48,56},{56,64},{64,7... | collective-permute-start | bytes 18440 | tf_op jit(solution)/shard_map/ppermute | solution.py:27
  10.8 1.1 copy-start.13
  12.1 3.8 %copy-start.6 = (f32[6,4,64,1]{2,1,0,3:T(4,128)}, f32[6,4,64,1]{2,1,0,3:T(4,128)S(1)}, u32[]{:S(2)}) copy-start(f32[6,4,64,1]{2,1,0,3:T(4,128)S(1)} %copy.53) | copy-start | bytes 18436
  20.3 1.4 %copy-start.5 = (f32[384,512]{1,0:T(8,128)S(1)}, f32[384,512]{1,0:T(8,128)}, u32[]{:S(2)}) copy-start(f32[384,512]{1,0:T(8,128)} %get-tuple-element.31) | copy-start | bytes 2359300
  75.6 1.4 %copy-start.2 = (bf16[384,2048]{1,0:T(8,128)(2,1)S(1)}, bf16[384,2048]{1,0:T(8,128)(2,1)}, u32[]{:S(2)}) copy-start(bf16[384,2048]{1,0:T(8,128)(2,1)} %param.14) | copy-start | bytes 4718596

commit v10 on v9

--- a/solution.py
+++ b/solution.py
@@ -268,14 +268,25 @@
 
 
 def span_kernel(
-    head_count, q_ref, k_ref, v_ref, gc_ref, gr_ref, bc_ref, shard_a_ref, shard_b_ref, mix_ref, entry_ref
+    head_count, q_ref, k_ref, v_ref, gc_ref, gr_ref, bc_ref, shard_a_ref, shard_b_ref, mix_ref, entry_ref,
+    q_pairs, k_pairs, v_pairs, decay_pairs, rate_pairs
 ):
-    queries = q_ref[...]
-    key_vecs = k_ref[...]
-    values = v_ref[...]
-    decay_col = gc_ref[...]
+    width = q_ref.shape[2] // head_count
+    for span in range(q_ref.shape[0]):
+        for head in range(head_count):
+            pair = span * head_count + head
+            lanes = slice(head * width, (head + 1) * width)
+            q_pairs[pair] = q_ref[span, :, lanes]
+            k_pairs[pair] = k_ref[span, :, lanes]
+            v_pairs[pair] = v_ref[span, :, lanes]
+            decay_pairs[pair] = gc_ref[span, :, head : head + 1]
+            rate_pairs[pair] = bc_ref[span, :, head : head + 1]
+    queries = q_pairs[...]
+    key_vecs = k_pairs[...]
+    values = v_pairs[...]
+    decay_col = decay_pairs[...]
     decay_row = gr_ref[...]
-    rate = bc_ref[...]
+    rate = rate_pairs[...]
     block_len = queries.shape[1]
     row_ids = lax.broadcasted_iota(jnp.int32, (1, block_len, block_len), 1)
     col_ids = lax.broadcasted_iota(jnp.int32, (1, block_len, block_len), 2)
@@ -324,16 +335,22 @@
     for span in range(queries.shape[0] // head_count):
         heads = slice(span * head_count, (span + 1) * head_count)
         if span == 0:
-            mix_ref[heads] = local_out[heads]
-            entry_ref[heads] = carry_map[heads]
+            span_mix = local_out[heads]
+            span_entry = carry_map[heads]
+        else:
+            span_mix = local_out[heads] + jnp.einsum(
+                "hsd,hde->hse", carry_map[heads], prefix_b, precision=highest,
+                preferred_element_type=jnp.float32)
+            span_entry = jnp.einsum("hsd,hde->hse", carry_map[heads], prefix_a, precision=highest,
+                                    preferred_element_type=jnp.float32)
+        for head in range(head_count):
+            lanes = slice(head * width, (head + 1) * width)
+            mix_ref[span, :, lanes] = span_mix[head]
+            entry_ref[span, :, lanes] = span_entry[head]
+        if span == 0:
             prefix_a = transition[heads]
             prefix_b = written[heads]
             continue
-        mix_ref[heads] = local_out[heads] + jnp.einsum(
-            "hsd,hde->hse", carry_map[heads], prefix_b, precision=highest,
-            preferred_element_type=jnp.float32)
-        entry_ref[heads] = jnp.einsum("hsd,hde->hse", carry_map[heads], prefix_a, precision=highest,
-                                      preferred_element_type=jnp.float32)
         prefix_b = written[heads] + jnp.einsum(
             "hde,hef->hdf", transition[heads], prefix_b, precision=highest,
             preferred_element_type=jnp.float32)
@@ -344,36 +361,37 @@
 
 
 def span_terms_kernel(queries, key_vecs, values, log_decay, write_rate):
-    lead = queries.shape[:2]
-    block_len, width = queries.shape[2], queries.shape[3]
-    flat = lambda x: x.reshape((-1,) + x.shape[2:])
-    pairs = lead[0] * lead[1]
-    decay = log_decay.reshape(pairs, block_len)
-    rate = write_rate.reshape(pairs, block_len)
+    tok_rows, head_count, width = queries.shape
+    spans = tok_rows // SPAN
+    pairs = spans * head_count
+    by_span = lambda x: x.reshape(spans, SPAN, -1)
+    decay_row = to_blocks(log_decay[..., None])[..., 0].reshape(pairs, 1, SPAN)
     shard_a, shard_b, local_mix, entry_map = pl.pallas_call(
-        functools.partial(span_kernel, lead[1]),
+        functools.partial(span_kernel, head_count),
         out_shape=[
-            jax.ShapeDtypeStruct((lead[1], width, width), jnp.float32),
-            jax.ShapeDtypeStruct((lead[1], width, values.shape[3]), jnp.float32),
-            jax.ShapeDtypeStruct((pairs, block_len, values.shape[3]), jnp.float32),
-            jax.ShapeDtypeStruct((pairs, block_len, width), jnp.float32),
+            jax.ShapeDtypeStruct((head_count, width, width), jnp.float32),
+            jax.ShapeDtypeStruct((head_count, width, values.shape[2]), jnp.float32),
+            jax.ShapeDtypeStruct((spans, SPAN, head_count * values.shape[2]), jnp.float32),
+            jax.ShapeDtypeStruct((spans, SPAN, head_count * width), jnp.float32),
         ],
         in_specs=[pl.BlockSpec(memory_space=pltpu.VMEM)] * 6,
         out_specs=[pl.BlockSpec(memory_space=pltpu.VMEM)] * 4,
+        scratch_shapes=[
+            pltpu.VMEM((pairs, SPAN, width), jnp.float32),
+            pltpu.VMEM((pairs, SPAN, width), jnp.float32),
+            pltpu.VMEM((pairs, SPAN, values.shape[2]), jnp.float32),
+            pltpu.VMEM((pairs, SPAN, 1), jnp.float32),
+            pltpu.VMEM((pairs, SPAN, 1), jnp.float32),
+        ],
     )(
-        flat(queries),
-        flat(key_vecs),
-        flat(values),
-        decay[:, :, None],
-        decay[:, None, :],
-        rate[:, :, None],
-    )
-    return (
-        shard_a,
-        shard_b,
-        local_mix.reshape(lead + local_mix.shape[1:]),
-        entry_map.reshape(lead + entry_map.shape[1:]),
-    )
+        by_span(queries),
+        by_span(key_vecs),
+        by_span(values),
+        by_span(log_decay),
+        decay_row,
+        by_span(write_rate),
+    )
+    return shard_a, shard_b, local_mix, entry_map
 
 
 def group_sum_kernel(group_count, gated_ref, w_ref, out_ref, outgoing, landed, send_sems, recv_sems):
@@ -481,16 +499,13 @@
         dt_bias,
     )
     shard_a, shard_b, local_mix, entry_map = span_terms_kernel(
-        to_blocks(queries),
-        to_blocks(key_vecs),
-        to_blocks(values),
-        to_blocks(log_decay[..., None])[..., 0],
-        to_blocks(write_rate[..., None])[..., 0],
+        queries, key_vecs, values, log_decay, write_rate
     )
     head_count = values.shape[1]
     state_in = shard_scan(shard_a, shard_b, lax.axis_size("seq"))
-    produced = local_mix + jnp.einsum("jhsd,hde->jhse", entry_map, state_in, precision=highest)
-    produced = produced.transpose(0, 2, 1, 3).reshape(tok_rows, head_count, DV)
+    produced = local_mix.reshape(tok_rows, head_count, DV) + jnp.einsum(
+        "thd,hde->the", entry_map.reshape(tok_rows, head_count, DK), state_in, precision=highest
+    )
     gated = gated_output(produced, zgate, norm_gain)
     return group_sum(gated, w_out, lax.axis_size("hg"))
 

time: 114 us -> 130 us (1.14)
  local copies, waits for them, and re-layouts: 15.1 us -> 25.6 us
  other arithmetic: 3.72 us -> 8.67 us
    reshape x0 -> x4, local copies, waits for them, and re-layouts: none -> 8.26 us  [the longest x2 4.6 us: on_device(): local_mix.reshape(tok_rows, head_count, DV)]
    mul x2, other arithmetic: 1.7 us -> 6.35 us  [conv_silu(): return jax.nn.silu(summed)]
    transpose x5 -> x1, local copies, waits for them, and re-layouts: 4.03 us -> 0.61 us  [to_blocks(): array_3d.reshape(tok_rows // SPAN, SPAN, head_count, -1)]
    another operation x2, local copies, waits for them, and re-layouts: 2.48 us -> 5.33 us  [span_terms_kernel(): by_span = lambda x: x.reshape(spans, SPAN, -1)]
    dot_general x1, matrix products: 3.47 us -> 1.9 us  [mixer_inputs(): jnp.dot(hidden_in, w_zgate, preferred_element_type=jnp.float32)]
    unnamed x31 -> x27, local copies, waits for them, and re-layouts: 4.65 us -> 4.01 us
  transfers between devices with their start and end apart: 1 -> 1, of which waited for: 0 -> 0; matrix products, arithmetic and copies ran while one was open for 3% -> 5% of each run, Pallas kernels for 0% -> 0%
where the time goes in v10:
time: 130 us; the launch traced here: 129 us
  Pallas kernels  80.3 us (62%)
  local copies, waits for them, and re-layouts  25.6 us (20%)
  matrix products  10.2 us (8%)
  other arithmetic  8.67 us (7%)
  starting transfers between devices  3.94 us (3%)
    pallas_call x1, Pallas kernels, shard_scan(): pl.pallas_call(functools.partial(shard_scan_kernel, shard_count), out_sha...  34.6 us
    pallas_call x1, Pallas kernels, group_sum(): pl.pallas_call(functools.partial(group_sum_kernel, group_count), out_shap...  31.6 us
    pallas_call x1, Pallas kernels, span_terms_kernel(): pl.pallas_call(functools.partial(span_kernel, head_count), out_shape=[jax...  14 us
    mul x2, other arithmetic, conv_silu(): return jax.nn.silu(summed)  6.35 us
    another operation x2, local copies, waits for them, and re-layouts, span_terms_kernel(): by_span = lambda x: x.reshape(spans, SPAN, -1)  5.33 us
    reshape x2, local copies, waits for them, and re-layouts, on_device(): local_mix.reshape(tok_rows, head_count, DV)  4.6 us
    unnamed x27, local copies, waits for them, and re-layouts  4.01 us
    ppermute x1, starting transfers between devices, passed_along(): return lax.ppermute(block, axis, route)  3.94 us
  transfers between devices with their start and end apart: 1, of which 0 were waited for; matrix products, arithmetic and copies ran while one was open for 5% of the time, Pallas kernels for 0%

profile of v10, /device:TPU:1, one launch (start us, length us, event | category | flops | bytes accessed | tf_op | source)
XLA Modules:
  0.0 128.9 jit_solution(18200541804330858423)
XLA Ops:
  0.0 0.0 copy-start
  0.0 1.6 %copy-done = bf16[2048,512]{1,0:T(8,128)(2,1)S(1)} copy-done((bf16[2048,512]{1,0:T(8,128)(2,1)S(1)}, bf16[2048,512]{1,0:T(8,128)(2,1)}, u32[]{:S(2)}) %copy-start) | copy-done | bytes 2097176
  1.6 3.3 %fusion.33 = (f32[384,512]{1,0:T(8,128)}, bf16[384,512]{1,0:T(8,128)(2,1)S(1)}) fusion(bf16[384,2048]{1,0:T(8,128)(2,1)} %param.14, bf16[2048,512]{1,0:T(8,128)(2,1)S(1)} %copy-done), kind=kOutput, calls=%fused_computation.79 | convolution fusion | flops 805699584 | bytes 4849664 | tf_op jit(solution)/shard_map/dot_general | solution.py:33
  4.9 0.0 copy-done.1
  4.9 0.0 copy-done.2
  4.9 0.0 copy-start.3
  4.9 0.6 fusion.31
  5.5 0.6 copy-done.3
  6.1 0.0 copy-start.11
  6.2 1.3 %fusion.32 = (f32[384,256]{1,0:T(8,128)}, bf16[384,256]{1,0:T(8,128)(2,1)S(1)}) fusion(bf16[384,2048]{1,0:T(8,128)(2,1)S(1)} %copy-done.1, bf16[2048,256]{1,0:T(8,128)(2,1)S(1)} %copy-done.3), kind=kOutput, calls=%fused_computation.78 | convolution fusion | flops 402849792 | bytes 3211264 | tf_op jit(solution)/shard_map/dot_general | solution.py:32
  7.5 3.9 %collective-permute-start = (bf16[3,1024]{1,0:T(4,128)(2,1)S(1)}, bf16[3,1024]{1,0:T(4,128)(2,1)S(1)}, u32[]{:S(2)}, u32[]{:S(2)}) collective-permute-start(bf16[3,1024]{1,0:T(4,128)(2,1)S(1)} %pad_maximum_fusion.3), channel_id=1, source_target_pairs={{0,8},{8,16},{16,24},{24,32},{32,40},{40,48},{48,56},{56,64},{64,7... | collective-permute-start | bytes 18440 | tf_op jit(solution)/shard_map/ppermute | solution.py:27
  11.4 0.0 copy-done.7
  11.5 0.0 copy-done.6
  11.5 0.5 fusion.4
  12.1 0.0 copy-start.5
  12.1 0.0 copy-start.9
  12.1 1.9 %fusion.1 = f32[384,512]{1,0:T(8,128)} fusion(bf16[384,2048]{1,0:T(8,128)(2,1)S(1)} %copy-done.1, bf16[2048,512]{1,0:T(8,128)(2,1)S(1)} %copy-done.11), kind=kOutput, calls=%fused_computation.3 | convolution fusion | flops 805699584 | bytes 4456448 | tf_op jit(solution)/shard_map/dot_general | solution.py:83
  14.0 0.5 fusion.30
  14.6 0.1 copy-done.8
  14.7 0.8 copy.23
  15.5 0.1 reshape_broadcast_in_dim.3
  15.6 0.6 copy.24
  16.2 0.8 copy.25
  17.0 1.4 %copy.29 = f32[384,512]{0,1:T(8,128)S(1)} copy(f32[384,512]{1,0:T(8,128)} %fusion.1) | data formatting | bytes 1572864 | tf_op jit(solution)/shard_map/reshape | solution.py:151
  18.4 0.0 collective-permute-done
  18.4 2.9 %divide_multiply_fusion.1 = (f32[384,256]{1,0:T(8,128)}, f32[384,256]{1,0:T(8,128)}) fusion(f32[384,256]{1,0:T(8,128)} %get-tuple-element.29, f32[3,256]{1,0:T(4,128)S(1)} %get-tuple-element.13, f32[256]{0:T(256)S(1)} %bitcast.55, f32[256]{0:T(256)S(1)} %bitcast.56, f32[256]{0:T(256)S(1)} %bitcast.54, f32[256]{0:T(256)S(1)} %bitcast.53, ...), kind=kLoop, calls=%fused_computation.50 | loop fusion | flops 2752512 | bytes 1587200 | tf_op jit(solution)/shard_map/jit(silu)/mul | solution.py:44
  21.3 1.2 reshape.50
  22.5 0.5 multiply_reduce_fusion.1
  23.0 0.5 broadcast_multiply_fusion
  23.5 1.2 broadcast_in_dim.5
  24.7 2.7 %reshape_reshape.10.k_ref = f32[6,64,512]{2,1,0:T(8,128)} reshape(f32[384,2,2,128]{3,2,1,0:T(2,128)} %broadcast_in_dim.5) | data formatting | bytes 1572864 | tf_op jit(solution)/shard_map/reshape;reshape | solution.py:367
  27.3 1.2 reshape.49
  28.5 0.5 multiply_reduce_fusion.2
  29.1 0.5 multiply_multiply_fusion
  29.5 1.2 broadcast_in_dim.4
  30.7 2.6 %reshape_reshape.9.q_ref = f32[6,64,512]{2,1,0:T(8,128)} reshape(f32[384,2,2,128]{3,2,1,0:T(2,128)} %broadcast_in_dim.4) | data formatting | bytes 1572864 | tf_op jit(solution)/shard_map/reshape;reshape | solution.py:367
  33.3 3.5 %divide_multiply_fusion = f32[384,512]{1,0:T(8,128)} fusion(f32[384,512]{1,0:T(8,128)} %get-tuple-element.31, f32[3,512]{1,0:T(4,128)S(1)} %slice_convert_fusion, f32[512]{0:T(512)S(1)} %bitcast.47, f32[512]{0:T(512)S(1)} %bitcast.48, f32[512]{0:T(512)S(1)} %bitcast.46, f32[512]{0:T(512)S(1)} %bitcast.45), kind=kLoop, calls=%fused_computation.26 | loop fusion | flops 2752512 | bytes 1587200 | tf_op jit(solution)/shard_map/jit(silu)/mul | solution.py:44
  36.8 14.0 %shard_map.136 = (f32[4,128,128]{2,1,0:T(8,128)}, f32[4,128,128]{2,1,0:T(8,128)}, f32[6,64,512]{2,1,0:T(8,128)}, f32[6,64,512]{2,1,0:T(8,128)}) custom-call(f32[6,64,512]{2,1,0:T(8,128)} %reshape_reshape.9.q_ref, f32[6,64,512]{2,1,0:T(8,128)} %reshape_reshape.10.k_ref, f32[6,64,512]{2,1,0:T(8,128)} %bitcast.39, f32[6,64,4]{2,1,0:T(8,128)} %bitcast.41, ...), custom_call_target="tpu_custom_call" | custom-call | tf_op jit(solution)/shard_map/pallas_call | solution.py:369
  50.8 2.3 %reshape.53 = f32[384,4,128]{2,1,0:T(4,128)} reshape(f32[6,64,512]{2,1,0:T(8,128)} %get-tuple-element.9) | data formatting | bytes 1572864 | tf_op jit(solution)/shard_map/reshape | solution.py:506
  53.1 2.3 %copy.28 = f32[384,4,128]{0,2,1:T(8,128)} copy(f32[384,4,128]{2,1,0:T(4,128)} %reshape.53) | data formatting | bytes 1572864 | tf_op jit(solution)/shard_map/reshape | solution.py:506
  55.4 2.3 %reshape.54 = f32[384,4,128]{2,1,0:T(4,128)} reshape(f32[6,64,512]{2,1,0:T(8,128)} %get-tuple-element.12) | data formatting | bytes 1572864 | tf_op jit(solution)/shard_map/reshape | solution.py:507
  57.7 34.6 %shard_map.137 = f32[4,128,128]{2,1,0:T(8,128)} custom-call(f32[4,128,128]{2,1,0:T(8,128)} %get-tuple-element.10.a_ref, f32[4,128,128]{2,1,0:T(8,128)} %get-tuple-element.11.b_ref), custom_call_target="tpu_custom_call" | custom-call | tf_op jit(solution)/shard_map/pallas_call | solution.py:251
  92.3 2.1 %multiply_reduce_fusion = (f32[384,4]{0,1:T(4,128)S(1)}, f32[384,4,128]{0,2,1:T(8,128)S(1)}) fusion(f32[384,4,128]{0,2,1:T(8,128)} %copy.28, f32[4,128,128]{2,1,0:T(8,128)} %shard_map.137, f32[384,4,128]{2,1,0:T(4,128)} %reshape.54), kind=kOutput, calls=%fused_computation.25 | convolution fusion | flops 151583232 | bytes 2627584 | tf_op jit(solution)/shard_map/thd,hde->the/dot_general | solution.py:506
  94.4 0.0 copy-done.10
  94.4 0.3 multiply_convert_fusion
  94.7 0.9 copy.32.gated_ref
  95.7 31.6 %shard_map.138 = bf16[48,2048]{1,0:T(8,128)(2,1)} custom-call(bf16[384,512]{1,0:T(8,128)(2,1)} %copy.32.gated_ref, bf16[512,2048]{1,0:T(8,128)(2,1)} %w_ref.1), custom_call_target="tpu_custom_call" | custom-call | tf_op jit(solution)/shard_map/pallas_call | solution.py:447
  127.3 1.6 %copy.38 = bf16[48,2048]{1,0:T(8,128)(2,1)} copy(bf16[48,2048]{1,0:T(8,128)(2,1)} %shard_map.138) | data formatting | bytes 393216
  (26 shorter events, 0.2 us)
Async XLA Ops:
  0.0 1.6 %copy-start = (bf16[2048,512]{1,0:T(8,128)(2,1)S(1)}, bf16[2048,512]{1,0:T(8,128)(2,1)}, u32[]{:S(2)}) copy-start(bf16[2048,512]{1,0:T(8,128)(2,1)} %param.17) | copy-start | bytes 6291460
  0.0 4.9 %copy-start.1 = (bf16[384,2048]{1,0:T(8,128)(2,1)S(1)}, bf16[384,2048]{1,0:T(8,128)(2,1)}, u32[]{:S(2)}) copy-start(bf16[384,2048]{1,0:T(8,128)(2,1)} %param.14) | copy-start | bytes 4718596
  0.0 4.9 %copy-start.2 = (bf16[2048,256]{1,0:T(8,128)(2,1)S(1)}, bf16[2048,256]{1,0:T(8,128)(2,1)}, u32[]{:S(2)}) copy-start(bf16[2048,256]{1,0:T(8,128)(2,1)} %param.15) | copy-start | bytes 3145732
  4.9 1.2 copy-start.3
  6.1 5.3 %copy-start.7 = (bf16[4,256]{1,0:T(4,128)(2,1)S(1)}, bf16[4,256]{1,0:T(4,128)(2,1)}, u32[]{:S(2)}) copy-start(bf16[4,256]{1,0:T(4,128)(2,1)} %param.21) | copy-start | bytes 6148
  6.1 5.3 %copy-start.6 = (bf16[4,512]{1,0:T(4,128)(2,1)S(1)}, bf16[4,512]{1,0:T(4,128)(2,1)}, u32[]{:S(2)}) copy-start(bf16[4,512]{1,0:T(4,128)(2,1)} %param.23) | copy-start | bytes 12292
  6.1 5.4 %copy-start.12 = (f32[4]{0:T(128)S(1)}, f32[4]{0:T(128)}, u32[]{:S(2)}) copy-start(f32[4]{0:T(128)} %param.24) | copy-start | bytes 52
  6.1 5.4 %copy-start.4 = (bf16[2048,4]{0,1:T(4,128)(2,1)S(1)}, bf16[2048,4]{0,1:T(4,128)(2,1)}, u32[]{:S(2)}) copy-start(bf16[2048,4]{0,1:T(4,128)(2,1)} %param.20) | copy-start | bytes 49156
  6.1 5.9 %copy-start.11 = (bf16[2048,512]{1,0:T(8,128)(2,1)S(1)}, bf16[2048,512]{1,0:T(8,128)(2,1)}, u32[]{:S(2)}) copy-start(bf16[2048,512]{1,0:T(8,128)(2,1)} %param.18) | copy-start | bytes 6291460
  7.5 10.9 %collective-permute-start = (bf16[3,1024]{1,0:T(4,128)(2,1)S(1)}, bf16[3,1024]{1,0:T(4,128)(2,1)S(1)}, u32[]{:S(2)}, u32[]{:S(2)}) collective-permute-start(bf16[3,1024]{1,0:T(4,128)(2,1)S(1)} %pad_maximum_fusion.3), channel_id=1, source_target_pairs={{0,8},{8,16},{16,24},{24,32},{32,40},{40,48},{48,56},{56,64},{64,7... | collective-permute-start | bytes 18440 | tf_op jit(solution)/shard_map/ppermute | solution.py:27
  12.1 1.9 %copy-start.5 = (bf16[2048,4]{0,1:T(4,128)(2,1)S(1)}, bf16[2048,4]{0,1:T(4,128)(2,1)}, u32[]{:S(2)}) copy-start(bf16[2048,4]{0,1:T(4,128)(2,1)} %param.19) | copy-start | bytes 49156
  12.1 1.9 %copy-start.9 = (f32[4]{0:T(128)S(1)}, f32[4]{0:T(128)}, u32[]{:S(2)}) copy-start(f32[4]{0:T(128)} %param.25) | copy-start | bytes 52
  14.0 0.7 copy-start.8
  57.7 36.7 %copy-start.10 = (f32[128]{0:T(128)S(1)}, f32[128]{0:T(128)}, u32[]{:S(2)}) copy-start(f32[128]{0:T(128)} %param.26) | copy-start | bytes 1540

commit v11 on v8

--- a/solution.py
+++ b/solution.py
@@ -165,7 +165,7 @@
 
 
 def shard_scan_kernel(
-    shard_count, a_ref, b_ref, out_ref, cur_a, cur_b, out_a, out_b, got_a, got_b, send_sems, recv_sems
+    shard_count, a_ref, b_ref, out_ref, cur_a, cur_b, out_ab, got_ab, send_sems, recv_sems
 ):
     me = lax.axis_index("seq")
     hg_me = lax.axis_index("hg")
@@ -182,33 +182,23 @@
     pl.semaphore_wait(barrier, 2 * len(distances))
     cur_a[0] = a_ref[...]
     cur_b[0] = b_ref[...]
-    out_a[0] = a_ref[...].astype(out_a.dtype)
-    out_b[0] = b_ref[...].astype(out_b.dtype)
+    out_ab[0, 0] = a_ref[...].astype(out_ab.dtype)
+    out_ab[0, 1] = b_ref[...].astype(out_ab.dtype)
     sem_index = 0
     for round_index, distance in enumerate(distances):
         target = lax.rem(me + distance, shard_count)
         sends_a = round_index + 1 < len(distances)
+        whole = slice(None) if sends_a else 1
         copies = [
             pltpu.make_async_remote_copy(
-                src_ref=out_b.at[round_index],
-                dst_ref=got_b.at[round_index],
+                src_ref=out_ab.at[round_index, whole],
+                dst_ref=got_ab.at[round_index, whole],
                 send_sem=send_sems.at[sem_index],
                 recv_sem=recv_sems.at[sem_index],
                 device_id=(target, hg_me),
                 device_id_type=MESH,
             )
         ]
-        if sends_a:
-            copies.append(
-                pltpu.make_async_remote_copy(
-                    src_ref=out_a.at[round_index],
-                    dst_ref=got_a.at[round_index],
-                    send_sem=send_sems.at[sem_index + 1],
-                    recv_sem=recv_sems.at[sem_index + 1],
-                    device_id=(target, hg_me),
-                    device_id_type=MESH,
-                )
-            )
         sem_index += len(copies)
         for copy in copies:
             copy.start()
@@ -219,23 +209,23 @@
             own_a = cur_a[round_index, head]
             own_b = cur_b[round_index, head]
             joined_b = (
-                jnp.dot(own_a, got_b[round_index, head].astype(jnp.float32), precision=highest,
+                jnp.dot(own_a, got_ab[round_index, 1, head].astype(jnp.float32), precision=highest,
                         preferred_element_type=jnp.float32)
                 + own_b
             )
             next_b = jnp.where(has_prev, joined_b, own_b)
             cur_b[round_index + 1, head] = next_b
-            out_b[round_index + 1, head] = next_b.astype(out_b.dtype)
+            out_ab[round_index + 1, 1, head] = next_b.astype(out_ab.dtype)
             if sends_a:
-                joined_a = jnp.dot(own_a, got_a[round_index, head].astype(jnp.float32),
+                joined_a = jnp.dot(own_a, got_ab[round_index, 0, head].astype(jnp.float32),
                                    precision=highest, preferred_element_type=jnp.float32)
                 next_a = jnp.where(has_prev, joined_a, own_a)
                 cur_a[round_index + 1, head] = next_a
-                out_a[round_index + 1, head] = next_a.astype(out_a.dtype)
+                out_ab[round_index + 1, 0, head] = next_a.astype(out_ab.dtype)
     last = len(distances)
     shift = pltpu.make_async_remote_copy(
-        src_ref=out_b.at[last],
-        dst_ref=got_b.at[last],
+        src_ref=out_ab.at[last, 1],
+        dst_ref=got_ab.at[last, 1],
         send_sem=send_sems.at[sem_index],
         recv_sem=recv_sems.at[sem_index],
         device_id=(lax.rem(me + 1, shard_count), hg_me),
@@ -243,7 +233,7 @@
     )
     shift.start()
     shift.wait()
-    out_ref[...] = jnp.where(me >= 1, got_b[last].astype(jnp.float32), 0.0)
+    out_ref[...] = jnp.where(me >= 1, got_ab[last, 1].astype(jnp.float32), 0.0)
 
 
 def shard_scan(shard_a, shard_b, shard_count):
@@ -256,10 +246,8 @@
         scratch_shapes=[
             pltpu.VMEM((rounds + 1,) + shard_a.shape, jnp.float32),
             pltpu.VMEM((rounds + 1,) + shard_b.shape, jnp.float32),
-            pltpu.VMEM((rounds + 1,) + shard_a.shape, jnp.bfloat16),
-            pltpu.VMEM((rounds + 1,) + shard_b.shape, jnp.bfloat16),
-            pltpu.VMEM((rounds + 1,) + shard_a.shape, jnp.bfloat16),
-            pltpu.VMEM((rounds + 1,) + shard_b.shape, jnp.bfloat16),
+            pltpu.VMEM((rounds + 1, 2) + shard_a.shape, jnp.bfloat16),
+            pltpu.VMEM((rounds + 1, 2) + shard_a.shape, jnp.bfloat16),
             pltpu.SemaphoreType.DMA((2 * rounds + 1,)),
             pltpu.SemaphoreType.DMA((2 * rounds + 1,)),
         ],

time: 115 us -> 115 us (level)
  no operation moved by 1% of the time
where the time goes in v11:
time: 115 us; the launch traced here: 114 us
  Pallas kernels  78.5 us (68%)
  local copies, waits for them, and re-layouts  14.1 us (12%)
  matrix products  13.8 us (12%)
  starting transfers between devices  3.95 us (3%)
  other arithmetic  3.72 us (3%)
    pallas_call x1, Pallas kernels, shard_scan(): pl.pallas_call(functools.partial(shard_scan_kernel, shard_count), out_sha...  34.6 us
    pallas_call x1, Pallas kernels, group_sum(): pl.pallas_call(functools.partial(group_sum_kernel, group_count), out_shap...  30.6 us
    pallas_call x1, Pallas kernels, span_terms_kernel(): pl.pallas_call(functools.partial(span_kernel, lead[1]), out_shape=[jax.Sh...  13.3 us
    dot_general x1, matrix products, on_device(): jnp.dot(gated, w_out, preferred_element_type=jnp.float32)  5.39 us
    dot_general x1, matrix products, project_inputs(): jnp.dot(hidden_in, w_value, preferred_element_type=jnp.float32)  4.09 us
    ppermute x1, starting transfers between devices, passed_along(): return lax.ppermute(block, axis, route)  3.95 us
    another operation x4, local copies, waits for them, and re-layouts, to_blocks(): array_3d.reshape(tok_rows // SPAN, SPAN, head_count, -1)  3.44 us
    unnamed x29, local copies, waits for them, and re-layouts  2.64 us
  transfers between devices with their start and end apart: 1, of which 0 were waited for; matrix products, arithmetic and copies ran while one was open for 3% of the time, Pallas kernels for 0%

profile of v11, /device:TPU:1, one launch (start us, length us, event | category | flops | bytes accessed | tf_op | source)
XLA Modules:
  0.0 114.4 jit_solution(8591475927209087302)
XLA Ops:
  0.0 0.0 copy-start
  0.0 4.1 %fusion.41 = (f32[384,512]{1,0:T(8,128)}, bf16[384,512]{1,0:T(8,128)(2,1)S(1)}) fusion(bf16[384,2048]{1,0:T(8,128)(2,1)} %param.14, bf16[2048,512]{1,0:T(8,128)(2,1)} %param.17), kind=kOutput, calls=%fused_computation.89 | convolution fusion | flops 805699584 | bytes 4849664 | tf_op jit(solution)/shard_map/dot_general | solution.py:33
  4.1 0.0 copy-done.1
  4.1 0.0 copy-done.2
  4.1 0.0 copy-start.3
  4.1 0.6 fusion.39
  4.7 0.6 copy-done.3
  5.4 0.0 copy-start.6
  5.4 0.6 fusion.40
  6.0 0.0 copy-start.7
  6.0 0.0 copy-start.11
  6.0 3.9 %collective-permute-start = (bf16[3,1024]{1,0:T(4,128)(2,1)S(1)}, bf16[3,1024]{1,0:T(4,128)(2,1)S(1)}, u32[]{:S(2)}, u32[]{:S(2)}) collective-permute-start(bf16[3,1024]{1,0:T(4,128)(2,1)S(1)} %pad_maximum_fusion.3), channel_id=1, source_target_pairs={{0,8},{8,16},{16,24},{24,32},{32,40},{40,48},{48,56},{56,64},{64,7... | collective-permute-start | bytes 18440 | tf_op jit(solution)/shard_map/ppermute | solution.py:27
  10.0 0.0 copy-done.9
  10.1 0.0 copy-start.12
  10.1 0.5 fusion.5
  10.6 0.0 copy-done.7
  10.6 0.0 copy-done.11
  10.6 0.5 fusion.37
  11.2 0.1 reshape_broadcast_in_dim.6
  11.3 1.2 %copy.56.gc_ref = f32[24,64,1]{2,1,0:T(8,128)} copy(f32[24,64,1]{1,0,2:T(8,128)S(1)} %bitcast.92) | data formatting | bytes 12288 | tf_op jit(solution)/shard_map/broadcast_in_dim;reshape;squeeze | solution.py:355
  12.5 0.1 reshape_broadcast_in_dim.7
  12.6 1.3 %copy.57.bc_ref = f32[24,64,1]{2,1,0:T(8,128)} copy(f32[24,64,1]{1,0,2:T(8,128)S(1)} %bitcast.96) | data formatting | bytes 12288 | tf_op jit(solution)/shard_map/broadcast_in_dim;reshape;squeeze | solution.py:357
  13.9 0.0 collective-permute-done
  13.9 1.2 %divide_multiply_fusion.1 = (f32[384,256]{1,0:T(8,128)}, f32[384,256]{1,0:T(8,128)S(1)}) fusion(f32[384,256]{1,0:T(8,128)S(1)} %get-tuple-element.29, f32[3,256]{1,0:T(4,128)S(1)} %get-tuple-element.13, f32[256]{0:T(256)S(1)} %bitcast.107, f32[256]{0:T(256)S(1)} %bitcast.108, f32[256]{0:T(256)S(1)} %bitcast.106, f32[256]{0:T(256)S(1)} %bitcast.105, ...), kind=kLoop, calls=%fused_computation.57 | loop fusion | flops 2752512 | bytes 1587200 | tf_op jit(solution)/shard_map/jit(silu)/mul | solution.py:44
  15.1 1.2 %reshape.63 = f32[384,2,128]{2,1,0:T(2,128)S(1)} reshape(f32[384,256]{1,0:T(8,128)} %get-tuple-element.35) | data formatting | bytes 786432 | tf_op jit(solution)/shard_map/reshape | solution.py:74
  16.3 0.5 multiply_reduce_fusion.1
  16.8 0.5 broadcast_multiply_fusion
  17.3 0.1 broadcast_in_dim.5
  17.4 0.9 copy.51
  18.3 0.2 reshape.61
  18.6 0.5 multiply_reduce_fusion.2
  19.1 0.5 multiply_multiply_fusion
  19.6 0.1 broadcast_in_dim.4
  19.7 1.0 copy.49
  20.6 0.3 copy-done.4
  21.0 0.5 divide_multiply_fusion
  21.4 1.1 %reshape_reshape.11 = f32[6,64,4,128]{3,2,1,0:T(4,128)} reshape(f32[384,512]{1,0:T(8,128)S(1)} %divide_multiply_fusion) | data formatting | bytes 1572864 | tf_op jit(solution)/shard_map/reshape;reshape | solution.py:92
  22.6 2.1 %copy.52 = f32[6,64,4,128]{3,1,2,0:T(8,128)} copy(f32[6,64,4,128]{3,2,1,0:T(4,128)} %reshape_reshape.11) | data formatting | bytes 1572864 | tf_op jit(solution)/shard_map/reshape;reshape | solution.py:92
  24.7 13.3 %shard_map.136 = (f32[4,128,128]{2,1,0:T(8,128)}, f32[4,128,128]{2,1,0:T(8,128)}, f32[24,64,128]{2,1,0:T(8,128)}, f32[24,64,128]{2,1,0:T(8,128)}) custom-call(f32[24,64,128]{2,1,0:T(8,128)} %bitcast.85, f32[24,64,128]{2,1,0:T(8,128)} %bitcast.84, f32[24,64,128]{2,1,0:T(8,128)} %bitcast.86, f32[24,64,1]{2,1,0:T(8,128)} %copy.56.gc_ref, ...), custom_call_target="tpu_custom_call" | custom-call | tf_op jit(solution)/shard_map/pallas_call | solution.py:341
  38.1 34.6 %shard_map.137 = f32[4,128,128]{2,1,0:T(8,128)} custom-call(f32[4,128,128]{2,1,0:T(8,128)} %get-tuple-element.10.a_ref, f32[4,128,128]{2,1,0:T(8,128)} %get-tuple-element.11.b_ref), custom_call_target="tpu_custom_call" | custom-call | tf_op jit(solution)/shard_map/pallas_call | solution.py:241
  72.6 2.1 %multiply_reduce_fusion = (f32[6,64,4]{1,0,2:T(8,128)S(1)}, f32[6,64,4,128]{3,1,0,2:T(8,128)S(1)}) fusion(f32[6,4,64,128]{3,2,1,0:T(8,128)} %bitcast.89, f32[4,128,128]{2,1,0:T(8,128)} %shard_map.137, f32[6,4,64,128]{3,2,1,0:T(8,128)} %bitcast.88), kind=kOutput, calls=%fused_computation.30 | convolution fusion | flops 151583232 | bytes 2627584 | tf_op jit(solution)/shard_map/jhsd,hde->jhse/dot_general | solution.py:480
  74.8 0.1 copy.63
  74.9 1.4 %copy.60 = f32[6,64,4,128]{3,2,1,0:T(4,128)} copy(f32[6,64,4,128]{3,1,0,2:T(8,128)S(1)} %get-tuple-element.34) | data formatting | bytes 1572864 | tf_op jit(solution)/shard_map/transpose | solution.py:481
  76.3 0.5 mul.302
  76.8 0.0 copy-done
  76.8 5.4 %convolution_convert_fusion.part_ref = bf16[384,2048]{1,0:T(8,128)(2,1)} fusion(bf16[512,2048]{1,0:T(8,128)(2,1)S(1)} %copy-done, f32[48,8,4,128]{3,2,1,0:T(4,128)S(1)} %bitcast.90, f32[48,8,4,128]{3,2,1,0:T(4,128)} %bitcast.87, bf16[384,2048]{1,0:T(8,128)(2,1)} %param.14, bf16[2048,512]{1,0:T(8,128)(2,1)} %param.18, f32[512]{0:T(512)S(1)} %broadcast_bitcast_fusion), kind=kOutput, calls=%fused_computation | convolution fusion | flops 1613365248 | bytes 8914944 | tf_op jit(solution)/shard_map/dot_general | solution.py:483
  82.2 30.6 %shard_map.138 = bf16[48,2048]{1,0:T(8,128)(2,1)} custom-call(bf16[384,2048]{1,0:T(8,128)(2,1)} %convolution_convert_fusion.part_ref), custom_call_target="tpu_custom_call" | custom-call | tf_op jit(solution)/shard_map/pallas_call | solution.py:417
  112.8 1.6 %copy.78 = bf16[48,2048]{1,0:T(8,128)(2,1)} copy(bf16[48,2048]{1,0:T(8,128)(2,1)} %shard_map.138) | data formatting | bytes 393216
  (32 shorter events, 0.2 us)
Async XLA Ops:
  0.0 76.8 %copy-start = (bf16[512,2048]{1,0:T(8,128)(2,1)S(1)}, bf16[512,2048]{1,0:T(8,128)(2,1)}, u32[]{:S(2)}) copy-start(bf16[512,2048]{1,0:T(8,128)(2,1)} %param.27) | copy-start | bytes 6291460
  0.0 4.1 %copy-start.1 = (bf16[384,2048]{1,0:T(8,128)(2,1)S(1)}, bf16[384,2048]{1,0:T(8,128)(2,1)}, u32[]{:S(2)}) copy-start(bf16[384,2048]{1,0:T(8,128)(2,1)} %param.14) | copy-start | bytes 4718596
  0.0 4.1 %copy-start.2 = (bf16[2048,256]{1,0:T(8,128)(2,1)S(1)}, bf16[2048,256]{1,0:T(8,128)(2,1)}, u32[]{:S(2)}) copy-start(bf16[2048,256]{1,0:T(8,128)(2,1)} %param.15) | copy-start | bytes 3145732
  4.1 1.2 %copy-start.3 = (bf16[2048,256]{1,0:T(8,128)(2,1)S(1)}, bf16[2048,256]{1,0:T(8,128)(2,1)}, u32[]{:S(2)}) copy-start(bf16[2048,256]{1,0:T(8,128)(2,1)} %param.16) | copy-start | bytes 3145732
  5.4 4.6 %copy-start.9 = (bf16[4,256]{1,0:T(4,128)(2,1)S(1)}, bf16[4,256]{1,0:T(4,128)(2,1)}, u32[]{:S(2)}) copy-start(bf16[4,256]{1,0:T(4,128)(2,1)} %param.21) | copy-start | bytes 6148
  5.4 4.6 %copy-start.10 = (bf16[4,256]{1,0:T(4,128)(2,1)S(1)}, bf16[4,256]{1,0:T(4,128)(2,1)}, u32[]{:S(2)}) copy-start(bf16[4,256]{1,0:T(4,128)(2,1)} %param.22) | copy-start | bytes 6148
  5.4 4.7 %copy-start.8 = (bf16[4,512]{1,0:T(4,128)(2,1)S(1)}, bf16[4,512]{1,0:T(4,128)(2,1)}, u32[]{:S(2)}) copy-start(bf16[4,512]{1,0:T(4,128)(2,1)} %param.23) | copy-start | bytes 12292
  5.4 4.7 %copy-start.13 = (f32[4]{0:T(128)S(1)}, f32[4]{0:T(128)}, u32[]{:S(2)}) copy-start(f32[4]{0:T(128)} %param.24) | copy-start | bytes 52
  5.4 4.7 %copy-start.6 = (bf16[2048,4]{0,1:T(4,128)(2,1)S(1)}, bf16[2048,4]{0,1:T(4,128)(2,1)}, u32[]{:S(2)}) copy-start(bf16[2048,4]{0,1:T(4,128)(2,1)} %param.20) | copy-start | bytes 49156
  6.0 4.7 %copy-start.7 = (bf16[2048,4]{0,1:T(4,128)(2,1)S(1)}, bf16[2048,4]{0,1:T(4,128)(2,1)}, u32[]{:S(2)}) copy-start(bf16[2048,4]{0,1:T(4,128)(2,1)} %param.19) | copy-start | bytes 49156
  6.0 4.7 %copy-start.11 = (f32[4]{0:T(128)S(1)}, f32[4]{0:T(128)}, u32[]{:S(2)}) copy-start(f32[4]{0:T(128)} %param.25) | copy-start | bytes 52
  6.0 7.9 %collective-permute-start = (bf16[3,1024]{1,0:T(4,128)(2,1)S(1)}, bf16[3,1024]{1,0:T(4,128)(2,1)S(1)}, u32[]{:S(2)}, u32[]{:S(2)}) collective-permute-start(bf16[3,1024]{1,0:T(4,128)(2,1)S(1)} %pad_maximum_fusion.3), channel_id=1, source_target_pairs={{0,8},{8,16},{16,24},{24,32},{32,40},{40,48},{48,56},{56,64},{64,7... | collective-permute-start | bytes 18440 | tf_op jit(solution)/shard_map/ppermute | solution.py:27
  10.1 1.1 copy-start.12
  11.3 3.8 %copy-start.5 = (f32[6,4,64,1]{2,1,0,3:T(4,128)}, f32[6,4,64,1]{2,1,0,3:T(4,128)S(1)}, u32[]{:S(2)}) copy-start(f32[6,4,64,1]{2,1,0,3:T(4,128)S(1)} %copy.53) | copy-start | bytes 18436
  19.6 1.4 %copy-start.4 = (f32[384,512]{1,0:T(8,128)S(1)}, f32[384,512]{1,0:T(8,128)}, u32[]{:S(2)}) copy-start(f32[384,512]{1,0:T(8,128)} %get-tuple-element.31) | copy-start | bytes 2359300

commit v12 on v8

--- a/solution.py
+++ b/solution.py
@@ -268,14 +268,14 @@
 
 
 def span_kernel(
-    head_count, q_ref, k_ref, v_ref, gc_ref, gr_ref, bc_ref, shard_a_ref, shard_b_ref, mix_ref, entry_ref
+    head_count, q_ref, k_ref, v_ref, gc_ref, gr_ref, shard_a_ref, shard_b_ref, mix_ref, entry_ref
 ):
     queries = q_ref[...]
     key_vecs = k_ref[...]
     values = v_ref[...]
-    decay_col = gc_ref[...]
+    decay_col = gc_ref[:, :, 0:1]
     decay_row = gr_ref[...]
-    rate = bc_ref[...]
+    rate = gc_ref[:, :, 1:2]
     block_len = queries.shape[1]
     row_ids = lax.broadcasted_iota(jnp.int32, (1, block_len, block_len), 1)
     col_ids = lax.broadcasted_iota(jnp.int32, (1, block_len, block_len), 2)
@@ -358,15 +358,14 @@
             jax.ShapeDtypeStruct((pairs, block_len, values.shape[3]), jnp.float32),
             jax.ShapeDtypeStruct((pairs, block_len, width), jnp.float32),
         ],
-        in_specs=[pl.BlockSpec(memory_space=pltpu.VMEM)] * 6,
+        in_specs=[pl.BlockSpec(memory_space=pltpu.VMEM)] * 5,
         out_specs=[pl.BlockSpec(memory_space=pltpu.VMEM)] * 4,
     )(
         flat(queries),
         flat(key_vecs),
         flat(values),
-        decay[:, :, None],
+        jnp.stack([decay, rate], axis=-1),
         decay[:, None, :],
-        rate[:, :, None],
     )
     return (
         shard_a,

time: 115 us -> 115 us (level)
  matrix products: 13.8 us -> 15.2 us
  local copies, waits for them, and re-layouts: 14.1 us -> 12.8 us
    dot_general x1, matrix products: 0.53 us -> 1.94 us  [mixer_inputs(): jnp.dot(hidden_in, w_beta, preferred_element_type=jnp.float32)]
    another operation x2 -> x1, local copies, waits for them, and re-layouts: 2.49 us -> 1.23 us  [span_terms_kernel(): jnp.stack([decay, rate], axis=-1)]
where the time goes in v12:
time: 115 us; the launch traced here: 114 us
  Pallas kernels  78.2 us (68%)
  matrix products  15.2 us (13%)
  local copies, waits for them, and re-layouts  12.8 us (11%)
  starting transfers between devices  3.95 us (3%)
  other arithmetic  3.74 us (3%)
    pallas_call x1, Pallas kernels, shard_scan(): pl.pallas_call(functools.partial(shard_scan_kernel, shard_count), out_sha...  34.6 us
    pallas_call x1, Pallas kernels, group_sum(): pl.pallas_call(functools.partial(group_sum_kernel, group_count), out_shap...  30.6 us
    pallas_call x1, Pallas kernels, span_terms_kernel(): pl.pallas_call(functools.partial(span_kernel, lead[1]), out_shape=[jax.Sh...  13 us
    dot_general x1, matrix products, on_device(): jnp.dot(gated, w_out, preferred_element_type=jnp.float32)  5.39 us
    dot_general x1, matrix products, project_inputs(): jnp.dot(hidden_in, w_value, preferred_element_type=jnp.float32)  4.08 us
    ppermute x1, starting transfers between devices, passed_along(): return lax.ppermute(block, axis, route)  3.95 us
    another operation x4, local copies, waits for them, and re-layouts, to_blocks(): array_3d.reshape(tok_rows // SPAN, SPAN, head_count, -1)  3.44 us
    unnamed x29, local copies, waits for them, and re-layouts  2.62 us
  transfers between devices with their start and end apart: 1, of which 0 were waited for; matrix products, arithmetic and copies ran while one was open for 3% of the time, Pallas kernels for 0%

profile of v12, /device:TPU:1, one launch (start us, length us, event | category | flops | bytes accessed | tf_op | source)
XLA Modules:
  0.0 114.3 jit_solution(11302509919956455147)
XLA Ops:
  0.0 0.0 copy-start
  0.0 4.1 %fusion.41 = (f32[384,512]{1,0:T(8,128)}, bf16[384,512]{1,0:T(8,128)(2,1)S(1)}) fusion(bf16[384,2048]{1,0:T(8,128)(2,1)} %param.14, bf16[2048,512]{1,0:T(8,128)(2,1)} %param.17), kind=kOutput, calls=%fused_computation.90 | convolution fusion | flops 805699584 | bytes 4849664 | tf_op jit(solution)/shard_map/dot_general | solution.py:33
  4.1 0.0 copy-done.1
  4.1 0.0 copy-done.2
  4.1 0.0 copy-start.3
  4.1 0.6 fusion.39
  4.7 0.6 copy-done.3
  5.3 0.0 copy-start.6
  5.4 0.0 copy-start.11
  5.4 0.6 fusion.40
  6.0 0.0 copy-start.7
  6.0 3.9 %collective-permute-start = (bf16[3,1024]{1,0:T(4,128)(2,1)S(1)}, bf16[3,1024]{1,0:T(4,128)(2,1)S(1)}, u32[]{:S(2)}, u32[]{:S(2)}) collective-permute-start(bf16[3,1024]{1,0:T(4,128)(2,1)S(1)} %pad_maximum_fusion.4), channel_id=1, source_target_pairs={{0,8},{8,16},{16,24},{24,32},{32,40},{40,48},{48,56},{56,64},{64,7... | collective-permute-start | bytes 18440 | tf_op jit(solution)/shard_map/ppermute | solution.py:27
  10.0 0.0 copy-done.9
  10.0 0.0 copy-done.10
  10.0 0.0 copy-done.8
  10.0 0.0 copy-done.13
  10.1 0.0 copy-start.12
  10.1 0.5 fusion.37
  10.6 0.1 reshape_broadcast_in_dim.6
  10.7 1.9 %fusion.5 = f32[384,4]{0,1:T(4,128)S(1)} fusion(bf16[384,2048]{1,0:T(8,128)(2,1)} %param.14, bf16[2048,4]{0,1:T(4,128)(2,1)S(1)} %copy-done.7), kind=kOutput, calls=%fused_computation.15 | convolution fusion | flops 6296064 | bytes 1595392 | tf_op jit(solution)/shard_map/dot_general | solution.py:86
  12.7 0.1 reshape_broadcast_in_dim.7
  12.8 1.2 %copy.55.gc_ref = f32[24,64,2]{2,1,0:T(8,128)} copy(f32[24,64,2]{1,0,2:T(8,128)S(1)} %pad_maximum_fusion.3) | data formatting | bytes 24576 | tf_op jit(solution)/shard_map/stack | solution.py:367
  14.0 0.0 collective-permute-done
  14.0 1.2 %divide_multiply_fusion.1 = (f32[384,256]{1,0:T(8,128)}, f32[384,256]{1,0:T(8,128)S(1)}) fusion(f32[384,256]{1,0:T(8,128)S(1)} %get-tuple-element.29, f32[3,256]{1,0:T(4,128)S(1)} %get-tuple-element.13, f32[256]{0:T(256)S(1)} %bitcast.107, f32[256]{0:T(256)S(1)} %bitcast.108, f32[256]{0:T(256)S(1)} %bitcast.106, f32[256]{0:T(256)S(1)} %bitcast.105, ...), kind=kLoop, calls=%fused_computation.57 | loop fusion | flops 2752512 | bytes 1587200 | tf_op jit(solution)/shard_map/jit(silu)/mul | solution.py:44
  15.3 0.0 copy-done.5
  15.3 1.2 %reshape.63 = f32[384,2,128]{2,1,0:T(2,128)S(1)} reshape(f32[384,256]{1,0:T(8,128)} %get-tuple-element.35) | data formatting | bytes 786432 | tf_op jit(solution)/shard_map/reshape | solution.py:74
  16.5 0.5 multiply_reduce_fusion.1
  17.0 0.5 broadcast_multiply_fusion
  17.5 0.1 broadcast_in_dim.5
  17.6 1.0 copy.50
  18.5 0.2 reshape.61
  18.7 0.5 multiply_reduce_fusion.2
  19.2 0.5 multiply_multiply_fusion
  19.8 0.1 broadcast_in_dim.4
  19.8 1.0 copy.48
  20.8 0.3 copy-done.4
  21.1 0.5 divide_multiply_fusion
  21.6 1.2 %reshape_reshape.11 = f32[6,64,4,128]{3,2,1,0:T(4,128)} reshape(f32[384,512]{1,0:T(8,128)S(1)} %divide_multiply_fusion) | data formatting | bytes 1572864 | tf_op jit(solution)/shard_map/reshape;reshape | solution.py:92
  22.8 2.1 %copy.51 = f32[6,64,4,128]{3,1,2,0:T(8,128)} copy(f32[6,64,4,128]{3,2,1,0:T(4,128)} %reshape_reshape.11) | data formatting | bytes 1572864 | tf_op jit(solution)/shard_map/reshape;reshape | solution.py:92
  24.9 13.0 %shard_map.136 = (f32[4,128,128]{2,1,0:T(8,128)}, f32[4,128,128]{2,1,0:T(8,128)}, f32[24,64,128]{2,1,0:T(8,128)}, f32[24,64,128]{2,1,0:T(8,128)}) custom-call(f32[24,64,128]{2,1,0:T(8,128)} %bitcast.85, f32[24,64,128]{2,1,0:T(8,128)} %bitcast.84, f32[24,64,128]{2,1,0:T(8,128)} %bitcast.86, f32[24,64,2]{2,1,0:T(8,128)} %copy.55.gc_ref, f32[24,1,64]{2,1,0:T(1,128)} %bitcast.93), custom_call_target="tpu_custom_call" | custom-call | tf_op jit(solution)/shard_map/pallas_call | solution.py:353
  37.9 34.6 %shard_map.137 = f32[4,128,128]{2,1,0:T(8,128)} custom-call(f32[4,128,128]{2,1,0:T(8,128)} %get-tuple-element.10.a_ref, f32[4,128,128]{2,1,0:T(8,128)} %get-tuple-element.11.b_ref), custom_call_target="tpu_custom_call" | custom-call | tf_op jit(solution)/shard_map/pallas_call | solution.py:251
  72.5 2.1 %multiply_reduce_fusion = (f32[6,64,4]{1,0,2:T(8,128)S(1)}, f32[6,64,4,128]{3,1,0,2:T(8,128)S(1)}) fusion(f32[6,4,64,128]{3,2,1,0:T(8,128)} %bitcast.89, f32[4,128,128]{2,1,0:T(8,128)} %shard_map.137, f32[6,4,64,128]{3,2,1,0:T(8,128)} %bitcast.88), kind=kOutput, calls=%fused_computation.30 | convolution fusion | flops 151583232 | bytes 2627584 | tf_op jit(solution)/shard_map/jhsd,hde->jhse/dot_general | solution.py:491
  74.6 0.1 copy.61
  74.8 1.4 %copy.58 = f32[6,64,4,128]{3,2,1,0:T(4,128)} copy(f32[6,64,4,128]{3,1,0,2:T(8,128)S(1)} %get-tuple-element.34) | data formatting | bytes 1572864 | tf_op jit(solution)/shard_map/transpose | solution.py:492
  76.2 0.5 mul.302
  76.7 5.4 %convolution_convert_fusion.part_ref = bf16[384,2048]{1,0:T(8,128)(2,1)} fusion(bf16[512,2048]{1,0:T(8,128)(2,1)S(1)} %copy-done, f32[48,8,4,128]{3,2,1,0:T(4,128)S(1)} %bitcast.90, f32[48,8,4,128]{3,2,1,0:T(4,128)} %bitcast.87, bf16[384,2048]{1,0:T(8,128)(2,1)} %param.14, bf16[2048,512]{1,0:T(8,128)(2,1)} %param.18, f32[512]{0:T(512)S(1)} %broadcast_bitcast_fusion), kind=kOutput, calls=%fused_computation | convolution fusion | flops 1613365248 | bytes 8914944 | tf_op jit(solution)/shard_map/dot_general | solution.py:494
  82.0 30.6 %shard_map.138 = bf16[48,2048]{1,0:T(8,128)(2,1)} custom-call(bf16[384,2048]{1,0:T(8,128)(2,1)} %convolution_convert_fusion.part_ref), custom_call_target="tpu_custom_call" | custom-call | tf_op jit(solution)/shard_map/pallas_call | solution.py:428
  112.7 1.6 %copy.76 = bf16[48,2048]{1,0:T(8,128)(2,1)} copy(bf16[48,2048]{1,0:T(8,128)(2,1)} %shard_map.138) | data formatting | bytes 393216
  (32 shorter events, 0.2 us)
Async XLA Ops:
  0.0 76.7 %copy-start = (bf16[512,2048]{1,0:T(8,128)(2,1)S(1)}, bf16[512,2048]{1,0:T(8,128)(2,1)}, u32[]{:S(2)}) copy-start(bf16[512,2048]{1,0:T(8,128)(2,1)} %param.27) | copy-start | bytes 6291460
  0.0 4.1 %copy-start.1 = (bf16[384,2048]{1,0:T(8,128)(2,1)S(1)}, bf16[384,2048]{1,0:T(8,128)(2,1)}, u32[]{:S(2)}) copy-start(bf16[384,2048]{1,0:T(8,128)(2,1)} %param.14) | copy-start | bytes 4718596
  0.0 4.1 %copy-start.2 = (bf16[2048,256]{1,0:T(8,128)(2,1)S(1)}, bf16[2048,256]{1,0:T(8,128)(2,1)}, u32[]{:S(2)}) copy-start(bf16[2048,256]{1,0:T(8,128)(2,1)} %param.15) | copy-start | bytes 3145732
  4.1 1.2 %copy-start.3 = (bf16[2048,256]{1,0:T(8,128)(2,1)S(1)}, bf16[2048,256]{1,0:T(8,128)(2,1)}, u32[]{:S(2)}) copy-start(bf16[2048,256]{1,0:T(8,128)(2,1)} %param.16) | copy-start | bytes 3145732
  5.3 4.6 %copy-start.9 = (bf16[4,256]{1,0:T(4,128)(2,1)S(1)}, bf16[4,256]{1,0:T(4,128)(2,1)}, u32[]{:S(2)}) copy-start(bf16[4,256]{1,0:T(4,128)(2,1)} %param.21) | copy-start | bytes 6148
  5.3 4.6 %copy-start.10 = (bf16[4,256]{1,0:T(4,128)(2,1)S(1)}, bf16[4,256]{1,0:T(4,128)(2,1)}, u32[]{:S(2)}) copy-start(bf16[4,256]{1,0:T(4,128)(2,1)} %param.22) | copy-start | bytes 6148
  5.3 4.7 %copy-start.8 = (bf16[4,512]{1,0:T(4,128)(2,1)S(1)}, bf16[4,512]{1,0:T(4,128)(2,1)}, u32[]{:S(2)}) copy-start(bf16[4,512]{1,0:T(4,128)(2,1)} %param.23) | copy-start | bytes 12292
  5.3 4.7 %copy-start.13 = (f32[4]{0:T(128)S(1)}, f32[4]{0:T(128)}, u32[]{:S(2)}) copy-start(f32[4]{0:T(128)} %param.24) | copy-start | bytes 52
  5.3 4.7 %copy-start.6 = (bf16[2048,4]{0,1:T(4,128)(2,1)S(1)}, bf16[2048,4]{0,1:T(4,128)(2,1)}, u32[]{:S(2)}) copy-start(bf16[2048,4]{0,1:T(4,128)(2,1)} %param.19) | copy-start | bytes 49156
  5.4 4.7 %copy-start.11 = (f32[4]{0:T(128)S(1)}, f32[4]{0:T(128)}, u32[]{:S(2)}) copy-start(f32[4]{0:T(128)} %param.25) | copy-start | bytes 52
  6.0 4.8 %copy-start.7 = (bf16[2048,4]{0,1:T(4,128)(2,1)S(1)}, bf16[2048,4]{0,1:T(4,128)(2,1)}, u32[]{:S(2)}) copy-start(bf16[2048,4]{0,1:T(4,128)(2,1)} %param.20) | copy-start | bytes 49156
  6.0 8.0 %collective-permute-start = (bf16[3,1024]{1,0:T(4,128)(2,1)S(1)}, bf16[3,1024]{1,0:T(4,128)(2,1)S(1)}, u32[]{:S(2)}, u32[]{:S(2)}) collective-permute-start(bf16[3,1024]{1,0:T(4,128)(2,1)S(1)} %pad_maximum_fusion.4), channel_id=1, source_target_pairs={{0,8},{8,16},{16,24},{24,32},{32,40},{40,48},{48,56},{56,64},{64,7... | collective-permute-start | bytes 18440 | tf_op jit(solution)/shard_map/ppermute | solution.py:27
  10.1 2.7 %copy-start.12 = (f32[128]{0:T(128)S(1)}, f32[128]{0:T(128)}, u32[]{:S(2)}) copy-start(f32[128]{0:T(128)} %param.26) | copy-start | bytes 1540
  10.7 4.5 %copy-start.5 = (f32[6,4,64,1]{2,1,0,3:T(4,128)}, f32[6,4,64,1]{2,1,0,3:T(4,128)S(1)}, u32[]{:S(2)}) copy-start(f32[6,4,64,1]{2,1,0,3:T(4,128)S(1)} %copy.52) | copy-start | bytes 18436
  19.7 1.4 %copy-start.4 = (f32[384,512]{1,0:T(8,128)S(1)}, f32[384,512]{1,0:T(8,128)}, u32[]{:S(2)}) copy-start(f32[384,512]{1,0:T(8,128)} %get-tuple-element.31) | copy-start | bytes 2359300

commit v13 on v12

--- a/solution.py
+++ b/solution.py
@@ -210,11 +210,29 @@
                 )
             )
         sem_index += len(copies)
-        for copy in copies:
-            copy.start()
-        for copy in copies:
-            copy.wait()
         has_prev = me >= distance
+        has_next = me + distance < shard_count
+
+        @pl.when(has_next)
+        def _():
+            for copy in copies:
+                copy.start()
+
+        @pl.when(has_prev)
+        def _():
+            for copy in copies:
+                copy.wait_recv()
+
+        @pl.when(jnp.logical_not(has_prev))
+        def _():
+            got_b[round_index] = jnp.zeros(got_b.shape[1:], got_b.dtype)
+            if sends_a:
+                got_a[round_index] = jnp.zeros(got_a.shape[1:], got_a.dtype)
+
+        @pl.when(has_next)
+        def _():
+            for copy in copies:
+                copy.wait_send()
         for head in range(head_count):
             own_a = cur_a[round_index, head]
             own_b = cur_b[round_index, head]

time: 115 us -> 115 us (level)
    pallas_call x1, Pallas kernels: 30.6 us -> 32.2 us  [group_sum(): pl.pallas_call(functools.partial(group_sum_kernel, group_count), out_shap...]
where the time goes in v13:
time: 115 us
  Pallas kernels  78.9 us (69%)
  matrix products  15.2 us (13%)
  local copies, waits for them, and re-layouts  12.8 us (11%)
  starting transfers between devices  3.95 us (3%)
  other arithmetic  3.74 us (3%)
    pallas_call x1, Pallas kernels, shard_scan(): pl.pallas_call(functools.partial(shard_scan_kernel, shard_count), out_sha...  33.7 us
    pallas_call x1, Pallas kernels, group_sum(): pl.pallas_call(functools.partial(group_sum_kernel, group_count), out_shap...  32.2 us
    pallas_call x1, Pallas kernels, span_terms_kernel(): pl.pallas_call(functools.partial(span_kernel, lead[1]), out_shape=[jax.Sh...  13 us
    dot_general x1, matrix products, on_device(): jnp.dot(gated, w_out, preferred_element_type=jnp.float32)  5.39 us
    dot_general x1, matrix products, project_inputs(): jnp.dot(hidden_in, w_value, preferred_element_type=jnp.float32)  4.08 us
    ppermute x1, starting transfers between devices, passed_along(): return lax.ppermute(block, axis, route)  3.95 us
    another operation x4, local copies, waits for them, and re-layouts, to_blocks(): array_3d.reshape(tok_rows // SPAN, SPAN, head_count, -1)  3.44 us
    unnamed x29, local copies, waits for them, and re-layouts  2.62 us
  transfers between devices with their start and end apart: 1, of which 0 were waited for; matrix products, arithmetic and copies ran while one was open for 3% of the time, Pallas kernels for 0%

profile of v13, /device:TPU:1, one launch (start us, length us, event | category | flops | bytes accessed | tf_op | source)
XLA Modules:
  0.0 115.0 jit_solution(11638448469224125458)
XLA Ops:
  0.0 0.0 copy-start
  0.0 4.1 %fusion.41 = (f32[384,512]{1,0:T(8,128)}, bf16[384,512]{1,0:T(8,128)(2,1)S(1)}) fusion(bf16[384,2048]{1,0:T(8,128)(2,1)} %param.14, bf16[2048,512]{1,0:T(8,128)(2,1)} %param.17), kind=kOutput, calls=%fused_computation.90 | convolution fusion | flops 805699584 | bytes 4849664 | tf_op jit(solution)/shard_map/dot_general | solution.py:33
  4.1 0.0 copy-done.1
  4.1 0.0 copy-done.2
  4.1 0.0 copy-start.3
  4.1 0.6 fusion.39
  4.7 0.6 copy-done.3
  5.3 0.0 copy-start.6
  5.4 0.0 copy-start.11
  5.4 0.6 fusion.40
  6.0 0.0 copy-start.7
  6.0 3.9 %collective-permute-start = (bf16[3,1024]{1,0:T(4,128)(2,1)S(1)}, bf16[3,1024]{1,0:T(4,128)(2,1)S(1)}, u32[]{:S(2)}, u32[]{:S(2)}) collective-permute-start(bf16[3,1024]{1,0:T(4,128)(2,1)S(1)} %pad_maximum_fusion.4), channel_id=1, source_target_pairs={{0,8},{8,16},{16,24},{24,32},{32,40},{40,48},{48,56},{56,64},{64,7... | collective-permute-start | bytes 18440 | tf_op jit(solution)/shard_map/ppermute | solution.py:27
  10.0 0.0 copy-done.9
  10.0 0.0 copy-done.10
  10.0 0.0 copy-done.8
  10.0 0.0 copy-done.13
  10.1 0.0 copy-start.12
  10.1 0.5 fusion.37
  10.6 0.1 reshape_broadcast_in_dim.6
  10.7 1.9 %fusion.5 = f32[384,4]{0,1:T(4,128)S(1)} fusion(bf16[384,2048]{1,0:T(8,128)(2,1)} %param.14, bf16[2048,4]{0,1:T(4,128)(2,1)S(1)} %copy-done.7), kind=kOutput, calls=%fused_computation.15 | convolution fusion | flops 6296064 | bytes 1595392 | tf_op jit(solution)/shard_map/dot_general | solution.py:86
  12.7 0.1 reshape_broadcast_in_dim.7
  12.8 1.2 %copy.55.gc_ref = f32[24,64,2]{2,1,0:T(8,128)} copy(f32[24,64,2]{1,0,2:T(8,128)S(1)} %pad_maximum_fusion.3) | data formatting | bytes 24576 | tf_op jit(solution)/shard_map/stack | solution.py:385
  14.0 0.0 collective-permute-done
  14.0 1.2 %divide_multiply_fusion.1 = (f32[384,256]{1,0:T(8,128)}, f32[384,256]{1,0:T(8,128)S(1)}) fusion(f32[384,256]{1,0:T(8,128)S(1)} %get-tuple-element.29, f32[3,256]{1,0:T(4,128)S(1)} %get-tuple-element.13, f32[256]{0:T(256)S(1)} %bitcast.107, f32[256]{0:T(256)S(1)} %bitcast.108, f32[256]{0:T(256)S(1)} %bitcast.106, f32[256]{0:T(256)S(1)} %bitcast.105, ...), kind=kLoop, calls=%fused_computation.57 | loop fusion | flops 2752512 | bytes 1587200 | tf_op jit(solution)/shard_map/jit(silu)/mul | solution.py:44
  15.3 0.0 copy-done.5
  15.3 1.2 %reshape.63 = f32[384,2,128]{2,1,0:T(2,128)S(1)} reshape(f32[384,256]{1,0:T(8,128)} %get-tuple-element.35) | data formatting | bytes 786432 | tf_op jit(solution)/shard_map/reshape | solution.py:74
  16.5 0.5 multiply_reduce_fusion.1
  17.0 0.5 broadcast_multiply_fusion
  17.5 0.1 broadcast_in_dim.5
  17.6 1.0 copy.50
  18.5 0.2 reshape.61
  18.7 0.5 multiply_reduce_fusion.2
  19.2 0.5 multiply_multiply_fusion
  19.8 0.1 broadcast_in_dim.4
  19.8 1.0 copy.48
  20.8 0.3 copy-done.4
  21.1 0.5 divide_multiply_fusion
  21.6 1.2 %reshape_reshape.11 = f32[6,64,4,128]{3,2,1,0:T(4,128)} reshape(f32[384,512]{1,0:T(8,128)S(1)} %divide_multiply_fusion) | data formatting | bytes 1572864 | tf_op jit(solution)/shard_map/reshape;reshape | solution.py:92
  22.8 2.1 %copy.51 = f32[6,64,4,128]{3,1,2,0:T(8,128)} copy(f32[6,64,4,128]{3,2,1,0:T(4,128)} %reshape_reshape.11) | data formatting | bytes 1572864 | tf_op jit(solution)/shard_map/reshape;reshape | solution.py:92
  24.9 13.0 %shard_map.136 = (f32[4,128,128]{2,1,0:T(8,128)}, f32[4,128,128]{2,1,0:T(8,128)}, f32[24,64,128]{2,1,0:T(8,128)}, f32[24,64,128]{2,1,0:T(8,128)}) custom-call(f32[24,64,128]{2,1,0:T(8,128)} %bitcast.85, f32[24,64,128]{2,1,0:T(8,128)} %bitcast.84, f32[24,64,128]{2,1,0:T(8,128)} %bitcast.86, f32[24,64,2]{2,1,0:T(8,128)} %copy.55.gc_ref, f32[24,1,64]{2,1,0:T(1,128)} %bitcast.93), custom_call_target="tpu_custom_call" | custom-call | tf_op jit(solution)/shard_map/pallas_call | solution.py:371
  37.9 33.7 %shard_map.137 = f32[4,128,128]{2,1,0:T(8,128)} custom-call(f32[4,128,128]{2,1,0:T(8,128)} %get-tuple-element.10.a_ref, f32[4,128,128]{2,1,0:T(8,128)} %get-tuple-element.11.b_ref), custom_call_target="tpu_custom_call" | custom-call | tf_op jit(solution)/shard_map/pallas_call | solution.py:269
  71.6 2.1 %multiply_reduce_fusion = (f32[6,64,4]{1,0,2:T(8,128)S(1)}, f32[6,64,4,128]{3,1,0,2:T(8,128)S(1)}) fusion(f32[6,4,64,128]{3,2,1,0:T(8,128)} %bitcast.89, f32[4,128,128]{2,1,0:T(8,128)} %shard_map.137, f32[6,4,64,128]{3,2,1,0:T(8,128)} %bitcast.88), kind=kOutput, calls=%fused_computation.30 | convolution fusion | flops 151583232 | bytes 2627584 | tf_op jit(solution)/shard_map/jhsd,hde->jhse/dot_general | solution.py:509
  73.8 0.1 copy.61
  73.9 1.4 %copy.58 = f32[6,64,4,128]{3,2,1,0:T(4,128)} copy(f32[6,64,4,128]{3,1,0,2:T(8,128)S(1)} %get-tuple-element.34) | data formatting | bytes 1572864 | tf_op jit(solution)/shard_map/transpose | solution.py:510
  75.3 0.5 mul.302
  75.8 5.4 %convolution_convert_fusion.part_ref = bf16[384,2048]{1,0:T(8,128)(2,1)} fusion(bf16[512,2048]{1,0:T(8,128)(2,1)S(1)} %copy-done, f32[48,8,4,128]{3,2,1,0:T(4,128)S(1)} %bitcast.90, f32[48,8,4,128]{3,2,1,0:T(4,128)} %bitcast.87, bf16[384,2048]{1,0:T(8,128)(2,1)} %param.14, bf16[2048,512]{1,0:T(8,128)(2,1)} %param.18, f32[512]{0:T(512)S(1)} %broadcast_bitcast_fusion), kind=kOutput, calls=%fused_computation | convolution fusion | flops 1613365248 | bytes 8914944 | tf_op jit(solution)/shard_map/dot_general | solution.py:512
  81.2 32.2 %shard_map.138 = bf16[48,2048]{1,0:T(8,128)(2,1)} custom-call(bf16[384,2048]{1,0:T(8,128)(2,1)} %convolution_convert_fusion.part_ref), custom_call_target="tpu_custom_call" | custom-call | tf_op jit(solution)/shard_map/pallas_call | solution.py:446
  113.4 1.6 %copy.76 = bf16[48,2048]{1,0:T(8,128)(2,1)} copy(bf16[48,2048]{1,0:T(8,128)(2,1)} %shard_map.138) | data formatting | bytes 393216
  (32 shorter events, 0.2 us)
Async XLA Ops:
  0.0 75.8 %copy-start = (bf16[512,2048]{1,0:T(8,128)(2,1)S(1)}, bf16[512,2048]{1,0:T(8,128)(2,1)}, u32[]{:S(2)}) copy-start(bf16[512,2048]{1,0:T(8,128)(2,1)} %param.27) | copy-start | bytes 6291460
  0.0 4.1 %copy-start.1 = (bf16[384,2048]{1,0:T(8,128)(2,1)S(1)}, bf16[384,2048]{1,0:T(8,128)(2,1)}, u32[]{:S(2)}) copy-start(bf16[384,2048]{1,0:T(8,128)(2,1)} %param.14) | copy-start | bytes 4718596
  0.0 4.1 %copy-start.2 = (bf16[2048,256]{1,0:T(8,128)(2,1)S(1)}, bf16[2048,256]{1,0:T(8,128)(2,1)}, u32[]{:S(2)}) copy-start(bf16[2048,256]{1,0:T(8,128)(2,1)} %param.15) | copy-start | bytes 3145732
  4.1 1.2 %copy-start.3 = (bf16[2048,256]{1,0:T(8,128)(2,1)S(1)}, bf16[2048,256]{1,0:T(8,128)(2,1)}, u32[]{:S(2)}) copy-start(bf16[2048,256]{1,0:T(8,128)(2,1)} %param.16) | copy-start | bytes 3145732
  5.3 4.6 %copy-start.9 = (bf16[4,256]{1,0:T(4,128)(2,1)S(1)}, bf16[4,256]{1,0:T(4,128)(2,1)}, u32[]{:S(2)}) copy-start(bf16[4,256]{1,0:T(4,128)(2,1)} %param.21) | copy-start | bytes 6148
  5.3 4.6 %copy-start.10 = (bf16[4,256]{1,0:T(4,128)(2,1)S(1)}, bf16[4,256]{1,0:T(4,128)(2,1)}, u32[]{:S(2)}) copy-start(bf16[4,256]{1,0:T(4,128)(2,1)} %param.22) | copy-start | bytes 6148
  5.3 4.7 %copy-start.8 = (bf16[4,512]{1,0:T(4,128)(2,1)S(1)}, bf16[4,512]{1,0:T(4,128)(2,1)}, u32[]{:S(2)}) copy-start(bf16[4,512]{1,0:T(4,128)(2,1)} %param.23) | copy-start | bytes 12292
  5.3 4.7 %copy-start.13 = (f32[4]{0:T(128)S(1)}, f32[4]{0:T(128)}, u32[]{:S(2)}) copy-start(f32[4]{0:T(128)} %param.24) | copy-start | bytes 52
  5.3 4.7 %copy-start.6 = (bf16[2048,4]{0,1:T(4,128)(2,1)S(1)}, bf16[2048,4]{0,1:T(4,128)(2,1)}, u32[]{:S(2)}) copy-start(bf16[2048,4]{0,1:T(4,128)(2,1)} %param.19) | copy-start | bytes 49156
  5.4 4.7 %copy-start.11 = (f32[4]{0:T(128)S(1)}, f32[4]{0:T(128)}, u32[]{:S(2)}) copy-start(f32[4]{0:T(128)} %param.25) | copy-start | bytes 52
  6.0 4.8 %copy-start.7 = (bf16[2048,4]{0,1:T(4,128)(2,1)S(1)}, bf16[2048,4]{0,1:T(4,128)(2,1)}, u32[]{:S(2)}) copy-start(bf16[2048,4]{0,1:T(4,128)(2,1)} %param.20) | copy-start | bytes 49156
  6.0 8.0 %collective-permute-start = (bf16[3,1024]{1,0:T(4,128)(2,1)S(1)}, bf16[3,1024]{1,0:T(4,128)(2,1)S(1)}, u32[]{:S(2)}, u32[]{:S(2)}) collective-permute-start(bf16[3,1024]{1,0:T(4,128)(2,1)S(1)} %pad_maximum_fusion.4), channel_id=1, source_target_pairs={{0,8},{8,16},{16,24},{24,32},{32,40},{40,48},{48,56},{56,64},{64,7... | collective-permute-start | bytes 18440 | tf_op jit(solution)/shard_map/ppermute | solution.py:27
  10.1 2.7 %copy-start.12 = (f32[128]{0:T(128)S(1)}, f32[128]{0:T(128)}, u32[]{:S(2)}) copy-start(f32[128]{0:T(128)} %param.26) | copy-start | bytes 1540
  10.7 4.5 %copy-start.5 = (f32[6,4,64,1]{2,1,0,3:T(4,128)}, f32[6,4,64,1]{2,1,0,3:T(4,128)S(1)}, u32[]{:S(2)}) copy-start(f32[6,4,64,1]{2,1,0,3:T(4,128)S(1)} %copy.52) | copy-start | bytes 18436
  19.7 1.4 %copy-start.4 = (f32[384,512]{1,0:T(8,128)S(1)}, f32[384,512]{1,0:T(8,128)}, u32[]{:S(2)}) copy-start(f32[384,512]{1,0:T(8,128)} %get-tuple-element.31) | copy-start | bytes 2359300

commit v14 on v12

--- a/solution.py
+++ b/solution.py
@@ -375,7 +375,7 @@
     )
 
 
-def group_sum_kernel(group_count, part_ref, out_ref, landed, send_sems, recv_sems, own_sem):
+def group_sum_kernel(group_count, part_ref, out_ref, landed, send_sems, recv_sems):
     me = lax.axis_index("hg")
     seq_me = lax.axis_index("seq")
     rows = out_ref.shape[0]
@@ -397,11 +397,7 @@
         )
         copy.start()
         sends.append(copy)
-    own = pltpu.make_async_copy(
-        part_ref.at[pl.ds(pl.multiple_of(me * rows, 8), rows)], landed.at[me], own_sem
-    )
-    own.start()
-    own.wait()
+    total = part_ref[pl.ds(pl.multiple_of(me * rows, 8), rows), :].astype(jnp.float32)
     for step in range(1, group_count):
         source = lax.rem(me + group_count - step, group_count)
         pltpu.make_async_remote_copy(
@@ -412,11 +408,9 @@
             device_id=(seq_me, source),
             device_id_type=MESH,
         ).wait_recv()
+        total = total + landed[source].astype(jnp.float32)
     for copy in sends:
         copy.wait_send()
-    total = landed[0].astype(jnp.float32)
-    for slot in range(1, group_count):
-        total = total + landed[slot].astype(jnp.float32)
     out_ref[...] = total.astype(out_ref.dtype)
 
 
@@ -434,7 +428,6 @@
             pltpu.VMEM((group_count, rows, cols), part.dtype),
             pltpu.SemaphoreType.DMA((group_count,)),
             pltpu.SemaphoreType.DMA((group_count,)),
-            pltpu.SemaphoreType.DMA,
         ],
         compiler_params=pltpu.CompilerParams(collective_id=0, has_side_effects=True),
     )(part)

time: 115 us -> 115 us (level)
  no operation moved by 1% of the time
where the time goes in v14:
time: 115 us; the launch traced here: 114 us
  Pallas kernels  78.2 us (68%)
  matrix products  15.2 us (13%)
  local copies, waits for them, and re-layouts  12.8 us (11%)
  starting transfers between devices  3.95 us (3%)
  other arithmetic  3.74 us (3%)
    pallas_call x1, Pallas kernels, shard_scan(): pl.pallas_call(functools.partial(shard_scan_kernel, shard_count), out_sha...  34.6 us
    pallas_call x1, Pallas kernels, group_sum(): pl.pallas_call(functools.partial(group_sum_kernel, group_count), out_shap...  30.6 us
    pallas_call x1, Pallas kernels, span_terms_kernel(): pl.pallas_call(functools.partial(span_kernel, lead[1]), out_shape=[jax.Sh...  13 us
    dot_general x1, matrix products, on_device(): jnp.dot(gated, w_out, preferred_element_type=jnp.float32)  5.39 us
    dot_general x1, matrix products, project_inputs(): jnp.dot(hidden_in, w_value, preferred_element_type=jnp.float32)  4.08 us
    ppermute x1, starting transfers between devices, passed_along(): return lax.ppermute(block, axis, route)  3.95 us
    another operation x4, local copies, waits for them, and re-layouts, to_blocks(): array_3d.reshape(tok_rows // SPAN, SPAN, head_count, -1)  3.44 us
    unnamed x29, local copies, waits for them, and re-layouts  2.62 us
  transfers between devices with their start and end apart: 1, of which 0 were waited for; matrix products, arithmetic and copies ran while one was open for 3% of the time, Pallas kernels for 0%

profile of v14, /device:TPU:1, one launch (start us, length us, event | category | flops | bytes accessed | tf_op | source)
XLA Modules:
  0.0 114.2 jit_solution(3386866117275213811)
XLA Ops:
  0.0 0.0 copy-start
  0.0 4.1 %fusion.41 = (f32[384,512]{1,0:T(8,128)}, bf16[384,512]{1,0:T(8,128)(2,1)S(1)}) fusion(bf16[384,2048]{1,0:T(8,128)(2,1)} %param.14, bf16[2048,512]{1,0:T(8,128)(2,1)} %param.17), kind=kOutput, calls=%fused_computation.90 | convolution fusion | flops 805699584 | bytes 4849664 | tf_op jit(solution)/shard_map/dot_general | solution.py:33
  4.1 0.0 copy-done.1
  4.1 0.0 copy-done.2
  4.1 0.0 copy-start.3
  4.1 0.6 fusion.39
  4.7 0.6 copy-done.3
  5.3 0.0 copy-start.6
  5.4 0.0 copy-start.11
  5.4 0.6 fusion.40
  6.0 0.0 copy-start.7
  6.0 3.9 %collective-permute-start = (bf16[3,1024]{1,0:T(4,128)(2,1)S(1)}, bf16[3,1024]{1,0:T(4,128)(2,1)S(1)}, u32[]{:S(2)}, u32[]{:S(2)}) collective-permute-start(bf16[3,1024]{1,0:T(4,128)(2,1)S(1)} %pad_maximum_fusion.4), channel_id=1, source_target_pairs={{0,8},{8,16},{16,24},{24,32},{32,40},{40,48},{48,56},{56,64},{64,7... | collective-permute-start | bytes 18440 | tf_op jit(solution)/shard_map/ppermute | solution.py:27
  10.0 0.0 copy-done.9
  10.0 0.0 copy-done.10
  10.0 0.0 copy-done.13
  10.1 0.0 copy-start.12
  10.1 0.5 fusion.37
  10.6 0.1 reshape_broadcast_in_dim.6
  10.7 0.0 copy-done.7
  10.7 1.9 %fusion.5 = f32[384,4]{0,1:T(4,128)S(1)} fusion(bf16[384,2048]{1,0:T(8,128)(2,1)} %param.14, bf16[2048,4]{0,1:T(4,128)(2,1)S(1)} %copy-done.7), kind=kOutput, calls=%fused_computation.15 | convolution fusion | flops 6296064 | bytes 1595392 | tf_op jit(solution)/shard_map/dot_general | solution.py:86
  12.7 0.1 reshape_broadcast_in_dim.7
  12.8 1.2 %copy.55.gc_ref = f32[24,64,2]{2,1,0:T(8,128)} copy(f32[24,64,2]{1,0,2:T(8,128)S(1)} %pad_maximum_fusion.3) | data formatting | bytes 24576 | tf_op jit(solution)/shard_map/stack | solution.py:367
  14.0 0.0 collective-permute-done
  14.0 1.2 %divide_multiply_fusion.1 = (f32[384,256]{1,0:T(8,128)}, f32[384,256]{1,0:T(8,128)S(1)}) fusion(f32[384,256]{1,0:T(8,128)S(1)} %get-tuple-element.29, f32[3,256]{1,0:T(4,128)S(1)} %get-tuple-element.13, f32[256]{0:T(256)S(1)} %bitcast.107, f32[256]{0:T(256)S(1)} %bitcast.108, f32[256]{0:T(256)S(1)} %bitcast.106, f32[256]{0:T(256)S(1)} %bitcast.105, ...), kind=kLoop, calls=%fused_computation.57 | loop fusion | flops 2752512 | bytes 1587200 | tf_op jit(solution)/shard_map/jit(silu)/mul | solution.py:44
  15.3 1.2 %reshape.63 = f32[384,2,128]{2,1,0:T(2,128)S(1)} reshape(f32[384,256]{1,0:T(8,128)} %get-tuple-element.35) | data formatting | bytes 786432 | tf_op jit(solution)/shard_map/reshape | solution.py:74
  16.5 0.5 multiply_reduce_fusion.1
  17.0 0.5 broadcast_multiply_fusion
  17.5 0.1 broadcast_in_dim.5
  17.6 1.0 copy.50
  18.5 0.2 reshape.61
  18.7 0.5 multiply_reduce_fusion.2
  19.2 0.5 multiply_multiply_fusion
  19.7 0.0 copy-start.4
  19.8 0.1 broadcast_in_dim.4
  19.8 1.0 copy.48
  20.8 0.3 copy-done.4
  21.1 0.5 divide_multiply_fusion
  21.6 1.2 %reshape_reshape.11 = f32[6,64,4,128]{3,2,1,0:T(4,128)} reshape(f32[384,512]{1,0:T(8,128)S(1)} %divide_multiply_fusion) | data formatting | bytes 1572864 | tf_op jit(solution)/shard_map/reshape;reshape | solution.py:92
  22.8 2.1 %copy.51 = f32[6,64,4,128]{3,1,2,0:T(8,128)} copy(f32[6,64,4,128]{3,2,1,0:T(4,128)} %reshape_reshape.11) | data formatting | bytes 1572864 | tf_op jit(solution)/shard_map/reshape;reshape | solution.py:92
  24.9 13.0 %shard_map.136 = (f32[4,128,128]{2,1,0:T(8,128)}, f32[4,128,128]{2,1,0:T(8,128)}, f32[24,64,128]{2,1,0:T(8,128)}, f32[24,64,128]{2,1,0:T(8,128)}) custom-call(f32[24,64,128]{2,1,0:T(8,128)} %bitcast.85, f32[24,64,128]{2,1,0:T(8,128)} %bitcast.84, f32[24,64,128]{2,1,0:T(8,128)} %bitcast.86, f32[24,64,2]{2,1,0:T(8,128)} %copy.55.gc_ref, f32[24,1,64]{2,1,0:T(1,128)} %bitcast.93), custom_call_target="tpu_custom_call" | custom-call | tf_op jit(solution)/shard_map/pallas_call | solution.py:353
  37.9 34.6 %shard_map.137 = f32[4,128,128]{2,1,0:T(8,128)} custom-call(f32[4,128,128]{2,1,0:T(8,128)} %get-tuple-element.10.a_ref, f32[4,128,128]{2,1,0:T(8,128)} %get-tuple-element.11.b_ref), custom_call_target="tpu_custom_call" | custom-call | tf_op jit(solution)/shard_map/pallas_call | solution.py:251
  72.5 2.1 %multiply_reduce_fusion = (f32[6,64,4]{1,0,2:T(8,128)S(1)}, f32[6,64,4,128]{3,1,0,2:T(8,128)S(1)}) fusion(f32[6,4,64,128]{3,2,1,0:T(8,128)} %bitcast.89, f32[4,128,128]{2,1,0:T(8,128)} %shard_map.137, f32[6,4,64,128]{3,2,1,0:T(8,128)} %bitcast.88), kind=kOutput, calls=%fused_computation.30 | convolution fusion | flops 151583232 | bytes 2627584 | tf_op jit(solution)/shard_map/jhsd,hde->jhse/dot_general | solution.py:484
  74.6 0.1 copy.61
  74.8 1.4 %copy.58 = f32[6,64,4,128]{3,2,1,0:T(4,128)} copy(f32[6,64,4,128]{3,1,0,2:T(8,128)S(1)} %get-tuple-element.34) | data formatting | bytes 1572864 | tf_op jit(solution)/shard_map/transpose | solution.py:485
  76.2 0.5 mul.302
  76.7 5.4 %convolution_convert_fusion.part_ref = bf16[384,2048]{1,0:T(8,128)(2,1)} fusion(bf16[512,2048]{1,0:T(8,128)(2,1)S(1)} %copy-done, f32[48,8,4,128]{3,2,1,0:T(4,128)S(1)} %bitcast.90, f32[48,8,4,128]{3,2,1,0:T(4,128)} %bitcast.87, bf16[384,2048]{1,0:T(8,128)(2,1)} %param.14, bf16[2048,512]{1,0:T(8,128)(2,1)} %param.18, f32[512]{0:T(512)S(1)} %broadcast_bitcast_fusion), kind=kOutput, calls=%fused_computation | convolution fusion | flops 1613365248 | bytes 8914944 | tf_op jit(solution)/shard_map/dot_general | solution.py:487
  82.0 30.6 %shard_map.138 = bf16[48,2048]{1,0:T(8,128)(2,1)} custom-call(bf16[384,2048]{1,0:T(8,128)(2,1)} %convolution_convert_fusion.part_ref), custom_call_target="tpu_custom_call" | custom-call | tf_op jit(solution)/shard_map/pallas_call | solution.py:422
  112.6 1.6 %copy.76 = bf16[48,2048]{1,0:T(8,128)(2,1)} copy(bf16[48,2048]{1,0:T(8,128)(2,1)} %shard_map.138) | data formatting | bytes 393216
  (32 shorter events, 0.2 us)
Async XLA Ops:
  0.0 76.7 %copy-start = (bf16[512,2048]{1,0:T(8,128)(2,1)S(1)}, bf16[512,2048]{1,0:T(8,128)(2,1)}, u32[]{:S(2)}) copy-start(bf16[512,2048]{1,0:T(8,128)(2,1)} %param.27) | copy-start | bytes 6291460
  0.0 4.1 %copy-start.1 = (bf16[384,2048]{1,0:T(8,128)(2,1)S(1)}, bf16[384,2048]{1,0:T(8,128)(2,1)}, u32[]{:S(2)}) copy-start(bf16[384,2048]{1,0:T(8,128)(2,1)} %param.14) | copy-start | bytes 4718596
  0.0 4.1 %copy-start.2 = (bf16[2048,256]{1,0:T(8,128)(2,1)S(1)}, bf16[2048,256]{1,0:T(8,128)(2,1)}, u32[]{:S(2)}) copy-start(bf16[2048,256]{1,0:T(8,128)(2,1)} %param.15) | copy-start | bytes 3145732
  4.1 1.2 %copy-start.3 = (bf16[2048,256]{1,0:T(8,128)(2,1)S(1)}, bf16[2048,256]{1,0:T(8,128)(2,1)}, u32[]{:S(2)}) copy-start(bf16[2048,256]{1,0:T(8,128)(2,1)} %param.16) | copy-start | bytes 3145732
  5.3 4.6 %copy-start.9 = (bf16[4,256]{1,0:T(4,128)(2,1)S(1)}, bf16[4,256]{1,0:T(4,128)(2,1)}, u32[]{:S(2)}) copy-start(bf16[4,256]{1,0:T(4,128)(2,1)} %param.21) | copy-start | bytes 6148
  5.3 4.6 %copy-start.10 = (bf16[4,256]{1,0:T(4,128)(2,1)S(1)}, bf16[4,256]{1,0:T(4,128)(2,1)}, u32[]{:S(2)}) copy-start(bf16[4,256]{1,0:T(4,128)(2,1)} %param.22) | copy-start | bytes 6148
  5.3 4.7 %copy-start.8 = (bf16[4,512]{1,0:T(4,128)(2,1)S(1)}, bf16[4,512]{1,0:T(4,128)(2,1)}, u32[]{:S(2)}) copy-start(bf16[4,512]{1,0:T(4,128)(2,1)} %param.23) | copy-start | bytes 12292
  5.3 4.7 %copy-start.13 = (f32[4]{0:T(128)S(1)}, f32[4]{0:T(128)}, u32[]{:S(2)}) copy-start(f32[4]{0:T(128)} %param.24) | copy-start | bytes 52
  5.3 4.7 %copy-start.6 = (bf16[2048,4]{0,1:T(4,128)(2,1)S(1)}, bf16[2048,4]{0,1:T(4,128)(2,1)}, u32[]{:S(2)}) copy-start(bf16[2048,4]{0,1:T(4,128)(2,1)} %param.19) | copy-start | bytes 49156
  5.4 4.7 %copy-start.11 = (f32[4]{0:T(128)S(1)}, f32[4]{0:T(128)}, u32[]{:S(2)}) copy-start(f32[4]{0:T(128)} %param.25) | copy-start | bytes 52
  6.0 4.8 %copy-start.7 = (bf16[2048,4]{0,1:T(4,128)(2,1)S(1)}, bf16[2048,4]{0,1:T(4,128)(2,1)}, u32[]{:S(2)}) copy-start(bf16[2048,4]{0,1:T(4,128)(2,1)} %param.20) | copy-start | bytes 49156
  6.0 8.0 %collective-permute-start = (bf16[3,1024]{1,0:T(4,128)(2,1)S(1)}, bf16[3,1024]{1,0:T(4,128)(2,1)S(1)}, u32[]{:S(2)}, u32[]{:S(2)}) collective-permute-start(bf16[3,1024]{1,0:T(4,128)(2,1)S(1)} %pad_maximum_fusion.4), channel_id=1, source_target_pairs={{0,8},{8,16},{16,24},{24,32},{32,40},{40,48},{48,56},{56,64},{64,7... | collective-permute-start | bytes 18440 | tf_op jit(solution)/shard_map/ppermute | solution.py:27
  10.1 2.7 %copy-start.12 = (f32[128]{0:T(128)S(1)}, f32[128]{0:T(128)}, u32[]{:S(2)}) copy-start(f32[128]{0:T(128)} %param.26) | copy-start | bytes 1540
  10.7 4.5 %copy-start.5 = (f32[6,4,64,1]{2,1,0,3:T(4,128)}, f32[6,4,64,1]{2,1,0,3:T(4,128)S(1)}, u32[]{:S(2)}) copy-start(f32[6,4,64,1]{2,1,0,3:T(4,128)S(1)} %copy.52) | copy-start | bytes 18436
  19.7 1.4 %copy-start.4 = (f32[384,512]{1,0:T(8,128)S(1)}, f32[384,512]{1,0:T(8,128)}, u32[]{:S(2)}) copy-start(f32[384,512]{1,0:T(8,128)} %get-tuple-element.31) | copy-start | bytes 2359300

commit v15 on v14

--- a/solution.py
+++ b/solution.py
@@ -180,8 +180,6 @@
         for target in (lax.rem(me + distance, shard_count), lax.rem(me + shard_count - distance, shard_count)):
             pl.semaphore_signal(barrier, inc=1, device_id=(target, hg_me), device_id_type=MESH)
     pl.semaphore_wait(barrier, 2 * len(distances))
-    cur_a[0] = a_ref[...]
-    cur_b[0] = b_ref[...]
     out_a[0] = a_ref[...].astype(out_a.dtype)
     out_b[0] = b_ref[...].astype(out_b.dtype)
     sem_index = 0
@@ -216,8 +214,8 @@
             copy.wait()
         has_prev = me >= distance
         for head in range(head_count):
-            own_a = cur_a[round_index, head]
-            own_b = cur_b[round_index, head]
+            own_a = a_ref[head] if round_index == 0 else cur_a[round_index, head]
+            own_b = b_ref[head] if round_index == 0 else cur_b[round_index, head]
             joined_b = (
                 jnp.dot(own_a, got_b[round_index, head].astype(jnp.float32), precision=highest,
                         preferred_element_type=jnp.float32)

time: 115 us -> 115 us (level)
  no operation moved by 1% of the time
where the time goes in v15:
time: 115 us; the launch traced here: 114 us
  Pallas kernels  78.2 us (68%)
  matrix products  15.2 us (13%)
  local copies, waits for them, and re-layouts  12.8 us (11%)
  starting transfers between devices  3.95 us (3%)
  other arithmetic  3.74 us (3%)
    pallas_call x1, Pallas kernels, shard_scan(): pl.pallas_call(functools.partial(shard_scan_kernel, shard_count), out_sha...  34.5 us
    pallas_call x1, Pallas kernels, group_sum(): pl.pallas_call(functools.partial(group_sum_kernel, group_count), out_shap...  30.6 us
    pallas_call x1, Pallas kernels, span_terms_kernel(): pl.pallas_call(functools.partial(span_kernel, lead[1]), out_shape=[jax.Sh...  13 us
    dot_general x1, matrix products, on_device(): jnp.dot(gated, w_out, preferred_element_type=jnp.float32)  5.39 us
    dot_general x1, matrix products, project_inputs(): jnp.dot(hidden_in, w_value, preferred_element_type=jnp.float32)  4.08 us
    ppermute x1, starting transfers between devices, passed_along(): return lax.ppermute(block, axis, route)  3.95 us
    another operation x4, local copies, waits for them, and re-layouts, to_blocks(): array_3d.reshape(tok_rows // SPAN, SPAN, head_count, -1)  3.44 us
    unnamed x29, local copies, waits for them, and re-layouts  2.62 us
  transfers between devices with their start and end apart: 1, of which 0 were waited for; matrix products, arithmetic and copies ran while one was open for 3% of the time, Pallas kernels for 0%

profile of v15, /device:TPU:1, one launch (start us, length us, event | category | flops | bytes accessed | tf_op | source)
XLA Modules:
  0.0 114.2 jit_solution(2072977495940687619)
XLA Ops:
  0.0 0.0 copy-start
  0.0 4.1 %fusion.41 = (f32[384,512]{1,0:T(8,128)}, bf16[384,512]{1,0:T(8,128)(2,1)S(1)}) fusion(bf16[384,2048]{1,0:T(8,128)(2,1)} %param.14, bf16[2048,512]{1,0:T(8,128)(2,1)} %param.17), kind=kOutput, calls=%fused_computation.90 | convolution fusion | flops 805699584 | bytes 4849664 | tf_op jit(solution)/shard_map/dot_general | solution.py:33
  4.1 0.0 copy-done.1
  4.1 0.0 copy-done.2
  4.1 0.0 copy-start.3
  4.1 0.6 fusion.39
  4.7 0.6 copy-done.3
  5.3 0.0 copy-start.6
  5.4 0.0 copy-start.11
  5.4 0.6 fusion.40
  6.0 0.0 copy-start.7
  6.0 3.9 %collective-permute-start = (bf16[3,1024]{1,0:T(4,128)(2,1)S(1)}, bf16[3,1024]{1,0:T(4,128)(2,1)S(1)}, u32[]{:S(2)}, u32[]{:S(2)}) collective-permute-start(bf16[3,1024]{1,0:T(4,128)(2,1)S(1)} %pad_maximum_fusion.4), channel_id=1, source_target_pairs={{0,8},{8,16},{16,24},{24,32},{32,40},{40,48},{48,56},{56,64},{64,7... | collective-permute-start | bytes 18440 | tf_op jit(solution)/shard_map/ppermute | solution.py:27
  10.0 0.0 copy-done.9
  10.0 0.0 copy-done.10
  10.0 0.0 copy-done.13
  10.1 0.0 copy-start.12
  10.1 0.5 fusion.37
  10.6 0.1 reshape_broadcast_in_dim.6
  10.7 0.0 copy-done.7
  10.7 1.9 %fusion.5 = f32[384,4]{0,1:T(4,128)S(1)} fusion(bf16[384,2048]{1,0:T(8,128)(2,1)} %param.14, bf16[2048,4]{0,1:T(4,128)(2,1)S(1)} %copy-done.7), kind=kOutput, calls=%fused_computation.15 | convolution fusion | flops 6296064 | bytes 1595392 | tf_op jit(solution)/shard_map/dot_general | solution.py:86
  12.7 0.1 reshape_broadcast_in_dim.7
  12.8 1.2 %copy.55.gc_ref = f32[24,64,2]{2,1,0:T(8,128)} copy(f32[24,64,2]{1,0,2:T(8,128)S(1)} %pad_maximum_fusion.3) | data formatting | bytes 24576 | tf_op jit(solution)/shard_map/stack | solution.py:365
  14.0 0.0 collective-permute-done
  14.0 1.2 %divide_multiply_fusion.1 = (f32[384,256]{1,0:T(8,128)}, f32[384,256]{1,0:T(8,128)S(1)}) fusion(f32[384,256]{1,0:T(8,128)S(1)} %get-tuple-element.29, f32[3,256]{1,0:T(4,128)S(1)} %get-tuple-element.13, f32[256]{0:T(256)S(1)} %bitcast.107, f32[256]{0:T(256)S(1)} %bitcast.108, f32[256]{0:T(256)S(1)} %bitcast.106, f32[256]{0:T(256)S(1)} %bitcast.105, ...), kind=kLoop, calls=%fused_computation.57 | loop fusion | flops 2752512 | bytes 1587200 | tf_op jit(solution)/shard_map/jit(silu)/mul | solution.py:44
  15.3 1.2 %reshape.63 = f32[384,2,128]{2,1,0:T(2,128)S(1)} reshape(f32[384,256]{1,0:T(8,128)} %get-tuple-element.35) | data formatting | bytes 786432 | tf_op jit(solution)/shard_map/reshape | solution.py:74
  16.5 0.5 multiply_reduce_fusion.1
  17.0 0.5 broadcast_multiply_fusion
  17.5 0.1 broadcast_in_dim.5
  17.6 1.0 copy.50
  18.5 0.2 reshape.61
  18.7 0.5 multiply_reduce_fusion.2
  19.2 0.5 multiply_multiply_fusion
  19.7 0.0 copy-start.4
  19.8 0.1 broadcast_in_dim.4
  19.8 1.0 copy.48
  20.8 0.3 copy-done.4
  21.1 0.5 divide_multiply_fusion
  21.6 1.2 %reshape_reshape.11 = f32[6,64,4,128]{3,2,1,0:T(4,128)} reshape(f32[384,512]{1,0:T(8,128)S(1)} %divide_multiply_fusion) | data formatting | bytes 1572864 | tf_op jit(solution)/shard_map/reshape;reshape | solution.py:92
  22.8 2.1 %copy.51 = f32[6,64,4,128]{3,1,2,0:T(8,128)} copy(f32[6,64,4,128]{3,2,1,0:T(4,128)} %reshape_reshape.11) | data formatting | bytes 1572864 | tf_op jit(solution)/shard_map/reshape;reshape | solution.py:92
  24.9 13.0 %shard_map.136 = (f32[4,128,128]{2,1,0:T(8,128)}, f32[4,128,128]{2,1,0:T(8,128)}, f32[24,64,128]{2,1,0:T(8,128)}, f32[24,64,128]{2,1,0:T(8,128)}) custom-call(f32[24,64,128]{2,1,0:T(8,128)} %bitcast.85, f32[24,64,128]{2,1,0:T(8,128)} %bitcast.84, f32[24,64,128]{2,1,0:T(8,128)} %bitcast.86, f32[24,64,2]{2,1,0:T(8,128)} %copy.55.gc_ref, f32[24,1,64]{2,1,0:T(1,128)} %bitcast.93), custom_call_target="tpu_custom_call" | custom-call | tf_op jit(solution)/shard_map/pallas_call | solution.py:351
  37.9 34.5 %shard_map.137 = f32[4,128,128]{2,1,0:T(8,128)} custom-call(f32[4,128,128]{2,1,0:T(8,128)} %get-tuple-element.10.a_ref, f32[4,128,128]{2,1,0:T(8,128)} %get-tuple-element.11.b_ref), custom_call_target="tpu_custom_call" | custom-call | tf_op jit(solution)/shard_map/pallas_call | solution.py:249
  72.5 2.1 %multiply_reduce_fusion = (f32[6,64,4]{1,0,2:T(8,128)S(1)}, f32[6,64,4,128]{3,1,0,2:T(8,128)S(1)}) fusion(f32[6,4,64,128]{3,2,1,0:T(8,128)} %bitcast.89, f32[4,128,128]{2,1,0:T(8,128)} %shard_map.137, f32[6,4,64,128]{3,2,1,0:T(8,128)} %bitcast.88), kind=kOutput, calls=%fused_computation.30 | convolution fusion | flops 151583232 | bytes 2627584 | tf_op jit(solution)/shard_map/jhsd,hde->jhse/dot_general | solution.py:482
  74.6 0.1 copy.61
  74.7 1.4 %copy.58 = f32[6,64,4,128]{3,2,1,0:T(4,128)} copy(f32[6,64,4,128]{3,1,0,2:T(8,128)S(1)} %get-tuple-element.34) | data formatting | bytes 1572864 | tf_op jit(solution)/shard_map/transpose | solution.py:483
  76.1 0.5 mul.302
  76.6 5.4 %convolution_convert_fusion.part_ref = bf16[384,2048]{1,0:T(8,128)(2,1)} fusion(bf16[512,2048]{1,0:T(8,128)(2,1)S(1)} %copy-done, f32[48,8,4,128]{3,2,1,0:T(4,128)S(1)} %bitcast.90, f32[48,8,4,128]{3,2,1,0:T(4,128)} %bitcast.87, bf16[384,2048]{1,0:T(8,128)(2,1)} %param.14, bf16[2048,512]{1,0:T(8,128)(2,1)} %param.18, f32[512]{0:T(512)S(1)} %broadcast_bitcast_fusion), kind=kOutput, calls=%fused_computation | convolution fusion | flops 1613365248 | bytes 8914944 | tf_op jit(solution)/shard_map/dot_general | solution.py:485
  82.0 30.6 %shard_map.138 = bf16[48,2048]{1,0:T(8,128)(2,1)} custom-call(bf16[384,2048]{1,0:T(8,128)(2,1)} %convolution_convert_fusion.part_ref), custom_call_target="tpu_custom_call" | custom-call | tf_op jit(solution)/shard_map/pallas_call | solution.py:420
  112.6 1.6 %copy.76 = bf16[48,2048]{1,0:T(8,128)(2,1)} copy(bf16[48,2048]{1,0:T(8,128)(2,1)} %shard_map.138) | data formatting | bytes 393216
  (32 shorter events, 0.2 us)
Async XLA Ops:
  0.0 76.6 %copy-start = (bf16[512,2048]{1,0:T(8,128)(2,1)S(1)}, bf16[512,2048]{1,0:T(8,128)(2,1)}, u32[]{:S(2)}) copy-start(bf16[512,2048]{1,0:T(8,128)(2,1)} %param.27) | copy-start | bytes 6291460
  0.0 4.1 %copy-start.1 = (bf16[384,2048]{1,0:T(8,128)(2,1)S(1)}, bf16[384,2048]{1,0:T(8,128)(2,1)}, u32[]{:S(2)}) copy-start(bf16[384,2048]{1,0:T(8,128)(2,1)} %param.14) | copy-start | bytes 4718596
  0.0 4.1 %copy-start.2 = (bf16[2048,256]{1,0:T(8,128)(2,1)S(1)}, bf16[2048,256]{1,0:T(8,128)(2,1)}, u32[]{:S(2)}) copy-start(bf16[2048,256]{1,0:T(8,128)(2,1)} %param.15) | copy-start | bytes 3145732
  4.1 1.2 %copy-start.3 = (bf16[2048,256]{1,0:T(8,128)(2,1)S(1)}, bf16[2048,256]{1,0:T(8,128)(2,1)}, u32[]{:S(2)}) copy-start(bf16[2048,256]{1,0:T(8,128)(2,1)} %param.16) | copy-start | bytes 3145732
  5.3 4.6 %copy-start.9 = (bf16[4,256]{1,0:T(4,128)(2,1)S(1)}, bf16[4,256]{1,0:T(4,128)(2,1)}, u32[]{:S(2)}) copy-start(bf16[4,256]{1,0:T(4,128)(2,1)} %param.21) | copy-start | bytes 6148
  5.3 4.6 %copy-start.10 = (bf16[4,256]{1,0:T(4,128)(2,1)S(1)}, bf16[4,256]{1,0:T(4,128)(2,1)}, u32[]{:S(2)}) copy-start(bf16[4,256]{1,0:T(4,128)(2,1)} %param.22) | copy-start | bytes 6148
  5.3 4.7 %copy-start.8 = (bf16[4,512]{1,0:T(4,128)(2,1)S(1)}, bf16[4,512]{1,0:T(4,128)(2,1)}, u32[]{:S(2)}) copy-start(bf16[4,512]{1,0:T(4,128)(2,1)} %param.23) | copy-start | bytes 12292
  5.3 4.7 %copy-start.13 = (f32[4]{0:T(128)S(1)}, f32[4]{0:T(128)}, u32[]{:S(2)}) copy-start(f32[4]{0:T(128)} %param.24) | copy-start | bytes 52
  5.3 4.7 %copy-start.6 = (bf16[2048,4]{0,1:T(4,128)(2,1)S(1)}, bf16[2048,4]{0,1:T(4,128)(2,1)}, u32[]{:S(2)}) copy-start(bf16[2048,4]{0,1:T(4,128)(2,1)} %param.19) | copy-start | bytes 49156
  5.4 4.7 %copy-start.11 = (f32[4]{0:T(128)S(1)}, f32[4]{0:T(128)}, u32[]{:S(2)}) copy-start(f32[4]{0:T(128)} %param.25) | copy-start | bytes 52
  6.0 4.8 %copy-start.7 = (bf16[2048,4]{0,1:T(4,128)(2,1)S(1)}, bf16[2048,4]{0,1:T(4,128)(2,1)}, u32[]{:S(2)}) copy-start(bf16[2048,4]{0,1:T(4,128)(2,1)} %param.20) | copy-start | bytes 49156
  6.0 8.0 %collective-permute-start = (bf16[3,1024]{1,0:T(4,128)(2,1)S(1)}, bf16[3,1024]{1,0:T(4,128)(2,1)S(1)}, u32[]{:S(2)}, u32[]{:S(2)}) collective-permute-start(bf16[3,1024]{1,0:T(4,128)(2,1)S(1)} %pad_maximum_fusion.4), channel_id=1, source_target_pairs={{0,8},{8,16},{16,24},{24,32},{32,40},{40,48},{48,56},{56,64},{64,7... | collective-permute-start | bytes 18440 | tf_op jit(solution)/shard_map/ppermute | solution.py:27
  10.1 2.7 %copy-start.12 = (f32[128]{0:T(128)S(1)}, f32[128]{0:T(128)}, u32[]{:S(2)}) copy-start(f32[128]{0:T(128)} %param.26) | copy-start | bytes 1540
  10.7 4.5 %copy-start.5 = (f32[6,4,64,1]{2,1,0,3:T(4,128)}, f32[6,4,64,1]{2,1,0,3:T(4,128)S(1)}, u32[]{:S(2)}) copy-start(f32[6,4,64,1]{2,1,0,3:T(4,128)S(1)} %copy.52) | copy-start | bytes 18436
  19.7 1.4 %copy-start.4 = (f32[384,512]{1,0:T(8,128)S(1)}, f32[384,512]{1,0:T(8,128)}, u32[]{:S(2)}) copy-start(f32[384,512]{1,0:T(8,128)} %get-tuple-element.31) | copy-start | bytes 2359300
